TPU v7x, 512 devices: a whole 4x4x16 slice. The times are simulated.
512 devices in a mesh: slab: 64 (over z, x), sec: 8 (over y, core).
Axes of the slice: x: 4, y: 4, z: 16, core: 2. Of those that a mesh axis runs over, the one named last changes fastest.
Arguments:
- source: float32 [64, 65536], P(None, ('slab', 'sec'))
- fine_blocks: bfloat16 [3, 64, 64, 65536], P(None, None, None, ('slab', 'sec'))
- fine_pattern: int32 [3, 65536], P(None, ('slab', 'sec')), may hold values from 0 to 65535, as said below
- fine_prolong: bfloat16 [3, 64, 6, 65536], P(None, None, None, ('slab', 'sec')), may hold values from -0.75 to 0.75
- prolong_pattern: int32 [3, 65536], P(None, ('slab', 'sec')), may hold values from 0 to 65535, as said below
- coarse_blocks: bfloat16 [3, 6, 6, 65536], P(None, None, None, 'slab')
- coarse_pattern: int32 [3, 65536], P(None, 'slab'), may hold values from 0 to 65535, as said below
- section_prolong: bfloat16 [3, 6, 24, 65536], P(None, None, None, 'slab'), may hold values from -0.046875 to 0.046875
- coarsest_inverse: float32 [1536, 1536], P('slab')
Outputs:
- solution: float32 [64, 65536], P(None, ('slab', 'sec'))
Inputs may be any that keep to these rules, and one draw needn't show every extreme that they name: `fine_pattern`: row 0 names the aggregate itself; the other rows name aggregates at most 96 away, and distance exactly 96 occurs in every draw. `prolong_pattern`: row 0 names the aggregate's own coarse block; the other rows name coarse blocks at most 96 away, and distance exactly 96 occurs in every draw. `coarse_pattern`: row 0 names the block itself; the other rows name coarse blocks at most 96 away, and distance exactly 96 occurs in every draw.
All inputs are finite; a program needn't handle non-finite values.
Results may differ from a plain program's by a relative error of at most 0.0003.
Values sent between devices are 32-bit elements; how exact they have to be, the bound alone decides.
No kernel may reach another device: no remote copies, remote signals or barrier semaphores. Data moves between devices by JAX's collectives and lax.ppermute only.
A program may use at most 64 MiB of HBM per device.

v0:
```python
import jax
import jax.numpy as jnp
from jax import lax
from jax.sharding import PartitionSpec as P

HB = 96
CYCLES = 2


KEEP = 1.0 / 7.0
FRESH = 8.0 / 7.0


def padded(array, sides, width):
    for axis, dim in sides:
        count, length = (lax.axis_size(axis), array.shape[dim])
        up = [(i, (i + 1) % count) for i in range(count - 1)]
        down = [(j, i) for i, j in up]
        last = lax.slice_in_dim(array, length - width, length, axis=dim)
        leading = lax.slice_in_dim(array, 0, width, axis=dim)
        before = lax.ppermute(last, axis, up)
        after = lax.ppermute(leading, axis, down)
        array = jnp.concatenate([before, array, after], axis=dim)
    return array


def from_behind(value, axis, steps):
    count = lax.axis_size(axis)
    leading, last = (max(0, -steps), min(count, count - steps))
    return lax.ppermute(value, axis, [(source, source + steps) for source in range(leading, last)])


def inverse_diagonal(matrix):
    return 1.0 / jnp.diagonal(matrix[0], axis1=0, axis2=1).T.astype(jnp.float32)


def apply_local(matrix, local_cols, extended):
    picked = jnp.swapaxes(extended[:, local_cols], 0, 1)
    return jnp.sum(matrix * picked[:, None, :, :], axis=(0, 2))


def smooth(operator, inverse, rhs, start):
    if start is None:
        change = inverse * rhs
        field = change
    else:
        change = inverse * (rhs - operator(start))
        field = start + change
    change = KEEP * change + FRESH * inverse * (rhs - operator(field))
    return field + change


def shards(
    source,
    fine_blocks,
    fine_pattern,
    fine_prolong,
    prolong_pattern,
    coarse_blocks,
    coarse_pattern,
    section_prolong,
    coarsest_inverse,
):
    reach = HB
    own_rows = source.shape[1]
    section_rows = coarse_blocks.shape[3]
    device = lax.axis_index(("slab", "sec"))
    section = lax.axis_index("slab")
    fine_cols = fine_pattern - (device * own_rows - reach)
    coarse_cols = coarse_pattern - (section * section_rows - reach)
    gather_cols = prolong_pattern - (section * section_rows - reach)
    fine_inverse = inverse_diagonal(fine_blocks)
    coarse_inverse = inverse_diagonal(coarse_blocks)

    def fine_apply(field):
        extended = padded(field, ((("slab", "sec"), 1),), reach)
        return apply_local(fine_blocks, fine_cols, extended)

    def coarse_extend(field):
        return padded(field, (("slab", 1),), reach)

    def coarse_apply(field):
        return apply_local(coarse_blocks, coarse_cols, coarse_extend(field))

    solution = None
    for turn_index in range(CYCLES):
        solution = smooth(fine_apply, fine_inverse, source, solution)
        residual = source - fine_apply(solution)
        terms = jnp.sum(fine_prolong * residual[None, :, None, :], axis=1)
        modes = terms.shape[1]
        flat = jnp.swapaxes(terms, 0, 1).reshape(modes, -1)
        slots = gather_cols.reshape(-1)
        partial_sum = (
            jnp.zeros((modes, section_rows + 2 * reach), jnp.float32).at[:, slots].add(flat)
        )
        partial_sum = lax.psum(partial_sum, "sec")
        lower = from_behind(partial_sum[:, section_rows + reach :], "slab", 1)
        upper = from_behind(partial_sum[:, :reach], "slab", -1)
        inner = partial_sum[:, reach : reach + section_rows]
        coarse_rhs = inner.at[:, :reach].add(lower).at[:, section_rows - reach :].add(upper)
        coarse_sol = smooth(coarse_apply, coarse_inverse, coarse_rhs, None)
        coarse_res = coarse_rhs - coarse_apply(coarse_sol)
        parts = jnp.sum(section_prolong * coarse_res[None, :, None, :], axis=(1, 3))
        width = parts.shape[1]
        every = lax.all_gather(parts[None], "slab", axis=0, tiled=True)
        zero = jnp.zeros((1, width), jnp.float32)
        total = (
            every[:, 1]
            + jnp.concatenate([every[1:, 0], zero], 0)
            + jnp.concatenate([zero, every[:-1, 2]], 0)
        )
        answer = jnp.dot(coarsest_inverse, total.reshape(-1), precision=lax.Precision.HIGHEST)
        nearby = padded(answer[None, :], (("slab", 0),), 1)
        coarse_sol = coarse_sol + jnp.sum(section_prolong * nearby[:, None, :, None], axis=(0, 2))
        coarse_sol = smooth(coarse_apply, coarse_inverse, coarse_rhs, coarse_sol)
        prolong_extended = coarse_extend(coarse_sol)
        picked = jnp.swapaxes(prolong_extended[:, gather_cols], 0, 1)
        solution = solution + jnp.sum(fine_prolong * picked[:, None, :, :], axis=(0, 2))
        solution = smooth(fine_apply, fine_inverse, source, solution)
    return solution


def solution(mesh):
    in_specs = (
        P(None, ("slab", "sec")),
        P(None, None, None, ("slab", "sec")),
        P(None, ("slab", "sec")),
        P(None, None, None, ("slab", "sec")),
        P(None, ("slab", "sec")),
        P(None, None, None, "slab"),
        P(None, "slab"),
        P(None, None, None, "slab"),
        P("slab", None),
    )
    out_specs = P(None, ("slab", "sec"))
    return jax.shard_map(shards, mesh=mesh, in_specs=in_specs, out_specs=out_specs, check_vma=False)
```

profile of v0, /device:TPU:127, one launch (start us, length us, event | category | flops | bytes accessed | tf_op | source)
XLA Modules:
  0.0 759.0 jit_solution(1430777949323937785)
XLA Ops:
  33.6 8.1 %collective-permute-done.3 = f32[64,96]{1,0:T(8,128)S(1)} collective-permute-done((f32[64,96]{1,0:T(8,128)S(1)}, f32[64,96]{1,0:T(8,128)S(1)}, u32[]{:S(2)}, u32[]{:S(2)}) %collective-permute-start.3) | collective-permute-done | bytes 24608 | tf_op jit(solution)/shard_map/ppermute | solution.py:22
  53.9 23.9 %psum.14 = f32[6,1216]{1,0:T(8,128)S(1)} all-reduce(f32[6,1216]{1,0:T(8,128)S(1)} %copy.153), channel_id=1, replica_groups=mesh['slab'=64,'sec'=8] {'sec'}, use_global_device_ids=true, to_apply=%region_4.5 | all-reduce | flops 7296 | bytes 58368 | tf_op jit(solution)/shard_map/psum | solution.py:96
  100.5 11.9 %gather_fusion.4 = f32[3072,6]{1,0:T(8,128)} fusion(f32[6,1216]{0,1:T(8,128)} %copy.154, s32[3072]{0:T(1024)S(1)} %broadcast_clamp_fusion), kind=kCustom, calls=%fused_computation.4 | custom fusion | bytes 159744 | tf_op jit(solution)/shard_map/gather | solution.py:38
  126.3 11.9 %gather_fusion.5 = f32[3072,6]{1,0:T(8,128)} fusion(f32[6,1216]{0,1:T(8,128)} %copy.156, s32[3072]{0:T(1024)S(1)} %broadcast_clamp_fusion), kind=kCustom, calls=%fused_computation.5 | custom fusion | bytes 159744 | tf_op jit(solution)/shard_map/gather | solution.py:38
  142.6 72.8 %all-gather.2 = f32[64,3,24]{2,1,0:T(4,128)S(1)} all-gather(f32[1,3,24]{2,1,0:T(4,128)S(1)} %bitcast.134), channel_id=2, replica_groups=mesh['slab'=64,'sec'=8] {'slab'}, dimensions={0}, use_global_device_ids=true | all-gather | bytes 18720 | tf_op jit(solution)/shard_map/all_gather | solution.py:105
  222.4 5.7 collective-permute-done.11
  240.4 11.9 %gather_fusion.6 = f32[3072,6]{1,0:T(8,128)} fusion(f32[6,1216]{0,1:T(8,128)} %copy.162, s32[3072]{0:T(1024)S(1)} %broadcast_clamp_fusion), kind=kCustom, calls=%fused_computation.6 | custom fusion | bytes 159744 | tf_op jit(solution)/shard_map/gather | solution.py:38
  268.2 11.9 %gather_fusion.7 = f32[3072,6]{1,0:T(8,128)} fusion(f32[6,1216]{0,1:T(8,128)} %copy.164, s32[3072]{0:T(1024)S(1)} %broadcast_clamp_fusion), kind=kCustom, calls=%fused_computation.7 | custom fusion | bytes 159744 | tf_op jit(solution)/shard_map/gather | solution.py:38
  299.4 38.0 %collective-permute-start.18 = (f32[64,96]{1,0:T(8,128)S(1)}, f32[64,96]{1,0:T(8,128)S(1)}, u32[]{:S(2)}, u32[]{:S(2)}) collective-permute-start(f32[64,96]{1,0:T(8,128)S(1)} %get-tuple-element.83), channel_id=1, source_target_pairs={{0,1},{1,2},{2,3},{3,4},{4,5},{5,6},{6,7},{7,8},{8,9},{9,10},{10,1... | collective-permute-start | bytes 73736 | tf_op jit(solution)/shard_map/ppermute | solution.py:21
  339.5 8.5 %collective-permute-done.19 = f32[64,96]{1,0:T(8,128)S(1)} collective-permute-done((f32[64,96]{1,0:T(8,128)S(1)}, f32[64,96]{1,0:T(8,128)S(1)}, u32[]{:S(2)}, u32[]{:S(2)}) %collective-permute-start.19) | collective-permute-done | bytes 24608 | tf_op jit(solution)/shard_map/ppermute | solution.py:22
  357.8 8.2 %collective-permute-done.21 = f32[64,96]{1,0:T(8,128)S(1)} collective-permute-done((f32[64,96]{1,0:T(8,128)S(1)}, f32[64,96]{1,0:T(8,128)S(1)}, u32[]{:S(2)}, u32[]{:S(2)}) %collective-permute-start.21) | collective-permute-done | bytes 24608 | tf_op jit(solution)/shard_map/ppermute | solution.py:22
  375.7 8.2 %collective-permute-done.23 = f32[64,96]{1,0:T(8,128)S(1)} collective-permute-done((f32[64,96]{1,0:T(8,128)S(1)}, f32[64,96]{1,0:T(8,128)S(1)}, u32[]{:S(2)}, u32[]{:S(2)}) %collective-permute-start.23) | collective-permute-done | bytes 24608 | tf_op jit(solution)/shard_map/ppermute | solution.py:22
  396.7 8.2 %collective-permute-done.25 = f32[64,96]{1,0:T(8,128)S(1)} collective-permute-done((f32[64,96]{1,0:T(8,128)S(1)}, f32[64,96]{1,0:T(8,128)S(1)}, u32[]{:S(2)}, u32[]{:S(2)}) %collective-permute-start.25) | collective-permute-done | bytes 24608 | tf_op jit(solution)/shard_map/ppermute | solution.py:22
  417.7 8.2 %collective-permute-done.27 = f32[64,96]{1,0:T(8,128)S(1)} collective-permute-done((f32[64,96]{1,0:T(8,128)S(1)}, f32[64,96]{1,0:T(8,128)S(1)}, u32[]{:S(2)}, u32[]{:S(2)}) %collective-permute-start.27) | collective-permute-done | bytes 24608 | tf_op jit(solution)/shard_map/ppermute | solution.py:22
  440.1 24.5 %psum.15 = f32[6,1216]{1,0:T(8,128)S(1)} all-reduce(f32[6,1216]{1,0:T(8,128)} %copy.179), channel_id=1, replica_groups=mesh['slab'=64,'sec'=8] {'sec'}, use_global_device_ids=true, to_apply=%region_20.21 | all-reduce | flops 7296 | bytes 58368 | tf_op jit(solution)/shard_map/psum | solution.py:96
  485.4 11.9 %gather_fusion.14 = f32[3072,6]{1,0:T(8,128)} fusion(f32[6,1216]{0,1:T(8,128)} %copy.180, s32[3072]{0:T(1024)S(1)} %broadcast_clamp_fusion), kind=kCustom, calls=%fused_computation.14 | custom fusion | bytes 159744 | tf_op jit(solution)/shard_map/gather | solution.py:38
  511.8 11.9 %gather_fusion.15 = f32[3072,6]{1,0:T(8,128)} fusion(f32[6,1216]{0,1:T(8,128)} %copy.182, s32[3072]{0:T(1024)S(1)} %broadcast_clamp_fusion), kind=kCustom, calls=%fused_computation.15 | custom fusion | bytes 159744 | tf_op jit(solution)/shard_map/gather | solution.py:38
  528.8 70.7 %all-gather.3 = f32[64,3,24]{2,1,0:T(4,128)S(1)} all-gather(f32[1,3,24]{2,1,0:T(4,128)S(1)} %bitcast.135), channel_id=3, replica_groups=mesh['slab'=64,'sec'=8] {'slab'}, dimensions={0}, use_global_device_ids=true | all-gather | bytes 18720 | tf_op jit(solution)/shard_map/all_gather | solution.py:105
  609.6 5.7 collective-permute-done.35
  627.6 11.9 %gather_fusion.16 = f32[3072,6]{1,0:T(8,128)} fusion(f32[6,1216]{0,1:T(8,128)} %copy.188, s32[3072]{0:T(1024)S(1)} %broadcast_clamp_fusion), kind=kCustom, calls=%fused_computation.16 | custom fusion | bytes 159744 | tf_op jit(solution)/shard_map/gather | solution.py:38
  655.3 11.9 %gather_fusion.17 = f32[3072,6]{1,0:T(8,128)} fusion(f32[6,1216]{0,1:T(8,128)} %copy.190, s32[3072]{0:T(1024)S(1)} %broadcast_clamp_fusion), kind=kCustom, calls=%fused_computation.17 | custom fusion | bytes 159744 | tf_op jit(solution)/shard_map/gather | solution.py:38
  686.5 38.0 %collective-permute-start.42 = (f32[64,96]{1,0:T(8,128)S(1)}, f32[64,96]{1,0:T(8,128)S(1)}, u32[]{:S(2)}, u32[]{:S(2)}) collective-permute-start(f32[64,96]{1,0:T(8,128)S(1)} %get-tuple-element.63), channel_id=1, source_target_pairs={{0,1},{1,2},{2,3},{3,4},{4,5},{5,6},{6,7},{7,8},{8,9},{9,10},{10,1... | collective-permute-start | bytes 73736 | tf_op jit(solution)/shard_map/ppermute | solution.py:21
  726.5 8.7 %collective-permute-done.43 = f32[64,96]{1,0:T(8,128)S(1)} collective-permute-done((f32[64,96]{1,0:T(8,128)S(1)}, f32[64,96]{1,0:T(8,128)S(1)}, u32[]{:S(2)}, u32[]{:S(2)}) %collective-permute-start.43) | collective-permute-done | bytes 24608 | tf_op jit(solution)/shard_map/ppermute | solution.py:22
  744.9 8.2 %collective-permute-done.45 = f32[64,96]{1,0:T(8,128)S(1)} collective-permute-done((f32[64,96]{1,0:T(8,128)S(1)}, f32[64,96]{1,0:T(8,128)S(1)}, u32[]{:S(2)}, u32[]{:S(2)}) %collective-permute-start.45) | collective-permute-done | bytes 24608 | tf_op jit(solution)/shard_map/ppermute | solution.py:22
  (303 shorter events, 316.9 us)
Async XLA Ops:
  4.9 11.6 %collective-permute-start = (f32[64,96]{1,0:T(8,128)S(1)}, f32[64,96]{1,0:T(8,128)S(1)}, u32[]{:S(2)}, u32[]{:S(2)}) collective-permute-start(f32[64,96]{1,0:T(8,128)S(1)} %get-tuple-element.97), channel_id=1, source_target_pairs={{0,1},{1,2},{2,3},{3,4},{4,5},{5,6},{6,7},{7,8},{8,9},{9,10},{10,1... | collective-permute-start | bytes 73736 | tf_op jit(solution)/shard_map/ppermute | solution.py:21
  9.8 10.7 %collective-permute-start.1 = (f32[64,96]{1,0:T(8,128)S(1)}, f32[64,96]{1,0:T(8,128)S(1)}, u32[]{:S(2)}, u32[]{:S(2)}) collective-permute-start(f32[64,96]{1,0:T(8,128)S(1)} %get-tuple-element.98), channel_id=1, source_target_pairs={{1,0},{2,1},{3,2},{4,3},{5,4},{6,5},{7,6},{8,7},{9,8},{10,9},{11,1... | collective-permute-start | bytes 73736 | tf_op jit(solution)/shard_map/ppermute | solution.py:22
  25.9 7.7 %collective-permute-start.2 = (f32[64,96]{1,0:T(8,128)S(1)}, f32[64,96]{1,0:T(8,128)S(1)}, u32[]{:S(2)}, u32[]{:S(2)}) collective-permute-start(f32[64,96]{1,0:T(8,128)S(1)} %get-tuple-element.95), channel_id=1, source_target_pairs={{0,1},{1,2},{2,3},{3,4},{4,5},{5,6},{6,7},{7,8},{8,9},{9,10},{10,1... | collective-permute-start | bytes 73736 | tf_op jit(solution)/shard_map/ppermute | solution.py:21
  31.1 10.7 %collective-permute-start.3 = (f32[64,96]{1,0:T(8,128)S(1)}, f32[64,96]{1,0:T(8,128)S(1)}, u32[]{:S(2)}, u32[]{:S(2)}) collective-permute-start(f32[64,96]{1,0:T(8,128)S(1)} %get-tuple-element.96), channel_id=1, source_target_pairs={{1,0},{2,1},{3,2},{4,3},{5,4},{6,5},{7,6},{8,7},{9,8},{10,9},{11,1... | collective-permute-start | bytes 73736 | tf_op jit(solution)/shard_map/ppermute | solution.py:22
  91.7 7.7 %collective-permute-start.7 = (f32[6,96]{1,0:T(8,128)S(1)}, f32[6,96]{1,0:T(8,128)S(1)}, u32[]{:S(2)}, u32[]{:S(2)}) collective-permute-start(f32[6,96]{1,0:T(8,128)S(1)} %get-tuple-element.93), channel_id=1, source_target_pairs={{8,0},{16,8},{24,16},{32,24},{40,32},{48,40},{56,48},{64,56},{72,6... | collective-permute-start | bytes 6920 | tf_op jit(solution)/shard_map/ppermute | solution.py:22
  117.4 7.7 %collective-permute-start.9 = (f32[6,96]{1,0:T(8,128)S(1)}, f32[6,96]{1,0:T(8,128)S(1)}, u32[]{:S(2)}, u32[]{:S(2)}) collective-permute-start(f32[6,96]{1,0:T(8,128)S(1)} %get-tuple-element.91), channel_id=1, source_target_pairs={{8,0},{16,8},{24,16},{32,24},{40,32},{48,40},{56,48},{64,56},{72,6... | collective-permute-start | bytes 6920 | tf_op jit(solution)/shard_map/ppermute | solution.py:22
  231.5 7.7 %collective-permute-start.13 = (f32[6,96]{1,0:T(8,128)S(1)}, f32[6,96]{1,0:T(8,128)S(1)}, u32[]{:S(2)}, u32[]{:S(2)}) collective-permute-start(f32[6,96]{1,0:T(8,128)S(1)} %get-tuple-element.89), channel_id=1, source_target_pairs={{8,0},{16,8},{24,16},{32,24},{40,32},{48,40},{56,48},{64,56},{72,6... | collective-permute-start | bytes 6920 | tf_op jit(solution)/shard_map/ppermute | solution.py:22
  257.9 7.7 %collective-permute-start.15 = (f32[6,96]{1,0:T(8,128)S(1)}, f32[6,96]{1,0:T(8,128)S(1)}, u32[]{:S(2)}, u32[]{:S(2)}) collective-permute-start(f32[6,96]{1,0:T(8,128)S(1)} %get-tuple-element.87), channel_id=1, source_target_pairs={{8,0},{16,8},{24,16},{32,24},{40,32},{48,40},{56,48},{64,56},{72,6... | collective-permute-start | bytes 6920 | tf_op jit(solution)/shard_map/ppermute | solution.py:22
  285.7 7.7 %collective-permute-start.17 = (f32[6,96]{1,0:T(8,128)S(1)}, f32[6,96]{1,0:T(8,128)S(1)}, u32[]{:S(2)}, u32[]{:S(2)}) collective-permute-start(f32[6,96]{1,0:T(8,128)S(1)} %get-tuple-element.85), channel_id=1, source_target_pairs={{8,0},{16,8},{24,16},{32,24},{40,32},{48,40},{56,48},{64,56},{72,6... | collective-permute-start | bytes 6920 | tf_op jit(solution)/shard_map/ppermute | solution.py:22
  299.4 40.1 %collective-permute-start.18 = (f32[64,96]{1,0:T(8,128)S(1)}, f32[64,96]{1,0:T(8,128)S(1)}, u32[]{:S(2)}, u32[]{:S(2)}) collective-permute-start(f32[64,96]{1,0:T(8,128)S(1)} %get-tuple-element.83), channel_id=1, source_target_pairs={{0,1},{1,2},{2,3},{3,4},{4,5},{5,6},{6,7},{7,8},{8,9},{9,10},{10,1... | collective-permute-start | bytes 73736 | tf_op jit(solution)/shard_map/ppermute | solution.py:21
  337.4 10.7 %collective-permute-start.19 = (f32[64,96]{1,0:T(8,128)S(1)}, f32[64,96]{1,0:T(8,128)S(1)}, u32[]{:S(2)}, u32[]{:S(2)}) collective-permute-start(f32[64,96]{1,0:T(8,128)S(1)} %get-tuple-element.84), channel_id=1, source_target_pairs={{1,0},{2,1},{3,2},{4,3},{5,4},{6,5},{7,6},{8,7},{9,8},{10,9},{11,1... | collective-permute-start | bytes 73736 | tf_op jit(solution)/shard_map/ppermute | solution.py:22
  355.4 10.7 %collective-permute-start.21 = (f32[64,96]{1,0:T(8,128)S(1)}, f32[64,96]{1,0:T(8,128)S(1)}, u32[]{:S(2)}, u32[]{:S(2)}) collective-permute-start(f32[64,96]{1,0:T(8,128)S(1)} %get-tuple-element.82), channel_id=1, source_target_pairs={{1,0},{2,1},{3,2},{4,3},{5,4},{6,5},{7,6},{8,7},{9,8},{10,9},{11,1... | collective-permute-start | bytes 73736 | tf_op jit(solution)/shard_map/ppermute | solution.py:22
  373.3 10.7 %collective-permute-start.23 = (f32[64,96]{1,0:T(8,128)S(1)}, f32[64,96]{1,0:T(8,128)S(1)}, u32[]{:S(2)}, u32[]{:S(2)}) collective-permute-start(f32[64,96]{1,0:T(8,128)S(1)} %get-tuple-element.80), channel_id=1, source_target_pairs={{1,0},{2,1},{3,2},{4,3},{5,4},{6,5},{7,6},{8,7},{9,8},{10,9},{11,1... | collective-permute-start | bytes 73736 | tf_op jit(solution)/shard_map/ppermute | solution.py:22
  394.3 10.7 %collective-permute-start.25 = (f32[64,96]{1,0:T(8,128)S(1)}, f32[64,96]{1,0:T(8,128)S(1)}, u32[]{:S(2)}, u32[]{:S(2)}) collective-permute-start(f32[64,96]{1,0:T(8,128)S(1)} %get-tuple-element.78), channel_id=1, source_target_pairs={{1,0},{2,1},{3,2},{4,3},{5,4},{6,5},{7,6},{8,7},{9,8},{10,9},{11,1... | collective-permute-start | bytes 73736 | tf_op jit(solution)/shard_map/ppermute | solution.py:22
  415.3 10.7 %collective-permute-start.27 = (f32[64,96]{1,0:T(8,128)S(1)}, f32[64,96]{1,0:T(8,128)S(1)}, u32[]{:S(2)}, u32[]{:S(2)}) collective-permute-start(f32[64,96]{1,0:T(8,128)S(1)} %get-tuple-element.76), channel_id=1, source_target_pairs={{1,0},{2,1},{3,2},{4,3},{5,4},{6,5},{7,6},{8,7},{9,8},{10,9},{11,1... | collective-permute-start | bytes 73736 | tf_op jit(solution)/shard_map/ppermute | solution.py:22
  466.6 7.7 %collective-permute-start.29 = (f32[6,96]{1,0:T(8,128)S(1)}, f32[6,96]{1,0:T(8,128)S(1)}, u32[]{:S(2)}, u32[]{:S(2)}) collective-permute-start(f32[6,96]{1,0:T(8,128)S(1)} %get-tuple-element.57), channel_id=1, source_target_pairs={{8,0},{16,8},{24,16},{32,24},{40,32},{48,40},{56,48},{64,56},{72,6... | collective-permute-start | bytes 6920 | tf_op jit(solution)/shard_map/ppermute | solution.py:30
  476.6 7.7 %collective-permute-start.31 = (f32[6,96]{1,0:T(8,128)S(1)}, f32[6,96]{1,0:T(8,128)S(1)}, u32[]{:S(2)}, u32[]{:S(2)}) collective-permute-start(f32[6,96]{1,0:T(8,128)S(1)} %get-tuple-element.73), channel_id=1, source_target_pairs={{8,0},{16,8},{24,16},{32,24},{40,32},{48,40},{56,48},{64,56},{72,6... | collective-permute-start | bytes 6920 | tf_op jit(solution)/shard_map/ppermute | solution.py:22
  502.9 7.7 %collective-permute-start.33 = (f32[6,96]{1,0:T(8,128)S(1)}, f32[6,96]{1,0:T(8,128)S(1)}, u32[]{:S(2)}, u32[]{:S(2)}) collective-permute-start(f32[6,96]{1,0:T(8,128)S(1)} %get-tuple-element.71), channel_id=1, source_target_pairs={{8,0},{16,8},{24,16},{32,24},{40,32},{48,40},{56,48},{64,56},{72,6... | collective-permute-start | bytes 6920 | tf_op jit(solution)/shard_map/ppermute | solution.py:22
  618.7 7.7 %collective-permute-start.37 = (f32[6,96]{1,0:T(8,128)S(1)}, f32[6,96]{1,0:T(8,128)S(1)}, u32[]{:S(2)}, u32[]{:S(2)}) collective-permute-start(f32[6,96]{1,0:T(8,128)S(1)} %get-tuple-element.69), channel_id=1, source_target_pairs={{8,0},{16,8},{24,16},{32,24},{40,32},{48,40},{56,48},{64,56},{72,6... | collective-permute-start | bytes 6920 | tf_op jit(solution)/shard_map/ppermute | solution.py:22
  645.1 7.7 %collective-permute-start.39 = (f32[6,96]{1,0:T(8,128)S(1)}, f32[6,96]{1,0:T(8,128)S(1)}, u32[]{:S(2)}, u32[]{:S(2)}) collective-permute-start(f32[6,96]{1,0:T(8,128)S(1)} %get-tuple-element.67), channel_id=1, source_target_pairs={{8,0},{16,8},{24,16},{32,24},{40,32},{48,40},{56,48},{64,56},{72,6... | collective-permute-start | bytes 6920 | tf_op jit(solution)/shard_map/ppermute | solution.py:22
  672.9 7.7 %collective-permute-start.41 = (f32[6,96]{1,0:T(8,128)S(1)}, f32[6,96]{1,0:T(8,128)S(1)}, u32[]{:S(2)}, u32[]{:S(2)}) collective-permute-start(f32[6,96]{1,0:T(8,128)S(1)} %get-tuple-element.65), channel_id=1, source_target_pairs={{8,0},{16,8},{24,16},{32,24},{40,32},{48,40},{56,48},{64,56},{72,6... | collective-permute-start | bytes 6920 | tf_op jit(solution)/shard_map/ppermute | solution.py:22
  686.5 40.0 %collective-permute-start.42 = (f32[64,96]{1,0:T(8,128)S(1)}, f32[64,96]{1,0:T(8,128)S(1)}, u32[]{:S(2)}, u32[]{:S(2)}) collective-permute-start(f32[64,96]{1,0:T(8,128)S(1)} %get-tuple-element.63), channel_id=1, source_target_pairs={{0,1},{1,2},{2,3},{3,4},{4,5},{5,6},{6,7},{7,8},{8,9},{9,10},{10,1... | collective-permute-start | bytes 73736 | tf_op jit(solution)/shard_map/ppermute | solution.py:21
  724.6 10.7 %collective-permute-start.43 = (f32[64,96]{1,0:T(8,128)S(1)}, f32[64,96]{1,0:T(8,128)S(1)}, u32[]{:S(2)}, u32[]{:S(2)}) collective-permute-start(f32[64,96]{1,0:T(8,128)S(1)} %get-tuple-element.64), channel_id=1, source_target_pairs={{1,0},{2,1},{3,2},{4,3},{5,4},{6,5},{7,6},{8,7},{9,8},{10,9},{11,1... | collective-permute-start | bytes 73736 | tf_op jit(solution)/shard_map/ppermute | solution.py:22
  742.5 10.7 %collective-permute-start.45 = (f32[64,96]{1,0:T(8,128)S(1)}, f32[64,96]{1,0:T(8,128)S(1)}, u32[]{:S(2)}, u32[]{:S(2)}) collective-permute-start(f32[64,96]{1,0:T(8,128)S(1)} %get-tuple-element.62), channel_id=1, source_target_pairs={{1,0},{2,1},{3,2},{4,3},{5,4},{6,5},{7,6},{8,7},{9,8},{10,9},{11,1... | collective-permute-start | bytes 73736 | tf_op jit(solution)/shard_map/ppermute | solution.py:22
  (39 other events, 689.8 us)
where the time goes:
time: 763 us; the launch traced here: 759 us
  local copies, waits for them, and re-layouts  195 us (26%)
  blocking collectives  192 us (25%)
  starting transfers between devices  191 us (25%)
  waiting for transfers between devices  131 us (17%)
  other arithmetic  49.2 us (6%)
    all_gather x2, blocking collectives, shards(): every = lax.all_gather(parts[None], 'slab', axis=0, tiled=True)  144 us
    ppermute x21, waiting for transfers between devices, padded(): after = lax.ppermute(leading, axis, down)  124 us
    ppermute x21, starting transfers between devices, padded(): before = lax.ppermute(last, axis, up)  123 us
    gather x17, local copies, waits for them, and re-layouts, apply_local(): picked = jnp.swapaxes(extended[:, local_cols], 0, 1)  115 us
    ppermute x21, starting transfers between devices, padded(): after = lax.ppermute(leading, axis, down)  57.4 us
    psum x2, blocking collectives, shards(): partial_sum = lax.psum(partial_sum, 'sec')  48.3 us
    transpose x17, local copies, waits for them, and re-layouts, apply_local(): picked = jnp.swapaxes(extended[:, local_cols], 0, 1)  30.7 us
    concatenate x29, local copies, waits for them, and re-layouts, padded(): array = jnp.concatenate([before, array, after], axis=dim)  25 us
  transfers between devices with their start and end apart: 46, of which 23 were waited for; matrix products, arithmetic and copies ran while one was open for 1% of the time, Pallas kernels for 0%

commit v1 on v0

v1 whole, which is shorter than its diff:
```python
import jax
import jax.numpy as jnp
from jax import lax
from jax.experimental import pallas as pl
from jax.experimental.pallas import tpu as pltpu
from jax.sharding import PartitionSpec as P

CYCLES = 2
KEEP = 1.0 / 7.0
FRESH = 8.0 / 7.0
LANES = 128
SUB = 8
EXT = 3
SPILL = EXT + 1
F32 = jnp.float32
BF16 = jnp.bfloat16
VMEM = pl.BlockSpec(memory_space=pltpu.VMEM)
SMEM = pl.BlockSpec(memory_space=pltpu.SMEM)


def call(body, outs, in_specs, scratch=(), flops=1 << 20, moved=1 << 20):
    return pl.pallas_call(
        body,
        out_shape=outs,
        in_specs=in_specs,
        out_specs=[VMEM] * len(outs),
        scratch_shapes=list(scratch),
        compiler_params=pltpu.CompilerParams(vmem_limit_bytes=24 << 20),
        cost_estimate=pl.CostEstimate(flops=flops, bytes_accessed=moved, transcendentals=0),
    )


def struct(*shape, dtype=F32):
    return jax.ShapeDtypeStruct(shape, dtype)


def take(x, lane):
    return jnp.take_along_axis(x, lane, axis=1, mode="promise_in_bounds")


def pick(three, target):
    lane = jnp.broadcast_to(target & (LANES - 1), three[0].shape)
    block = jnp.broadcast_to((target + LANES) >> 7, three[0].shape)
    a, b, c = (take(x, lane) for x in three)
    return jnp.where(block == 0, a, jnp.where(block == 1, b, c))


def fold_rows(terms):
    row = lax.broadcasted_iota(jnp.int32, (SUB, LANES), 0)
    for step in (4, 2, 1):
        high = (row & step) != 0
        half = len(terms) // 2
        folded = []
        for i in range(half):
            low_sum = terms[i] + pltpu.roll(terms[i], SUB - step, 0)
            high_sum = terms[i + half] + pltpu.roll(terms[i + half], step, 0)
            folded.append(jnp.where(high, high_sum, low_sum))
        terms = folded
    return terms[0]


def split3(x):
    high = x.astype(BF16)
    rest = x - high.astype(F32)
    middle = rest.astype(BF16)
    low = (rest - middle.astype(F32)).astype(BF16)
    return high, middle, low


def lanes_dot(a, b):
    return lax.dot_general(a, b, (((1,), (1,)), ((), ())), preferred_element_type=F32)


def base_and_iota(where_ref, slot):
    return where_ref[slot]


def load_halo(where_ref, pair_ref, odd_ref, ext):
    parity = where_ref[0]
    ext[1] = pair_ref[parity]
    ext[2 - 2 * parity] = pair_ref[1 - parity]
    ext[2 * parity] = odd_ref[...]


def fine_product(where_ref, matrix_ref, pattern_ref, ext, picked, out):
    rows = out.shape[0]
    base = where_ref[1]
    picked[0] = ext[1]
    for k in (1, 2):
        target = pattern_ref[k : k + 1, :] - base
        lane = jnp.broadcast_to(target & (LANES - 1), (SUB, LANES))
        block = jnp.broadcast_to((target + LANES) >> 7, (SUB, LANES))
        for t in range(rows // SUB):
            part = pl.ds(t * SUB, SUB)
            a, b, c = (take(ext[i, part, :], lane) for i in range(3))
            picked[k, part, :] = jnp.where(block == 0, a, jnp.where(block == 1, b, c))

    def group(g, carry):
        terms = []
        for p in range(SUB):
            total = None
            for k in range(3):
                block = matrix_ref[k, g * SUB + p].astype(F32)
                product = jnp.sum((block * picked[k]).reshape(rows // SUB, SUB, LANES), axis=0)
                total = product if total is None else total + product
            terms.append(total)
        out[pl.ds(pl.multiple_of(g * SUB, SUB), SUB), :] = fold_rows(terms)
        return carry

    lax.fori_loop(0, rows // SUB, group, 0)


def first_body(matrix_ref, source_ref, inverse_ref, field_ref):
    rows = source_ref.shape[0]
    row = lax.broadcasted_iota(jnp.int32, (SUB, LANES), 0)
    for g in range(rows // SUB):
        part = pl.ds(g * SUB, SUB)
        diagonal = jnp.zeros((SUB, LANES), F32)
        for p in range(SUB):
            entry = matrix_ref[0, g * SUB + p].astype(F32)[g * SUB : (g + 1) * SUB]
            diagonal = jnp.where(row == p, entry, diagonal)
        inverse = 1.0 / diagonal
        inverse_ref[part, :] = inverse
        field_ref[part, :] = inverse * source_ref[part, :]


def field_body(where_ref, pair_ref, odd_ref, matrix_ref, pattern_ref, source_ref, inverse_ref, change_ref, field_ref, ext, picked, out):
    load_halo(where_ref, pair_ref, odd_ref, ext)
    fine_product(where_ref, matrix_ref, pattern_ref, ext, picked, out)
    change = inverse_ref[...] * (source_ref[...] - out[...])
    change_ref[...] = change
    field_ref[...] = ext[1] + change


def solution_body(where_ref, pair_ref, odd_ref, matrix_ref, pattern_ref, source_ref, inverse_ref, change_ref, field_ref, ext, picked, out):
    load_halo(where_ref, pair_ref, odd_ref, ext)
    fine_product(where_ref, matrix_ref, pattern_ref, ext, picked, out)
    second = KEEP * change_ref[...] + FRESH * inverse_ref[...] * (source_ref[...] - out[...])
    field_ref[...] = ext[1] + second


def restrict_body(where_ref, pair_ref, odd_ref, matrix_ref, pattern_ref, source_ref, prolong_ref, targets_ref, sums_ref, ext, picked, out):
    load_halo(where_ref, pair_ref, odd_ref, ext)
    fine_product(where_ref, matrix_ref, pattern_ref, ext, picked, out)
    residual = source_ref[...] - out[...]
    modes = prolong_ref.shape[1]
    rows = residual.shape[0]
    slots = lax.broadcasted_iota(jnp.int32, (3 * LANES, LANES), 0)
    total = None
    for k in range(3):
        terms = []
        for m in range(SUB):
            if m < modes:
                product = prolong_ref[k, m].astype(F32) * residual
                terms.append(jnp.sum(product.reshape(rows // SUB, SUB, LANES), axis=0))
            else:
                terms.append(jnp.zeros((SUB, LANES), F32))
        parts = split3(fold_rows(terms))
        target = targets_ref[k : k + 1, :] - where_ref[1] + LANES
        hot = (slots == target).astype(F32).astype(BF16)
        stacked = jnp.concatenate([p.astype(F32) for p in parts] + [jnp.zeros((SUB, LANES), F32)], axis=0)
        spread = lanes_dot(stacked.astype(BF16), hot)
        total = spread if total is None else total + spread
    sums = total[0:SUB] + total[SUB : 2 * SUB] + total[2 * SUB : 3 * SUB]
    for i in range(sums_ref.shape[0]):
        sums_ref[i] = sums


def setup_body(own_cols, where_ref, left_ref, right_ref, blocks_ref, pattern_ref, section_ref, matrix_ref, sections_ref, offset_ref, inverse_ref):
    modes = blocks_ref.shape[1]
    count = own_cols // LANES
    width = section_ref.shape[2]
    matrix_ref[...] = jnp.zeros_like(matrix_ref)
    row = lax.broadcasted_iota(jnp.int32, (SUB, LANES), 0)
    column = lax.broadcasted_iota(jnp.int32, (1, LANES), 1)
    at_offset = 3 * modes * modes
    at_section = at_offset + 2
    for b in range(count + 2 * EXT):
        inner = EXT <= b < EXT + count
        side = left_ref if b < EXT else right_ref
        at = b - EXT if inner else (b if b < EXT else b - EXT - count)
        cols = pl.ds(at * LANES, LANES)
        diagonal = jnp.zeros((SUB, LANES), F32)
        for k in range(3):
            for p in range(modes):
                if inner:
                    entry = blocks_ref[k, p, :, cols].astype(F32)
                else:
                    entry = side[pl.ds((k * modes + p) * modes, modes), cols]
                matrix_ref[b, k, p, 0:modes, :] = entry
                if k == 0:
                    diagonal = jnp.where(row == p, entry[p : p + 1, :], diagonal)
            for p in range(modes):
                if inner:
                    sections_ref[b, k, p] = section_ref[k, p, :, cols].astype(F32)
                else:
                    sections_ref[b, k, p] = side[pl.ds(at_section + (k * modes + p) * width, width), cols]
        inverse_ref[b] = jnp.where(row < modes, 1.0 / jnp.where(row < modes, diagonal, 1.0), 0.0)
        for k in range(2):
            if inner:
                offset = pattern_ref[k + 1 : k + 2, cols] - (where_ref[2] + at * LANES) - column
            else:
                offset = side[at_offset + k : at_offset + k + 1, cols].astype(jnp.int32)
            offset_ref[b, k : k + 1, :] = jnp.clip(offset, -LANES, LANES)


def coarse_product(matrix_ref, offset_ref, field, b):
    lanes = lax.broadcasted_iota(jnp.int32, (1, LANES), 1)
    three = [field[b + i] for i in range(3)]
    picked = [three[1]] + [pick(three, lanes + offset_ref[b, k : k + 1, :]) for k in range(2)]
    terms = []
    modes = matrix_ref.shape[2]
    for p in range(SUB):
        if p < modes:
            terms.append(sum(matrix_ref[b, k, p] * picked[k] for k in range(3)))
        else:
            terms.append(jnp.zeros((SUB, LANES), F32))
    return fold_rows(terms)


def gather_body(parts_ref, low_ref, all_ref, high_ref):
    count = parts_ref.shape[0]
    blocks = []
    for b in range(-1, count + 1):
        total = None
        for device in (b - 1, b, b + 1):
            if 0 <= device < count:
                at = (b - device + 1) * LANES
                term = parts_ref[device, :, at : at + LANES]
                total = term if total is None else total + term
        blocks.append(total)
    for i, block in enumerate(blocks):
        all_ref[i] = block
    for i in range(SPILL):
        low_ref[i] = blocks[i]
        high_ref[i] = blocks[count + 2 - SPILL + i]


def coarse_down_body(all_ref, below_ref, above_ref, matrix_ref, offset_ref, inverse_ref, section_ref, rhs_ref, sol_ref, top_ref, field, other):
    total = matrix_ref.shape[0]
    count = total - 2 * EXT
    modes = matrix_ref.shape[2]
    width = section_ref.shape[2]
    zero = jnp.zeros((SUB, LANES), F32)
    for b in range(total):
        terms = []
        at = b - (EXT - 1)
        if 0 <= at < count + 2:
            terms.append(all_ref[at])
        if b < SPILL:
            terms.append(below_ref[b])
        if b >= total - SPILL:
            terms.append(above_ref[b - (total - SPILL)])
        value = sum(terms[1:], terms[0])
        rhs_ref[b] = value
        field[b + 1] = inverse_ref[b] * value
    for edge in (0, total + 1):
        field[edge] = zero
        other[edge] = zero

    def first(b, carry):
        start = field[b + 1]
        second = KEEP * start + FRESH * inverse_ref[b] * (rhs_ref[b] - coarse_product(matrix_ref, offset_ref, field, b))
        other[b + 1] = start + second
        sol_ref[b] = start + second
        return carry

    lax.fori_loop(0, total, first, 0)

    def down(i, carry):
        b = i + EXT
        residual = rhs_ref[b] - coarse_product(matrix_ref, offset_ref, other, b)
        cols = pl.ds(pl.multiple_of(i * LANES, LANES), LANES)
        out = []
        for k in range(3):
            value = carry[k]
            for p in range(modes):
                value = value + section_ref[k, p, :, cols].astype(F32) * residual[p : p + 1, :]
            out.append(value)
        return tuple(out)

    sums = lax.fori_loop(0, count, down, tuple(jnp.zeros((width, LANES), F32) for _ in range(3)))
    stacked = jnp.concatenate(list(sums) + [jnp.zeros((LANES - 3 * width, LANES), F32)], axis=0)
    ones = jnp.ones((16, LANES), BF16)
    row = sum(lanes_dot(ones, part) for part in split3(stacked))
    top_ref[...] = jnp.broadcast_to(row[0:1], top_ref.shape)


def coarse_up_body(where_ref, parts_ref, top_inverse_ref, rhs_ref, sol_ref, matrix_ref, offset_ref, inverse_ref, sections_ref, fine_ref, prolong_ref, targets_ref, field_out, padded, column, field, other, final):
    total = matrix_ref.shape[0]
    count = total - 2 * EXT
    modes = matrix_ref.shape[2]
    width = sections_ref.shape[3]
    sections = parts_ref.shape[0]
    zero = jnp.zeros((SUB, LANES), F32)
    padded[0:SUB, :] = zero
    padded[pl.ds(SUB + sections, SUB), :] = zero
    padded[pl.ds(SUB, sections), :] = parts_ref[...]
    same = pltpu.roll(parts_ref[...], LANES - width, 1)
    upper = padded[pl.ds(SUB + 1, sections), :]
    lower = pltpu.roll(padded[pl.ds(SUB - 1, sections), :], LANES - 2 * width, 1)
    top = same + upper + lower
    answer = jnp.zeros((sections, LANES), F32)
    for c in range(width):
        answer = answer + top_inverse_ref[c] * top[:, c : c + 1]
    answer = jnp.sum(answer, axis=0, keepdims=True)
    rows = lax.broadcasted_iota(jnp.int32, (LANES, LANES), 0)
    lanes = lax.broadcasted_iota(jnp.int32, (LANES, LANES), 1)
    spread = jnp.sum(jnp.where(rows == lanes, answer, 0.0), axis=1, keepdims=True)
    column[...] = jnp.broadcast_to(spread, (LANES, LANES))
    for edge in (0, total + 1):
        field[edge] = zero
        other[edge] = zero

    def correct(b, carry):
        shift = jnp.where(b < EXT, 0, jnp.where(b < EXT + count, 1, 2)) * width
        terms = []
        for p in range(SUB):
            if p < modes:
                value = sum(
                    sections_ref[b, k, p] * column[pl.ds(pl.multiple_of(shift + k * width, SUB), width), :] for k in range(3)
                )
                terms.append(jnp.sum(value.reshape(width // SUB, SUB, LANES), axis=0))
            else:
                terms.append(zero)
        field[b + 1] = sol_ref[b] + fold_rows(terms)
        return carry

    lax.fori_loop(0, total, correct, 0)

    def smooth_first(b, carry):
        change = inverse_ref[b] * (rhs_ref[b] - coarse_product(matrix_ref, offset_ref, field, b))
        final[b] = change
        other[b + 1] = field[b + 1] + change
        return carry

    lax.fori_loop(0, total, smooth_first, 0)

    def smooth_second(b, carry):
        second = KEEP * final[b] + FRESH * inverse_ref[b] * (rhs_ref[b] - coarse_product(matrix_ref, offset_ref, other, b))
        final[b] = other[b + 1] + second
        return carry

    lax.fori_loop(EXT - 1, EXT + count + 1, smooth_second, 0)
    at = where_ref[3] + EXT - 1
    three = [final[at + i] for i in range(3)]
    picked = [three[1]] + [pick(three, targets_ref[k : k + 1, :] - where_ref[1]) for k in (1, 2)]
    for t in range(fine_ref.shape[0] // SUB):
        part = pl.ds(t * SUB, SUB)
        value = fine_ref[part, :]
        for k in range(3):
            for m in range(modes):
                value = value + prolong_ref[k, m, part, :].astype(F32) * picked[k][m : m + 1, :]
        field_out[part, :] = value


def shards(
    source,
    fine_blocks,
    fine_pattern,
    fine_prolong,
    prolong_pattern,
    coarse_blocks,
    coarse_pattern,
    section_prolong,
    coarsest_inverse,
):
    both = ("slab", "sec")
    slabs, secs = lax.axis_size("slab"), lax.axis_size("sec")
    devices = slabs * secs
    rows, own = source.shape
    modes = fine_prolong.shape[2]
    section_rows = coarse_blocks.shape[3]
    width = section_prolong.shape[2]
    blocks = section_rows // LANES + 2 * EXT
    halo = EXT * LANES
    section = lax.axis_index("slab")
    place = lax.axis_index("sec")
    device = section * secs + place
    where = jnp.stack([place % 2, device * own, section * section_rows, place]).astype(jnp.int32)

    prolong = jnp.transpose(fine_prolong, (0, 2, 1, 3))
    swap = [(i, i + 1) for i in range(1, devices - 1, 2)] + [(i + 1, i) for i in range(1, devices - 1, 2)]
    pairs = [[2 * i, 2 * i + 1] for i in range(secs // 2)]

    def nearby(field):
        odd = lax.ppermute(field, both, swap)
        pair = lax.all_gather(field, "sec", axis_index_groups=pairs, axis=0)
        return pair, odd

    def beside(value, step):
        return lax.ppermute(value, "slab", [(i, i + step) for i in range(max(0, -step), min(slabs, slabs - step))])

    offsets = coarse_pattern[1:] - section * section_rows - jnp.arange(section_rows, dtype=jnp.int32)

    def packed(at):
        def cut(x):
            return lax.slice_in_dim(x, at, at + halo, axis=x.ndim - 1).astype(F32).reshape(-1, halo)

        return jnp.concatenate([cut(coarse_blocks), cut(offsets), cut(section_prolong)], axis=0)

    left_data = beside(packed(section_rows - halo), 1)
    right_data = beside(packed(0), -1)
    near = [beside(coarsest_inverse, step) for step in (2, 1)] + [coarsest_inverse] + [beside(coarsest_inverse, step) for step in (-1, -2)]
    top_inverse = jnp.concatenate(near + [jnp.zeros((LANES - 5 * width, coarsest_inverse.shape[1]), F32)], axis=0)
    top_inverse = jnp.transpose(top_inverse.reshape(LANES, slabs, width), (2, 1, 0))
    matrix, sections, offset, coarse_inverse = call(
        lambda *refs: setup_body(section_rows, *refs),
        [
            struct(blocks, 3, modes, SUB, LANES),
            struct(blocks, 3, modes, width, LANES),
            struct(blocks, SUB, LANES, dtype=jnp.int32),
            struct(blocks, SUB, LANES),
        ],
        [SMEM] + [VMEM] * 5,
    )(where, left_data, right_data, coarse_blocks, coarse_pattern, section_prolong)

    fine = struct(rows, own)
    work = [pltpu.VMEM((3, rows, own), F32), pltpu.VMEM((3, rows, own), F32), pltpu.VMEM((rows, own), F32)]
    inverse, start = call(first_body, [fine, fine], [VMEM] * 2)(fine_blocks, source)

    def step(body, outs, field, *rest):
        pair, odd = nearby(field)
        return call(body, outs, [SMEM] + [VMEM] * (4 + len(rest)), work)(where, pair, odd, fine_blocks, fine_pattern, *rest)

    def smooth(field):
        change, field = step(field_body, [fine, fine], field, source, inverse)
        return step(solution_body, [fine], field, source, inverse, change)[0]

    coarse = struct(blocks, SUB, LANES)
    ends = struct(SPILL, SUB, LANES)
    line = pltpu.VMEM((blocks + 2, SUB, LANES), F32)
    for cycle in range(CYCLES):
        if cycle == 0:
            solution = step(solution_body, [fine], start, source, inverse, start)[0]
        else:
            solution = smooth(solution)
        sums = step(restrict_body, [struct(secs, SUB, 3 * LANES)], solution, source, prolong, prolong_pattern)[0]
        parts = lax.all_to_all(sums, "sec", 0, 0, tiled=True)
        low, everything, high = call(gather_body, [ends, struct(secs + 2, SUB, LANES), ends], [VMEM])(parts)
        below, above = beside(high, 1), beside(low, -1)
        rhs, coarse_sol, top = call(
            coarse_down_body, [coarse, coarse, struct(slabs, LANES)], [VMEM] * 7, [line, line]
        )(everything, below, above, matrix, offset, coarse_inverse, section_prolong)
        tops = lax.all_to_all(top, "slab", 0, 0, tiled=True)
        solution = call(
            coarse_up_body,
            [fine],
            [SMEM] + [VMEM] * 11,
            [pltpu.VMEM((slabs + 2 * SUB, LANES), F32), pltpu.VMEM((LANES, LANES), F32), line, line, line],
        )(where, tops, top_inverse, rhs, coarse_sol, matrix, offset, coarse_inverse, sections, solution, prolong, prolong_pattern)[0]
        solution = smooth(solution)
    return solution


def solution(mesh):
    in_specs = (
        P(None, ("slab", "sec")),
        P(None, None, None, ("slab", "sec")),
        P(None, ("slab", "sec")),
        P(None, None, None, ("slab", "sec")),
        P(None, ("slab", "sec")),
        P(None, None, None, "slab"),
        P(None, "slab"),
        P(None, None, None, "slab"),
        P("slab", None),
    )
    out_specs = P(None, ("slab", "sec"))
    return jax.shard_map(shards, mesh=mesh, in_specs=in_specs, out_specs=out_specs, check_vma=False)
```

time: 763 us -> 281 us (0.37)
  the two profiles are of different devices: /device:TPU:127 before, /device:TPU:32 now
where the time goes in v1:
time: 281 us; the launch traced here: 279 us
  starting transfers between devices  88 us (31%)
  blocking collectives  69.8 us (25%)
  waiting for transfers between devices  51.3 us (18%)
  local copies, waits for them, and re-layouts  34.3 us (12%)
  Pallas kernels  29 us (10%)
  other arithmetic  6.56 us (2%)
    ppermute x9, waiting for transfers between devices, nearby(): odd = lax.ppermute(field, both, swap)  49.8 us
    ppermute x10, starting transfers between devices, beside(): lax.ppermute(value, 'slab', [(i, i + step) for i in range(max(0, -step),...  38.9 us
    all_to_all x1, blocking collectives, shards(): tops = lax.all_to_all(top, 'slab', 0, 0, tiled=True)  36.5 us
    ppermute x9, starting transfers between devices, nearby(): odd = lax.ppermute(field, both, swap)  27.5 us
    all_to_all x1, starting transfers between devices, shards(): tops = lax.all_to_all(top, 'slab', 0, 0, tiled=True)  21.6 us
    all_gather x9, blocking collectives, nearby(): pair = lax.all_gather(field, 'sec', axis_index_groups=pairs, axis=0)  17 us
    all_to_all x2, blocking collectives, shards(): parts = lax.all_to_all(sums, 'sec', 0, 0, tiled=True)  16.4 us
    unnamed x61, local copies, waits for them, and re-layouts  14.9 us
  transfers between devices with their start and end apart: 20, of which 9 were waited for; matrix products, arithmetic and copies ran while one was open for 8% of the time, Pallas kernels for 3%

profile of v1, /device:TPU:32, one launch (start us, length us, event | category | flops | bytes accessed | tf_op | source)
XLA Modules:
  0.0 279.4 jit_solution(5182715091998513002)
XLA Ops:
  6.4 3.4 %collective-permute-start.4 = (f32[542,384]{1,0:T(8,128)}, f32[542,384]{1,0:T(8,128)}, u32[]{:S(2)}, u32[]{:S(2)}) collective-permute-start(f32[542,384]{1,0:T(8,128)} %pad_maximum_fusion), channel_id=1, source_target_pairs={{0,8},{8,16},{16,24},{24,32},{32,40},{40,48},{48,56},{56,64},{64,7... | collective-permute-start | bytes 2497544 | tf_op jit(solution)/shard_map/ppermute | solution.py:392
  13.4 4.7 %collective-permute-start.5 = (f32[542,384]{1,0:T(8,128)}, f32[542,384]{1,0:T(8,128)}, u32[]{:S(2)}, u32[]{:S(2)}) collective-permute-start(f32[542,384]{1,0:T(8,128)} %pad_maximum_fusion.1), channel_id=1, source_target_pairs={{8,0},{16,8},{24,16},{32,24},{40,32},{48,40},{56,48},{64,56},{72,6... | collective-permute-start | bytes 2497544 | tf_op jit(solution)/shard_map/ppermute | solution.py:392
  18.2 3.5 %collective-permute-start = (f32[64,128]{1,0:T(8,128)S(1)}, f32[64,128]{1,0:T(8,128)}, u32[]{:S(2)}, u32[]{:S(2)}) collective-permute-start(f32[64,128]{1,0:T(8,128)S(1)} %get-tuple-element.29.change_ref), channel_id=1, source_target_pairs={{1,2},{3,4},{5,6},{7,8},{9,10},{11,12},{13,14},{15,16},{17,18},{19... | collective-permute-start | bytes 98312 | tf_op jit(solution)/shard_map/ppermute | solution.py:387
  23.6 12.6 %collective-permute-done.odd_ref = f32[64,128]{1,0:T(8,128)} collective-permute-done((f32[64,128]{1,0:T(8,128)S(1)}, f32[64,128]{1,0:T(8,128)}, u32[]{:S(2)}, u32[]{:S(2)}) %collective-permute-start) | collective-permute-done | bytes 32800 | tf_op jit(solution)/shard_map/ppermute | solution.py:387
  38.7 8.1 %collective-permute-start.1 = (f32[64,128]{1,0:T(8,128)S(1)}, f32[64,128]{1,0:T(8,128)S(1)}, u32[]{:S(2)}, u32[]{:S(2)}) collective-permute-start(f32[64,128]{1,0:T(8,128)S(1)} %shard_map.92.fine_ref), channel_id=1, source_target_pairs={{1,2},{3,4},{5,6},{7,8},{9,10},{11,12},{13,14},{15,16},{17,18},{19... | collective-permute-start | bytes 98312 | tf_op jit(solution)/shard_map/ppermute | solution.py:387
  50.4 8.2 %all_to_all.32.parts_ref = f32[8,8,384]{2,1,0:T(8,128)S(1)} all-to-all(f32[8,8,384]{2,1,0:T(8,128)S(1)} %shard_map.93), channel_id=1, replica_groups=mesh['slab'=64,'sec'=8] {'sec'}, dimensions={0} | all-to-all | bytes 196608 | tf_op jit(solution)/shard_map/all_to_all | solution.py:439
  60.5 8.3 %collective-permute-start.9 = (f32[24,1536]{1,0:T(8,128)}, f32[24,1536]{1,0:T(8,128)}, u32[]{:S(2)}, u32[]{:S(2)}) collective-permute-start(f32[24,1536]{1,0:T(8,128)} %param.17), channel_id=1, source_target_pairs={{16,0},{24,8},{32,16},{40,24},{48,32},{56,40},{64,48},{72,56},{80,... | collective-permute-start | bytes 442376 | tf_op jit(solution)/shard_map/ppermute | solution.py:392
  73.1 6.0 %collective-permute-start.8 = (f32[24,1536]{1,0:T(8,128)}, f32[24,1536]{1,0:T(8,128)}, u32[]{:S(2)}, u32[]{:S(2)}) collective-permute-start(f32[24,1536]{1,0:T(8,128)} %param.17), channel_id=1, source_target_pairs={{8,0},{16,8},{24,16},{32,24},{40,32},{48,40},{56,48},{64,56},{72,6... | collective-permute-start | bytes 442376 | tf_op jit(solution)/shard_map/ppermute | solution.py:392
  85.0 2.5 shard_map.96
  90.4 21.6 %all-to-all-start.1 = ((f32[64,1,128]{2,1,0:T(1,128)}), f32[64,1,128]{2,1,0:T(1,128)}, u32[]{:S(2)}, u32[]{:S(2)}) async-start(f32[64,1,128]{2,1,0:T(1,128)} %bitcast.48), calls=%async_computation.1 | async-start | bytes 65536 | tf_op jit(solution)/shard_map/all_to_all | solution.py:445
  123.4 4.4 %concatenate.11 = f32[128,1536]{0,1:T(8,128)} concatenate(f32[24,1536]{0,1:T(8,128)} %copy.17, f32[24,1536]{0,1:T(8,128)} %copy.18, f32[24,1536]{0,1:T(8,128)} %copy.19, f32[24,1536]{0,1:T(8,128)} %copy.20, f32[24,1536]{0,1:T(8,128)} %copy.21, f32[8,1536]{0,1:T(8,128)} %broadcast_in_dim.4), dimensions={0} | concatenate | bytes 1572864 | tf_op jit(solution)/shard_map/concatenate | solution.py:405
  137.6 4.1 %shard_map.97 = f32[64,128]{1,0:T(8,128)S(1)} custom-call(s32[4]{0:T(128)S(1)} %pad_add_fusion.where_ref.refs_0_, f32[64,128]{1,0:T(8,128)} %bitcast.11.parts_ref, f32[24,64,128]{2,1,0:T(8,128)S(1)} %bitcast.32, f32[14,8,128]{2,1,0:T(8,128)S(1)} %copy-done.24, f32[14,8,128]{2,1,0:T(8,128)S(1)} %copy-done.26, f32[14,3,6,8,128]{4,3,2,1,0:T(8,128)S(1)} %copy-done.2, ...), custom_call_target="tpu_custom_call" | custom-call | flops 1048576 | bytes 1048576 | tf_op jit(solution)/shard_map/pallas_call | solution.py:446
  145.9 5.3 %collective-permute-done.10.odd_ref = f32[64,128]{1,0:T(8,128)S(1)} collective-permute-done((f32[64,128]{1,0:T(8,128)S(1)}, f32[64,128]{1,0:T(8,128)S(1)}, u32[]{:S(2)}, u32[]{:S(2)}) %collective-permute-start.10) | collective-permute-done | bytes 32800 | tf_op jit(solution)/shard_map/ppermute | solution.py:387
  156.7 5.3 %collective-permute-done.11.odd_ref = f32[64,128]{1,0:T(8,128)S(1)} collective-permute-done((f32[64,128]{1,0:T(8,128)S(1)}, f32[64,128]{1,0:T(8,128)S(1)}, u32[]{:S(2)}, u32[]{:S(2)}) %collective-permute-start.11) | collective-permute-done | bytes 32800 | tf_op jit(solution)/shard_map/ppermute | solution.py:387
  167.6 5.3 %collective-permute-done.12.odd_ref = f32[64,128]{1,0:T(8,128)S(1)} collective-permute-done((f32[64,128]{1,0:T(8,128)S(1)}, f32[64,128]{1,0:T(8,128)S(1)}, u32[]{:S(2)}, u32[]{:S(2)}) %collective-permute-start.12) | collective-permute-done | bytes 32800 | tf_op jit(solution)/shard_map/ppermute | solution.py:387
  178.5 5.3 %collective-permute-done.13.odd_ref = f32[64,128]{1,0:T(8,128)S(1)} collective-permute-done((f32[64,128]{1,0:T(8,128)S(1)}, f32[64,128]{1,0:T(8,128)S(1)}, u32[]{:S(2)}, u32[]{:S(2)}) %collective-permute-start.13) | collective-permute-done | bytes 32800 | tf_op jit(solution)/shard_map/ppermute | solution.py:387
  185.2 2.6 collective-permute-start.14
  189.6 5.3 %collective-permute-done.14.odd_ref = f32[64,128]{1,0:T(8,128)S(1)} collective-permute-done((f32[64,128]{1,0:T(8,128)S(1)}, f32[64,128]{1,0:T(8,128)S(1)}, u32[]{:S(2)}, u32[]{:S(2)}) %collective-permute-start.14) | collective-permute-done | bytes 32800 | tf_op jit(solution)/shard_map/ppermute | solution.py:387
  196.6 8.2 %all_to_all.33.parts_ref = f32[8,8,384]{2,1,0:T(8,128)S(1)} all-to-all(f32[8,8,384]{2,1,0:T(8,128)S(1)} %shard_map.102), channel_id=1, replica_groups=mesh['slab'=64,'sec'=8] {'sec'}, dimensions={0} | all-to-all | bytes 196608 | tf_op jit(solution)/shard_map/all_to_all | solution.py:439
  206.7 6.0 %collective-permute-start.16 = (f32[4,8,128]{2,1,0:T(8,128)S(1)}, f32[4,8,128]{2,1,0:T(8,128)S(1)}, u32[]{:S(2)}, u32[]{:S(2)}) collective-permute-start(f32[4,8,128]{2,1,0:T(8,128)S(1)} %get-tuple-element.47), channel_id=1, source_target_pairs={{8,0},{16,8},{24,16},{32,24},{40,32},{48,40},{56,48},{64,56},{72,6... | collective-permute-start | bytes 49160 | tf_op jit(solution)/shard_map/ppermute | solution.py:392
  216.6 36.5 %all_to_all.34 = f32[64,1,128]{2,1,0:T(1,128)S(1)} all-to-all(f32[64,1,128]{2,1,0:T(1,128)S(1)} %bitcast.49), channel_id=1, replica_groups=mesh['slab'=64,'sec'=8] {'slab'}, dimensions={0} | all-to-all | bytes 65536 | tf_op jit(solution)/shard_map/all_to_all | solution.py:445
  253.1 3.9 %shard_map.105 = f32[64,128]{1,0:T(8,128)S(1)} custom-call(s32[4]{0:T(128)S(1)} %pad_add_fusion.where_ref.refs_0_, f32[64,128]{1,0:T(8,128)S(1)} %bitcast.47, f32[24,64,128]{2,1,0:T(8,128)S(1)} %bitcast.33, f32[14,8,128]{2,1,0:T(8,128)S(1)} %get-tuple-element.49.rhs_ref, f32[14,8,128]{2,1,0:T(8,128)S(1)} %get-tuple-element.50.sol_ref, ...), custom_call_target="tpu_custom_call" | custom-call | flops 1048576 | bytes 1048576 | tf_op jit(solution)/shard_map/pallas_call | solution.py:446
  261.2 5.3 %collective-permute-done.17.odd_ref = f32[64,128]{1,0:T(8,128)S(1)} collective-permute-done((f32[64,128]{1,0:T(8,128)S(1)}, f32[64,128]{1,0:T(8,128)S(1)}, u32[]{:S(2)}, u32[]{:S(2)}) %collective-permute-start.17) | collective-permute-done | bytes 32800 | tf_op jit(solution)/shard_map/ppermute | solution.py:387
  272.0 5.4 %collective-permute-done.18.odd_ref = f32[64,128]{1,0:T(8,128)S(1)} collective-permute-done((f32[64,128]{1,0:T(8,128)S(1)}, f32[64,128]{1,0:T(8,128)S(1)}, u32[]{:S(2)}, u32[]{:S(2)}) %collective-permute-start.18) | collective-permute-done | bytes 32800 | tf_op jit(solution)/shard_map/ppermute | solution.py:387
  (124 shorter events, 97.0 us)
Async XLA Ops:
  6.4 66.7 %collective-permute-start.4 = (f32[542,384]{1,0:T(8,128)}, f32[542,384]{1,0:T(8,128)}, u32[]{:S(2)}, u32[]{:S(2)}) collective-permute-start(f32[542,384]{1,0:T(8,128)} %pad_maximum_fusion), channel_id=1, source_target_pairs={{0,8},{8,16},{16,24},{24,32},{32,40},{40,48},{48,56},{56,64},{64,7... | collective-permute-start | bytes 2497544 | tf_op jit(solution)/shard_map/ppermute | solution.py:392
  13.4 65.8 %collective-permute-start.5 = (f32[542,384]{1,0:T(8,128)}, f32[542,384]{1,0:T(8,128)}, u32[]{:S(2)}, u32[]{:S(2)}) collective-permute-start(f32[542,384]{1,0:T(8,128)} %pad_maximum_fusion.1), channel_id=1, source_target_pairs={{8,0},{16,8},{24,16},{32,24},{40,32},{48,40},{56,48},{64,56},{72,6... | collective-permute-start | bytes 2497544 | tf_op jit(solution)/shard_map/ppermute | solution.py:392
  18.2 18.0 %collective-permute-start = (f32[64,128]{1,0:T(8,128)S(1)}, f32[64,128]{1,0:T(8,128)}, u32[]{:S(2)}, u32[]{:S(2)}) collective-permute-start(f32[64,128]{1,0:T(8,128)S(1)} %get-tuple-element.29.change_ref), channel_id=1, source_target_pairs={{1,2},{3,4},{5,6},{7,8},{9,10},{11,12},{13,14},{15,16},{17,18},{19... | collective-permute-start | bytes 98312 | tf_op jit(solution)/shard_map/ppermute | solution.py:387
  37.0 44.5 %copy-start.27 = (s32[3,1024]{1,0:T(4,128)S(1)}, s32[3,1024]{1,0:T(4,128)}, u32[]{:S(2)}) copy-start(s32[3,1024]{1,0:T(4,128)} %refs_4_.1) | copy-start | bytes 36868
  38.7 10.0 %collective-permute-start.1 = (f32[64,128]{1,0:T(8,128)S(1)}, f32[64,128]{1,0:T(8,128)S(1)}, u32[]{:S(2)}, u32[]{:S(2)}) collective-permute-start(f32[64,128]{1,0:T(8,128)S(1)} %shard_map.92.fine_ref), channel_id=1, source_target_pairs={{1,2},{3,4},{5,6},{7,8},{9,10},{11,12},{13,14},{15,16},{17,18},{19... | collective-permute-start | bytes 98312 | tf_op jit(solution)/shard_map/ppermute | solution.py:387
  58.6 12.6 %collective-permute-start.2 = (f32[4,8,128]{2,1,0:T(8,128)S(1)}, f32[4,8,128]{2,1,0:T(8,128)S(1)}, u32[]{:S(2)}, u32[]{:S(2)}) collective-permute-start(f32[4,8,128]{2,1,0:T(8,128)S(1)} %get-tuple-element.32), channel_id=1, source_target_pairs={{0,8},{8,16},{16,24},{24,32},{32,40},{40,48},{48,56},{56,64},{64,7... | collective-permute-start | bytes 49160 | tf_op jit(solution)/shard_map/ppermute | solution.py:392
  60.5 53.6 %collective-permute-start.9 = (f32[24,1536]{1,0:T(8,128)}, f32[24,1536]{1,0:T(8,128)}, u32[]{:S(2)}, u32[]{:S(2)}) collective-permute-start(f32[24,1536]{1,0:T(8,128)} %param.17), channel_id=1, source_target_pairs={{16,0},{24,8},{32,16},{40,24},{48,32},{56,40},{64,48},{72,56},{80,... | collective-permute-start | bytes 442376 | tf_op jit(solution)/shard_map/ppermute | solution.py:392
  68.8 47.4 %collective-permute-start.6 = (f32[24,1536]{1,0:T(8,128)}, f32[24,1536]{1,0:T(8,128)}, u32[]{:S(2)}, u32[]{:S(2)}) collective-permute-start(f32[24,1536]{1,0:T(8,128)} %param.17), channel_id=1, source_target_pairs={{0,16},{8,24},{16,32},{24,40},{32,48},{40,56},{48,64},{56,72},{64,... | collective-permute-start | bytes 442376 | tf_op jit(solution)/shard_map/ppermute | solution.py:392
  71.2 47.1 %collective-permute-start.7 = (f32[24,1536]{1,0:T(8,128)}, f32[24,1536]{1,0:T(8,128)}, u32[]{:S(2)}, u32[]{:S(2)}) collective-permute-start(f32[24,1536]{1,0:T(8,128)} %param.17), channel_id=1, source_target_pairs={{0,8},{8,16},{16,24},{24,32},{32,40},{40,48},{48,56},{56,64},{64,7... | collective-permute-start | bytes 442376 | tf_op jit(solution)/shard_map/ppermute | solution.py:392
  73.1 47.2 %collective-permute-start.8 = (f32[24,1536]{1,0:T(8,128)}, f32[24,1536]{1,0:T(8,128)}, u32[]{:S(2)}, u32[]{:S(2)}) collective-permute-start(f32[24,1536]{1,0:T(8,128)} %param.17), channel_id=1, source_target_pairs={{8,0},{16,8},{24,16},{32,24},{40,32},{48,40},{56,48},{64,56},{72,6... | collective-permute-start | bytes 442376 | tf_op jit(solution)/shard_map/ppermute | solution.py:392
  79.2 5.8 %collective-permute-start.3 = (f32[4,8,128]{2,1,0:T(8,128)S(1)}, f32[4,8,128]{2,1,0:T(8,128)S(1)}, u32[]{:S(2)}, u32[]{:S(2)}) collective-permute-start(f32[4,8,128]{2,1,0:T(8,128)S(1)} %get-tuple-element.33), channel_id=1, source_target_pairs={{8,0},{16,8},{24,16},{32,24},{40,32},{48,40},{56,48},{64,56},{72,6... | collective-permute-start | bytes 49160 | tf_op jit(solution)/shard_map/ppermute | solution.py:392
  90.4 39.7 %all-to-all-start.1 = ((f32[64,1,128]{2,1,0:T(1,128)}), f32[64,1,128]{2,1,0:T(1,128)}, u32[]{:S(2)}, u32[]{:S(2)}) async-start(f32[64,1,128]{2,1,0:T(1,128)} %bitcast.48), calls=%async_computation.1 | async-start | bytes 65536 | tf_op jit(solution)/shard_map/all_to_all | solution.py:445
  141.7 9.5 %collective-permute-start.10 = (f32[64,128]{1,0:T(8,128)S(1)}, f32[64,128]{1,0:T(8,128)S(1)}, u32[]{:S(2)}, u32[]{:S(2)}) collective-permute-start(f32[64,128]{1,0:T(8,128)S(1)} %shard_map.97), channel_id=1, source_target_pairs={{1,2},{3,4},{5,6},{7,8},{9,10},{11,12},{13,14},{15,16},{17,18},{19... | collective-permute-start | bytes 98312 | tf_op jit(solution)/shard_map/ppermute | solution.py:387
  152.6 9.5 %collective-permute-start.11 = (f32[64,128]{1,0:T(8,128)S(1)}, f32[64,128]{1,0:T(8,128)S(1)}, u32[]{:S(2)}, u32[]{:S(2)}) collective-permute-start(f32[64,128]{1,0:T(8,128)S(1)} %get-tuple-element.41), channel_id=1, source_target_pairs={{1,2},{3,4},{5,6},{7,8},{9,10},{11,12},{13,14},{15,16},{17,18},{19... | collective-permute-start | bytes 98312 | tf_op jit(solution)/shard_map/ppermute | solution.py:387
  163.4 9.5 %collective-permute-start.12 = (f32[64,128]{1,0:T(8,128)S(1)}, f32[64,128]{1,0:T(8,128)S(1)}, u32[]{:S(2)}, u32[]{:S(2)}) collective-permute-start(f32[64,128]{1,0:T(8,128)S(1)} %shard_map.99), channel_id=1, source_target_pairs={{1,2},{3,4},{5,6},{7,8},{9,10},{11,12},{13,14},{15,16},{17,18},{19... | collective-permute-start | bytes 98312 | tf_op jit(solution)/shard_map/ppermute | solution.py:387
  174.3 9.5 %collective-permute-start.13 = (f32[64,128]{1,0:T(8,128)S(1)}, f32[64,128]{1,0:T(8,128)S(1)}, u32[]{:S(2)}, u32[]{:S(2)}) collective-permute-start(f32[64,128]{1,0:T(8,128)S(1)} %get-tuple-element.43), channel_id=1, source_target_pairs={{1,2},{3,4},{5,6},{7,8},{9,10},{11,12},{13,14},{15,16},{17,18},{19... | collective-permute-start | bytes 98312 | tf_op jit(solution)/shard_map/ppermute | solution.py:387
  185.2 67.9 %copy-start.8 = (f32[14,3,6,24,128]{4,3,2,1,0:T(8,128)S(1)}, f32[14,3,6,24,128]{4,3,2,1,0:T(8,128)}, u32[]{:S(2)}) copy-start(f32[14,3,6,24,128]{4,3,2,1,0:T(8,128)} %copy-done.6) | copy-start | bytes 9289732
  185.2 67.9 %copy-start.10 = (f32[128,64,24]{0,1,2:T(8,128)S(1)}, f32[128,64,24]{0,1,2:T(8,128)}, u32[]{:S(2)}) copy-start(f32[128,64,24]{0,1,2:T(8,128)} %copy.25) | copy-start | bytes 2359300
  185.2 67.9 %copy-start.15 = (s32[14,8,128]{2,1,0:T(8,128)S(1)}, s32[14,8,128]{2,1,0:T(8,128)}, u32[]{:S(2)}) copy-start(s32[14,8,128]{2,1,0:T(8,128)} %copy-done.13) | copy-start | bytes 172036
  185.2 9.7 %collective-permute-start.14 = (f32[64,128]{1,0:T(8,128)S(1)}, f32[64,128]{1,0:T(8,128)S(1)}, u32[]{:S(2)}, u32[]{:S(2)}) collective-permute-start(f32[64,128]{1,0:T(8,128)S(1)} %shard_map.101.fine_ref), channel_id=1, source_target_pairs={{1,2},{3,4},{5,6},{7,8},{9,10},{11,12},{13,14},{15,16},{17,18},{19... | collective-permute-start | bytes 98312 | tf_op jit(solution)/shard_map/ppermute | solution.py:387
  204.7 8.0 %collective-permute-start.15 = (f32[4,8,128]{2,1,0:T(8,128)S(1)}, f32[4,8,128]{2,1,0:T(8,128)S(1)}, u32[]{:S(2)}, u32[]{:S(2)}) collective-permute-start(f32[4,8,128]{2,1,0:T(8,128)S(1)} %get-tuple-element.46), channel_id=1, source_target_pairs={{0,8},{8,16},{16,24},{24,32},{32,40},{40,48},{48,56},{56,64},{64,7... | collective-permute-start | bytes 49160 | tf_op jit(solution)/shard_map/ppermute | solution.py:392
  206.7 7.5 %collective-permute-start.16 = (f32[4,8,128]{2,1,0:T(8,128)S(1)}, f32[4,8,128]{2,1,0:T(8,128)S(1)}, u32[]{:S(2)}, u32[]{:S(2)}) collective-permute-start(f32[4,8,128]{2,1,0:T(8,128)S(1)} %get-tuple-element.47), channel_id=1, source_target_pairs={{8,0},{16,8},{24,16},{32,24},{40,32},{48,40},{56,48},{64,56},{72,6... | collective-permute-start | bytes 49160 | tf_op jit(solution)/shard_map/ppermute | solution.py:392
  257.1 9.5 %collective-permute-start.17 = (f32[64,128]{1,0:T(8,128)S(1)}, f32[64,128]{1,0:T(8,128)S(1)}, u32[]{:S(2)}, u32[]{:S(2)}) collective-permute-start(f32[64,128]{1,0:T(8,128)S(1)} %shard_map.105), channel_id=1, source_target_pairs={{1,2},{3,4},{5,6},{7,8},{9,10},{11,12},{13,14},{15,16},{17,18},{19... | collective-permute-start | bytes 98312 | tf_op jit(solution)/shard_map/ppermute | solution.py:387
  267.9 9.5 %collective-permute-start.18 = (f32[64,128]{1,0:T(8,128)S(1)}, f32[64,128]{1,0:T(8,128)S(1)}, u32[]{:S(2)}, u32[]{:S(2)}) collective-permute-start(f32[64,128]{1,0:T(8,128)S(1)} %get-tuple-element.51), channel_id=1, source_target_pairs={{1,2},{3,4},{5,6},{7,8},{9,10},{11,12},{13,14},{15,16},{17,18},{19... | collective-permute-start | bytes 98312 | tf_op jit(solution)/shard_map/ppermute | solution.py:387
  (26 other events, 343.6 us)

commit v2 on v1

--- a/solution.py
+++ b/solution.py
@@ -69,10 +69,6 @@
 
 def lanes_dot(a, b):
     return lax.dot_general(a, b, (((1,), (1,)), ((), ())), preferred_element_type=F32)
-
-
-def base_and_iota(where_ref, slot):
-    return where_ref[slot]
 
 
 def load_halo(where_ref, pair_ref, odd_ref, ext):
@@ -166,15 +162,41 @@
         sums_ref[i] = sums
 
 
-def setup_body(own_cols, where_ref, left_ref, right_ref, blocks_ref, pattern_ref, section_ref, matrix_ref, sections_ref, offset_ref, inverse_ref):
+def pack_body(where_ref, blocks_ref, pattern_ref, top_ref, prolong_ref, targets_ref, low_ref, high_ref, fine_ref):
     modes = blocks_ref.shape[1]
-    count = own_cols // LANES
-    width = section_ref.shape[2]
+    total = blocks_ref.shape[3]
+    halo = low_ref.shape[1]
+    width = top_ref.shape[0]
+    column = lax.broadcasted_iota(jnp.int32, (1, halo), 1)
+    for out, at in ((low_ref, 0), (high_ref, total - halo)):
+        cols = pl.ds(at, halo)
+        for k in range(3):
+            for p in range(modes):
+                row = (k * modes + p) * SUB
+                out[row : row + modes, :] = blocks_ref[k, p, :, cols].astype(F32)
+        row = 3 * modes * SUB
+        for k in range(2):
+            offset = pattern_ref[k + 1 : k + 2, cols] - (where_ref[2] + at) - column
+            out[row + k : row + k + 1, :] = offset.astype(F32)
+        row += SUB
+        for i in range(top_ref.shape[1] // halo):
+            out[row + i * width : row + (i + 1) * width, :] = top_ref[:, i * halo : (i + 1) * halo]
+    rows = prolong_ref.shape[2]
+    for k in range(3):
+        for m in range(modes):
+            at = (k * modes + m) * rows
+            fine_ref[at : at + rows, :] = prolong_ref[k, m].astype(F32)
+        at = 3 * modes * rows + k
+        fine_ref[at : at + 1, :] = targets_ref[k : k + 1, :].astype(F32)
+
+
+def setup_body(where_ref, left_ref, right_ref, blocks_ref, pattern_ref, matrix_ref, offset_ref, inverse_ref):
+    modes = blocks_ref.shape[1]
+    count = blocks_ref.shape[3] // LANES
     matrix_ref[...] = jnp.zeros_like(matrix_ref)
     row = lax.broadcasted_iota(jnp.int32, (SUB, LANES), 0)
     column = lax.broadcasted_iota(jnp.int32, (1, LANES), 1)
-    at_offset = 3 * modes * modes
-    at_section = at_offset + 2
+    at_offset = 3 * modes * SUB
     for b in range(count + 2 * EXT):
         inner = EXT <= b < EXT + count
         side = left_ref if b < EXT else right_ref
@@ -186,15 +208,10 @@
                 if inner:
                     entry = blocks_ref[k, p, :, cols].astype(F32)
                 else:
-                    entry = side[pl.ds((k * modes + p) * modes, modes), cols]
+                    entry = side[pl.ds((k * modes + p) * SUB, modes), cols]
                 matrix_ref[b, k, p, 0:modes, :] = entry
                 if k == 0:
                     diagonal = jnp.where(row == p, entry[p : p + 1, :], diagonal)
-            for p in range(modes):
-                if inner:
-                    sections_ref[b, k, p] = section_ref[k, p, :, cols].astype(F32)
-                else:
-                    sections_ref[b, k, p] = side[pl.ds(at_section + (k * modes + p) * width, width), cols]
         inverse_ref[b] = jnp.where(row < modes, 1.0 / jnp.where(row < modes, diagonal, 1.0), 0.0)
         for k in range(2):
             if inner:
@@ -236,7 +253,7 @@
         high_ref[i] = blocks[count + 2 - SPILL + i]
 
 
-def coarse_down_body(all_ref, below_ref, above_ref, matrix_ref, offset_ref, inverse_ref, section_ref, rhs_ref, sol_ref, top_ref, field, other):
+def coarse_down_body(where_ref, all_ref, below_ref, above_ref, matrix_ref, offset_ref, inverse_ref, section_ref, rhs_ref, sol_ref, top_ref, field, other):
     total = matrix_ref.shape[0]
     count = total - 2 * EXT
     modes = matrix_ref.shape[2]
@@ -283,50 +300,102 @@
     stacked = jnp.concatenate(list(sums) + [jnp.zeros((LANES - 3 * width, LANES), F32)], axis=0)
     ones = jnp.ones((16, LANES), BF16)
     row = sum(lanes_dot(ones, part) for part in split3(stacked))
-    top_ref[...] = jnp.broadcast_to(row[0:1], top_ref.shape)
-
-
-def coarse_up_body(where_ref, parts_ref, top_inverse_ref, rhs_ref, sol_ref, matrix_ref, offset_ref, inverse_ref, sections_ref, fine_ref, prolong_ref, targets_ref, field_out, padded, column, field, other, final):
+    top_ref[...] = jnp.broadcast_to(pltpu.roll(row, where_ref[4], 1)[0:1], top_ref.shape)
+
+
+def top_body(where_ref, parts_ref, left_ref, top_inverse_ref, right_ref, sol_ref, section_ref, field_ref, edge_ref, column):
+    count, modes, width = section_ref.shape[3] // LANES, section_ref.shape[1], section_ref.shape[2]
+    sections = parts_ref.shape[0]
+    chunk_count = sections * width // LANES
+    sub = lax.broadcasted_iota(jnp.int32, (SUB, LANES), 0)
+    lane = lax.broadcasted_iota(jnp.int32, (SUB, LANES), 1)
+    chunks = [None] * chunk_count
+    for tile in range(sections // SUB):
+        first = (sub + (tile * SUB - 1)) * width
+        chunk = (first + ((lane - first) & (LANES - 1))) >> 7
+        value = parts_ref[tile * SUB : (tile + 1) * SUB, :]
+        low = (tile * SUB - 1) * width
+        for q in range(max(0, low // LANES), min(chunk_count, (low + (SUB + 2) * width) // LANES + 1)):
+            term = jnp.where(chunk == q, value, 0.0)
+            chunks[q] = term if chunks[q] is None else chunks[q] + term
+    chunks = [jnp.sum(c, axis=0, keepdims=True) for c in chunks]
+    halo = left_ref.shape[1]
+    at_top = 3 * modes * SUB + SUB
+    answers = []
+    for side in range(3):
+        total = None
+        for q in range(chunk_count):
+            if side == 1:
+                part = top_inverse_ref[:, q * LANES : (q + 1) * LANES]
+            else:
+                ref = left_ref if side == 0 else right_ref
+                i, at = divmod(q * LANES, halo)
+                part = ref[pl.ds(at_top + i * width, width), pl.ds(at, LANES)]
+            term = part * chunks[q]
+            total = term if total is None else total + term
+        answers.append(jnp.sum(total, axis=1, keepdims=True))
+    for side in range(3):
+        column[side * width : (side + 1) * width, :] = jnp.broadcast_to(answers[side], (width, LANES))
+    zero = jnp.zeros((SUB, LANES), F32)
+
+    def correct(b, carry):
+        cols = pl.ds(pl.multiple_of(b * LANES, LANES), LANES)
+        terms = []
+        for p in range(SUB):
+            if p < modes:
+                value = sum(section_ref[k, p, :, cols].astype(F32) * column[k * width : (k + 1) * width, :] for k in range(3))
+                terms.append(jnp.sum(value.reshape(width // SUB, SUB, LANES), axis=0))
+            else:
+                terms.append(zero)
+        field_ref[b] = sol_ref[b + EXT] + fold_rows(terms)
+        return carry
+
+    lax.fori_loop(0, count, correct, 0)
+    start = jnp.where(where_ref[5] > 0, count - EXT, 0)
+    for i in range(EXT):
+        edge_ref[i] = field_ref[start + i]
+
+
+def up_body(
+    where_ref,
+    middle_ref,
+    edge_ref,
+    rhs_ref,
+    matrix_ref,
+    offset_ref,
+    inverse_ref,
+    pair_ref,
+    odd_ref,
+    prolong_ref,
+    even_prolong_ref,
+    odd_prolong_ref,
+    targets_ref,
+    fine_matrix_ref,
+    fine_pattern_ref,
+    source_ref,
+    fine_inverse_ref,
+    change_ref,
+    field_ref,
+    field,
+    other,
+    final,
+    ext,
+    picked,
+    out,
+):
     total = matrix_ref.shape[0]
     count = total - 2 * EXT
     modes = matrix_ref.shape[2]
-    width = sections_ref.shape[3]
-    sections = parts_ref.shape[0]
     zero = jnp.zeros((SUB, LANES), F32)
-    padded[0:SUB, :] = zero
-    padded[pl.ds(SUB + sections, SUB), :] = zero
-    padded[pl.ds(SUB, sections), :] = parts_ref[...]
-    same = pltpu.roll(parts_ref[...], LANES - width, 1)
-    upper = padded[pl.ds(SUB + 1, sections), :]
-    lower = pltpu.roll(padded[pl.ds(SUB - 1, sections), :], LANES - 2 * width, 1)
-    top = same + upper + lower
-    answer = jnp.zeros((sections, LANES), F32)
-    for c in range(width):
-        answer = answer + top_inverse_ref[c] * top[:, c : c + 1]
-    answer = jnp.sum(answer, axis=0, keepdims=True)
-    rows = lax.broadcasted_iota(jnp.int32, (LANES, LANES), 0)
-    lanes = lax.broadcasted_iota(jnp.int32, (LANES, LANES), 1)
-    spread = jnp.sum(jnp.where(rows == lanes, answer, 0.0), axis=1, keepdims=True)
-    column[...] = jnp.broadcast_to(spread, (LANES, LANES))
+    from_left = where_ref[5] > 0
+    for i in range(EXT):
+        field[1 + i] = jnp.where(from_left, edge_ref[i], 0.0)
+        field[1 + EXT + count + i] = jnp.where(from_left, 0.0, edge_ref[i])
+    for i in range(count):
+        field[1 + EXT + i] = middle_ref[i]
     for edge in (0, total + 1):
         field[edge] = zero
         other[edge] = zero
-
-    def correct(b, carry):
-        shift = jnp.where(b < EXT, 0, jnp.where(b < EXT + count, 1, 2)) * width
-        terms = []
-        for p in range(SUB):
-            if p < modes:
-                value = sum(
-                    sections_ref[b, k, p] * column[pl.ds(pl.multiple_of(shift + k * width, SUB), width), :] for k in range(3)
-                )
-                terms.append(jnp.sum(value.reshape(width // SUB, SUB, LANES), axis=0))
-            else:
-                terms.append(zero)
-        field[b + 1] = sol_ref[b] + fold_rows(terms)
-        return carry
-
-    lax.fori_loop(0, total, correct, 0)
 
     def smooth_first(b, carry):
         change = inverse_ref[b] * (rhs_ref[b] - coarse_product(matrix_ref, offset_ref, field, b))
@@ -341,17 +410,38 @@
         final[b] = other[b + 1] + second
         return carry
 
-    lax.fori_loop(EXT - 1, EXT + count + 1, smooth_second, 0)
-    at = where_ref[3] + EXT - 1
-    three = [final[at + i] for i in range(3)]
-    picked = [three[1]] + [pick(three, targets_ref[k : k + 1, :] - where_ref[1]) for k in (1, 2)]
-    for t in range(fine_ref.shape[0] // SUB):
-        part = pl.ds(t * SUB, SUB)
-        value = fine_ref[part, :]
+    lax.fori_loop(EXT - 2, EXT + count + 2, smooth_second, 0)
+    load_halo(where_ref, pair_ref, odd_ref, ext)
+    rows = ext.shape[1]
+    parity = where_ref[0]
+    for which in range(3):
+        block = (1, 2 - 2 * parity, 2 * parity)[which]
+        side = (None, even_prolong_ref, odd_prolong_ref)[which]
+        at = where_ref[3] + EXT + block - 2
+        three = [final[at + i] for i in range(3)]
+        terms = []
         for k in range(3):
-            for m in range(modes):
-                value = value + prolong_ref[k, m, part, :].astype(F32) * picked[k][m : m + 1, :]
-        field_out[part, :] = value
+            if which == 0:
+                target = targets_ref[k : k + 1, :] - where_ref[1]
+            else:
+                row = 3 * modes * rows + k
+                target = side[row : row + 1, :].astype(jnp.int32) - (where_ref[1] + (block - 1) * LANES)
+            terms.append(three[1] if k == 0 else pick(three, target))
+        for t in range(rows // SUB):
+            part = pl.ds(t * SUB, SUB)
+            value = ext[block, part, :]
+            for k in range(3):
+                for m in range(modes):
+                    if which == 0:
+                        weight = prolong_ref[k, m, part, :].astype(F32)
+                    else:
+                        weight = side[pl.ds((k * modes + m) * rows + t * SUB, SUB), :]
+                    value = value + weight * terms[k][m : m + 1, :]
+            ext[block, part, :] = value
+    fine_product(where_ref, fine_matrix_ref, fine_pattern_ref, ext, picked, out)
+    change = fine_inverse_ref[...] * (source_ref[...] - out[...])
+    change_ref[...] = change
+    field_ref[...] = ext[1] + change
 
 
 def shards(
@@ -372,84 +462,81 @@
     modes = fine_prolong.shape[2]
     section_rows = coarse_blocks.shape[3]
     width = section_prolong.shape[2]
-    blocks = section_rows // LANES + 2 * EXT
+    count = section_rows // LANES
+    blocks = count + 2 * EXT
     halo = EXT * LANES
     section = lax.axis_index("slab")
     place = lax.axis_index("sec")
     device = section * secs + place
-    where = jnp.stack([place % 2, device * own, section * section_rows, place]).astype(jnp.int32)
+    roll = ((section + LANES - 1) * width) % LANES
+    from_left = (place < secs // 2).astype(jnp.int32)
+    where = jnp.stack([place % 2, device * own, section * section_rows, place, roll, from_left]).astype(jnp.int32)
 
     prolong = jnp.transpose(fine_prolong, (0, 2, 1, 3))
-    swap = [(i, i + 1) for i in range(1, devices - 1, 2)] + [(i + 1, i) for i in range(1, devices - 1, 2)]
+    odd_swap = [(i, i + 1) for i in range(1, devices - 1, 2)] + [(i + 1, i) for i in range(1, devices - 1, 2)]
+    even_swap = [(i, i ^ 1) for i in range(devices)]
     pairs = [[2 * i, 2 * i + 1] for i in range(secs // 2)]
+    reach = [c for c in range(secs // 2) if c < EXT]
+    edge_moves = [(s * secs + c, (s + 1) * secs + c) for s in range(slabs - 1) for c in reach]
+    edge_moves += [((s + 1) * secs + secs - 1 - c, s * secs + secs - 1 - c) for s in range(slabs - 1) for c in reach]
 
     def nearby(field):
-        odd = lax.ppermute(field, both, swap)
+        odd = lax.ppermute(field, both, odd_swap)
         pair = lax.all_gather(field, "sec", axis_index_groups=pairs, axis=0)
         return pair, odd
 
     def beside(value, step):
         return lax.ppermute(value, "slab", [(i, i + step) for i in range(max(0, -step), min(slabs, slabs - step))])
-
-    offsets = coarse_pattern[1:] - section * section_rows - jnp.arange(section_rows, dtype=jnp.int32)
-
-    def packed(at):
-        def cut(x):
-            return lax.slice_in_dim(x, at, at + halo, axis=x.ndim - 1).astype(F32).reshape(-1, halo)
-
-        return jnp.concatenate([cut(coarse_blocks), cut(offsets), cut(section_prolong)], axis=0)
-
-    left_data = beside(packed(section_rows - halo), 1)
-    right_data = beside(packed(0), -1)
-    near = [beside(coarsest_inverse, step) for step in (2, 1)] + [coarsest_inverse] + [beside(coarsest_inverse, step) for step in (-1, -2)]
-    top_inverse = jnp.concatenate(near + [jnp.zeros((LANES - 5 * width, coarsest_inverse.shape[1]), F32)], axis=0)
-    top_inverse = jnp.transpose(top_inverse.reshape(LANES, slabs, width), (2, 1, 0))
-    matrix, sections, offset, coarse_inverse = call(
-        lambda *refs: setup_body(section_rows, *refs),
-        [
-            struct(blocks, 3, modes, SUB, LANES),
-            struct(blocks, 3, modes, width, LANES),
-            struct(blocks, SUB, LANES, dtype=jnp.int32),
-            struct(blocks, SUB, LANES),
-        ],
-        [SMEM] + [VMEM] * 5,
-    )(where, left_data, right_data, coarse_blocks, coarse_pattern, section_prolong)
 
     fine = struct(rows, own)
     work = [pltpu.VMEM((3, rows, own), F32), pltpu.VMEM((3, rows, own), F32), pltpu.VMEM((rows, own), F32)]
     inverse, start = call(first_body, [fine, fine], [VMEM] * 2)(fine_blocks, source)
 
-    def step(body, outs, field, *rest):
-        pair, odd = nearby(field)
-        return call(body, outs, [SMEM] + [VMEM] * (4 + len(rest)), work)(where, pair, odd, fine_blocks, fine_pattern, *rest)
-
-    def smooth(field):
-        change, field = step(field_body, [fine, fine], field, source, inverse)
-        return step(solution_body, [fine], field, source, inverse, change)[0]
+    side = struct(3 * modes * SUB + SUB + width * (coarsest_inverse.shape[1] // halo), halo)
+    low, high, fine_pack = call(pack_body, [side, side, struct(3 * modes * rows + SUB, own)], [SMEM] + [VMEM] * 5)(
+        where, coarse_blocks, coarse_pattern, coarsest_inverse, prolong, prolong_pattern
+    )
+    left_data, right_data = beside(high, 1), beside(low, -1)
+    odd_prolong = lax.ppermute(fine_pack, both, odd_swap)
+    even_prolong = lax.ppermute(fine_pack, both, even_swap)
+    matrix, offset, coarse_inverse = call(
+        setup_body,
+        [struct(blocks, 3, modes, SUB, LANES), struct(blocks, SUB, LANES, dtype=jnp.int32), struct(blocks, SUB, LANES)],
+        [SMEM] + [VMEM] * 4,
+    )(where, left_data, right_data, coarse_blocks, coarse_pattern)
+
+    def step(body, outs, near, *rest):
+        return call(body, outs, [SMEM] + [VMEM] * (4 + len(rest)), work)(where, *near, fine_blocks, fine_pattern, *rest)
 
     coarse = struct(blocks, SUB, LANES)
     ends = struct(SPILL, SUB, LANES)
     line = pltpu.VMEM((blocks + 2, SUB, LANES), F32)
     for cycle in range(CYCLES):
         if cycle == 0:
-            solution = step(solution_body, [fine], start, source, inverse, start)[0]
+            change = field = start
         else:
-            solution = smooth(solution)
-        sums = step(restrict_body, [struct(secs, SUB, 3 * LANES)], solution, source, prolong, prolong_pattern)[0]
+            change, field = step(field_body, [fine, fine], nearby(solution), source, inverse)
+        solution = step(solution_body, [fine], nearby(field), source, inverse, change)[0]
+        near = nearby(solution)
+        sums = step(restrict_body, [struct(secs, SUB, 3 * LANES)], near, source, prolong, prolong_pattern)[0]
         parts = lax.all_to_all(sums, "sec", 0, 0, tiled=True)
         low, everything, high = call(gather_body, [ends, struct(secs + 2, SUB, LANES), ends], [VMEM])(parts)
         below, above = beside(high, 1), beside(low, -1)
         rhs, coarse_sol, top = call(
-            coarse_down_body, [coarse, coarse, struct(slabs, LANES)], [VMEM] * 7, [line, line]
-        )(everything, below, above, matrix, offset, coarse_inverse, section_prolong)
+            coarse_down_body, [coarse, coarse, struct(slabs, LANES)], [SMEM] + [VMEM] * 7, [line, line]
+        )(where, everything, below, above, matrix, offset, coarse_inverse, section_prolong)
         tops = lax.all_to_all(top, "slab", 0, 0, tiled=True)
-        solution = call(
-            coarse_up_body,
-            [fine],
-            [SMEM] + [VMEM] * 11,
-            [pltpu.VMEM((slabs + 2 * SUB, LANES), F32), pltpu.VMEM((LANES, LANES), F32), line, line, line],
-        )(where, tops, top_inverse, rhs, coarse_sol, matrix, offset, coarse_inverse, sections, solution, prolong, prolong_pattern)[0]
-        solution = smooth(solution)
+        middle, edge = call(
+            top_body,
+            [struct(count, SUB, LANES), struct(EXT, SUB, LANES)],
+            [SMEM] + [VMEM] * 6,
+            [pltpu.VMEM((3 * width, LANES), F32)],
+        )(where, tops, left_data, coarsest_inverse, right_data, coarse_sol, section_prolong)
+        edge = lax.ppermute(edge, both, edge_moves)
+        change, field = call(up_body, [fine, fine], [SMEM] + [VMEM] * 16, [line, line, line] + work)(
+            where, middle, edge, rhs, matrix, offset, coarse_inverse, *near, prolong, even_prolong, odd_prolong, prolong_pattern, fine_blocks, fine_pattern, source, inverse
+        )
+        solution = step(solution_body, [fine], nearby(field), source, inverse, change)[0]
     return solution
 
 

time: 281 us -> 238 us (0.85)
  starting transfers between devices: 88 us -> 53.9 us
  blocking collectives: 69.8 us -> 98.4 us
  local copies, waits for them, and re-layouts: 34.3 us -> 6.99 us
  other arithmetic: 6.56 us -> 0 us
  waiting for transfers between devices: 51.3 us -> 48.1 us
    all_to_all x1 -> x2, blocking collectives: 36.5 us -> 68.1 us  [shards(): tops = lax.all_to_all(top, 'slab', 0, 0, tiled=True)]
    all_to_all x1 -> x0, starting transfers between devices: 21.6 us -> none  [shards(): tops = lax.all_to_all(top, 'slab', 0, 0, tiled=True)]
    ppermute x10 -> x6, starting transfers between devices: 38.9 us -> 23.9 us  [beside(): lax.ppermute(value, 'slab', [(i, i + step) for i in range(max(0, -step),...]
    ppermute x4 -> x0, local copies, waits for them, and re-layouts: 8.38 us -> none  [beside(): lax.ppermute(value, 'slab', [(i, i + step) for i in range(max(0, -step),...]
    unnamed x61 -> x30, local copies, waits for them, and re-layouts: 14.9 us -> 6.91 us
    reshape x3 -> x0, local copies, waits for them, and re-layouts: 4.52 us -> none  [the longest x2 2.32 us: cut(): lax.slice_in_dim(x, at, at + halo, axis=x.ndim - 1).astype(F32)]
    concatenate x1 -> x0, local copies, waits for them, and re-layouts: 4.41 us -> none  [shards(): jnp.concatenate(near + [jnp.zeros((LANES - 5 * width, coarsest_inverse.sh...]
    concatenate x2 -> x0, other arithmetic: 3.91 us -> none  [packed(): jnp.concatenate([cut(coarse_blocks), cut(offsets), cut(section_prolong)],...]
  transfers between devices with their start and end apart: 20 -> 17, of which waited for: 9 -> 11; matrix products, arithmetic and copies ran while one was open for 8% -> 0% of each run, Pallas kernels for 3% -> 3%
where the time goes in v2:
time: 238 us; the launch traced here: 237 us
  blocking collectives  98.4 us (41%)
  starting transfers between devices  53.9 us (23%)
  waiting for transfers between devices  48.1 us (20%)
  Pallas kernels  29.1 us (12%)
  local copies, waits for them, and re-layouts  6.99 us (3%)
    all_to_all x2, blocking collectives, shards(): tops = lax.all_to_all(top, 'slab', 0, 0, tiled=True)  68.1 us
    ppermute x7, waiting for transfers between devices, nearby(): odd = lax.ppermute(field, both, odd_swap)  35.5 us
    ppermute x6, starting transfers between devices, beside(): lax.ppermute(value, 'slab', [(i, i + step) for i in range(max(0, -step),...  23.9 us
    ppermute x7, starting transfers between devices, nearby(): odd = lax.ppermute(field, both, odd_swap)  17.2 us
    all_to_all x2, blocking collectives, shards(): parts = lax.all_to_all(sums, 'sec', 0, 0, tiled=True)  16.6 us
    all_gather x7, blocking collectives, nearby(): pair = lax.all_gather(field, 'sec', axis_index_groups=pairs, axis=0)  13.6 us
    pallas_call x7, Pallas kernels, step(): call(body, outs, [SMEM] + [VMEM] * (4 + len(rest)), work)  11 us
    ppermute x2, waiting for transfers between devices, shards(): edge = lax.ppermute(edge, both, edge_moves)  10.5 us
  transfers between devices with their start and end apart: 17, of which 11 were waited for; matrix products, arithmetic and copies ran while one was open for 0% of the time, Pallas kernels for 3%

profile of v2, /device:TPU:32, one launch (start us, length us, event | category | flops | bytes accessed | tf_op | source)
XLA Modules:
  0.0 236.9 jit_solution(17785568741295909888)
XLA Ops:
  5.0 6.1 %collective-permute-start.8 = (f32[1160,128]{1,0:T(8,128)S(1)}, f32[1160,128]{1,0:T(8,128)S(1)}, u32[]{:S(2)}, u32[]{:S(2)}) collective-permute-start(f32[1160,128]{1,0:T(8,128)S(1)} %get-tuple-element.50), channel_id=1, source_target_pairs={{1,2},{3,4},{5,6},{7,8},{9,10},{11,12},{13,14},{15,16},{17,18},{19... | collective-permute-start | bytes 1781768 | tf_op jit(solution)/shard_map/ppermute | solution.py:500
  14.9 6.0 %collective-permute-start.5 = (f32[248,384]{1,0:T(8,128)S(1)}, f32[248,384]{1,0:T(8,128)S(1)}, u32[]{:S(2)}, u32[]{:S(2)}) collective-permute-start(f32[248,384]{1,0:T(8,128)S(1)} %get-tuple-element.41), channel_id=1, source_target_pairs={{8,0},{16,8},{24,16},{32,24},{40,32},{48,40},{56,48},{64,56},{72,6... | collective-permute-start | bytes 1142792 | tf_op jit(solution)/shard_map/ppermute | solution.py:489
  27.6 5.7 %collective-permute-done.odd_ref = f32[64,128]{1,0:T(8,128)S(1)} collective-permute-done((f32[64,128]{1,0:T(8,128)S(1)}, f32[64,128]{1,0:T(8,128)S(1)}, u32[]{:S(2)}, u32[]{:S(2)}) %collective-permute-start) | collective-permute-done | bytes 32800 | tf_op jit(solution)/shard_map/ppermute | solution.py:484
  34.7 4.7 %collective-permute-start.1 = (f32[64,128]{1,0:T(8,128)S(1)}, f32[64,128]{1,0:T(8,128)S(1)}, u32[]{:S(2)}, u32[]{:S(2)}) collective-permute-start(f32[64,128]{1,0:T(8,128)S(1)} %shard_map.92), channel_id=1, source_target_pairs={{1,2},{3,4},{5,6},{7,8},{9,10},{11,12},{13,14},{15,16},{17,18},{19... | collective-permute-start | bytes 98312 | tf_op jit(solution)/shard_map/ppermute | solution.py:484
  41.2 3.0 %collective-permute-done.1.odd_ref = f32[64,128]{1,0:T(8,128)S(1)} collective-permute-done((f32[64,128]{1,0:T(8,128)S(1)}, f32[64,128]{1,0:T(8,128)S(1)}, u32[]{:S(2)}, u32[]{:S(2)}) %collective-permute-start.1) | collective-permute-done | bytes 32800 | tf_op jit(solution)/shard_map/ppermute | solution.py:484
  45.9 8.4 %all_to_all.32.parts_ref = f32[8,8,384]{2,1,0:T(8,128)S(1)} all-to-all(f32[8,8,384]{2,1,0:T(8,128)S(1)} %shard_map.93), channel_id=1, replica_groups=mesh['slab'=64,'sec'=8] {'sec'}, dimensions={0} | all-to-all | bytes 196608 | tf_op jit(solution)/shard_map/all_to_all | solution.py:522
  56.3 6.0 %collective-permute-start.3 = (f32[4,8,128]{2,1,0:T(8,128)S(1)}, f32[4,8,128]{2,1,0:T(8,128)S(1)}, u32[]{:S(2)}, u32[]{:S(2)}) collective-permute-start(f32[4,8,128]{2,1,0:T(8,128)S(1)} %get-tuple-element.39), channel_id=1, source_target_pairs={{8,0},{16,8},{24,16},{32,24},{40,32},{48,40},{56,48},{64,56},{72,6... | collective-permute-start | bytes 49160 | tf_op jit(solution)/shard_map/ppermute | solution.py:489
  63.8 3.1 %shard_map.97 = (f32[14,8,128]{2,1,0:T(8,128)S(1)}, f32[14,8,128]{2,1,0:T(8,128)S(1)}, f32[64,128]{1,0:T(8,128)S(1)}) custom-call(s32[6]{0:T(128)S(1)} %stack.31.where_ref, f32[10,8,128]{2,1,0:T(8,128)S(1)} %get-tuple-element.37.all_ref, f32[4,8,128]{2,1,0:T(8,128)S(1)} %collective-permute-done.2.below_ref, ...), custom_call_target="tpu_custom_call" | custom-call | flops 1048576 | bytes 1048576 | tf_op jit(solution)/shard_map/pallas_call | solution.py:525
  66.9 38.4 %all_to_all.33 = f32[64,1,128]{2,1,0:T(1,128)S(1)} all-to-all(f32[64,1,128]{2,1,0:T(1,128)S(1)} %bitcast.38), channel_id=1, replica_groups=mesh['slab'=64,'sec'=8] {'slab'}, dimensions={0} | all-to-all | bytes 65536 | tf_op jit(solution)/shard_map/all_to_all | solution.py:528
  106.3 2.4 %collective-permute-start.6 = (f32[3,8,128]{2,1,0:T(8,128)S(1)}, f32[3,8,128]{2,1,0:T(8,128)S(1)}, u32[]{:S(2)}, u32[]{:S(2)}) collective-permute-start(f32[3,8,128]{2,1,0:T(8,128)S(1)} %get-tuple-element.48), channel_id=1, source_target_pairs={{0,8},{1,9},{2,10},{8,16},{9,17},{10,18},{16,24},{17,25},{18,26},{... | collective-permute-start | bytes 36872 | tf_op jit(solution)/shard_map/ppermute | solution.py:535
  108.7 5.3 %collective-permute-done.6.edge_ref = f32[3,8,128]{2,1,0:T(8,128)S(1)} collective-permute-done((f32[3,8,128]{2,1,0:T(8,128)S(1)}, f32[3,8,128]{2,1,0:T(8,128)S(1)}, u32[]{:S(2)}, u32[]{:S(2)}) %collective-permute-start.6) | collective-permute-done | bytes 12320 | tf_op jit(solution)/shard_map/ppermute | solution.py:535
  114.0 4.2 %shard_map.99 = (f32[64,128]{1,0:T(8,128)S(1)}, f32[64,128]{1,0:T(8,128)S(1)}) custom-call(s32[6]{0:T(128)S(1)} %stack.31.where_ref, f32[8,8,128]{2,1,0:T(8,128)S(1)} %get-tuple-element.47.middle_ref, f32[3,8,128]{2,1,0:T(8,128)S(1)} %collective-permute-done.6.edge_ref, f32[14,8,128]{2,1,0:T(8,128)S(1)} %get-tuple-element.49.rhs_ref, ...), custom_call_target="tpu_custom_call" | custom-call | flops 1048576 | bytes 1048576 | tf_op jit(solution)/shard_map/pallas_call | solution.py:536
  122.3 5.3 %collective-permute-done.9.odd_ref = f32[64,128]{1,0:T(8,128)S(1)} collective-permute-done((f32[64,128]{1,0:T(8,128)S(1)}, f32[64,128]{1,0:T(8,128)S(1)}, u32[]{:S(2)}, u32[]{:S(2)}) %collective-permute-start.9) | collective-permute-done | bytes 32800 | tf_op jit(solution)/shard_map/ppermute | solution.py:484
  133.1 5.4 %collective-permute-done.10.odd_ref = f32[64,128]{1,0:T(8,128)S(1)} collective-permute-done((f32[64,128]{1,0:T(8,128)S(1)}, f32[64,128]{1,0:T(8,128)S(1)}, u32[]{:S(2)}, u32[]{:S(2)}) %collective-permute-start.10) | collective-permute-done | bytes 32800 | tf_op jit(solution)/shard_map/ppermute | solution.py:484
  144.0 5.4 %collective-permute-done.11.odd_ref = f32[64,128]{1,0:T(8,128)S(1)} collective-permute-done((f32[64,128]{1,0:T(8,128)S(1)}, f32[64,128]{1,0:T(8,128)S(1)}, u32[]{:S(2)}, u32[]{:S(2)}) %collective-permute-start.11) | collective-permute-done | bytes 32800 | tf_op jit(solution)/shard_map/ppermute | solution.py:484
  154.9 5.4 %collective-permute-done.12.odd_ref = f32[64,128]{1,0:T(8,128)S(1)} collective-permute-done((f32[64,128]{1,0:T(8,128)S(1)}, f32[64,128]{1,0:T(8,128)S(1)}, u32[]{:S(2)}, u32[]{:S(2)}) %collective-permute-start.12) | collective-permute-done | bytes 32800 | tf_op jit(solution)/shard_map/ppermute | solution.py:484
  162.0 8.2 %all_to_all.34.parts_ref = f32[8,8,384]{2,1,0:T(8,128)S(1)} all-to-all(f32[8,8,384]{2,1,0:T(8,128)S(1)} %shard_map.103), channel_id=1, replica_groups=mesh['slab'=64,'sec'=8] {'sec'}, dimensions={0} | all-to-all | bytes 196608 | tf_op jit(solution)/shard_map/all_to_all | solution.py:522
  172.1 6.0 %collective-permute-start.14 = (f32[4,8,128]{2,1,0:T(8,128)S(1)}, f32[4,8,128]{2,1,0:T(8,128)S(1)}, u32[]{:S(2)}, u32[]{:S(2)}) collective-permute-start(f32[4,8,128]{2,1,0:T(8,128)S(1)} %get-tuple-element.57), channel_id=1, source_target_pairs={{8,0},{16,8},{24,16},{32,24},{40,32},{48,40},{56,48},{64,56},{72,6... | collective-permute-start | bytes 49160 | tf_op jit(solution)/shard_map/ppermute | solution.py:489
  179.5 3.1 %shard_map.105 = (f32[14,8,128]{2,1,0:T(8,128)S(1)}, f32[14,8,128]{2,1,0:T(8,128)S(1)}, f32[64,128]{1,0:T(8,128)S(1)}) custom-call(s32[6]{0:T(128)S(1)} %stack.31.where_ref, f32[10,8,128]{2,1,0:T(8,128)S(1)} %get-tuple-element.55.all_ref, f32[4,8,128]{2,1,0:T(8,128)S(1)} %collective-permute-done.13.below_ref, ...), custom_call_target="tpu_custom_call" | custom-call | flops 1048576 | bytes 1048576 | tf_op jit(solution)/shard_map/pallas_call | solution.py:525
  182.6 29.8 %all_to_all.35 = f32[64,1,128]{2,1,0:T(1,128)S(1)} all-to-all(f32[64,1,128]{2,1,0:T(1,128)S(1)} %bitcast.39), channel_id=1, replica_groups=mesh['slab'=64,'sec'=8] {'slab'}, dimensions={0} | all-to-all | bytes 65536 | tf_op jit(solution)/shard_map/all_to_all | solution.py:528
  213.5 2.4 %collective-permute-start.15 = (f32[3,8,128]{2,1,0:T(8,128)S(1)}, f32[3,8,128]{2,1,0:T(8,128)S(1)}, u32[]{:S(2)}, u32[]{:S(2)}) collective-permute-start(f32[3,8,128]{2,1,0:T(8,128)S(1)} %get-tuple-element.61), channel_id=1, source_target_pairs={{0,8},{1,9},{2,10},{8,16},{9,17},{10,18},{16,24},{17,25},{18,26},{... | collective-permute-start | bytes 36872 | tf_op jit(solution)/shard_map/ppermute | solution.py:535
  215.9 5.3 %collective-permute-done.15.edge_ref = f32[3,8,128]{2,1,0:T(8,128)S(1)} collective-permute-done((f32[3,8,128]{2,1,0:T(8,128)S(1)}, f32[3,8,128]{2,1,0:T(8,128)S(1)}, u32[]{:S(2)}, u32[]{:S(2)}) %collective-permute-start.15) | collective-permute-done | bytes 12320 | tf_op jit(solution)/shard_map/ppermute | solution.py:535
  221.2 4.2 %shard_map.107 = (f32[64,128]{1,0:T(8,128)S(1)}, f32[64,128]{1,0:T(8,128)S(1)}) custom-call(s32[6]{0:T(128)S(1)} %stack.31.where_ref, f32[8,8,128]{2,1,0:T(8,128)S(1)} %get-tuple-element.60.middle_ref, f32[3,8,128]{2,1,0:T(8,128)S(1)} %collective-permute-done.15.edge_ref, f32[14,8,128]{2,1,0:T(8,128)S(1)} %get-tuple-element.62.rhs_ref, ...), custom_call_target="tpu_custom_call" | custom-call | flops 1048576 | bytes 1048576 | tf_op jit(solution)/shard_map/pallas_call | solution.py:536
  229.5 5.3 %collective-permute-done.16.odd_ref = f32[64,128]{1,0:T(8,128)S(1)} collective-permute-done((f32[64,128]{1,0:T(8,128)S(1)}, f32[64,128]{1,0:T(8,128)S(1)}, u32[]{:S(2)}, u32[]{:S(2)}) %collective-permute-start.16) | collective-permute-done | bytes 32800 | tf_op jit(solution)/shard_map/ppermute | solution.py:484
  (70 shorter events, 57.4 us)
Async XLA Ops:
  0.0 33.2 %copy-start.10 = (s32[3,128]{1,0:T(4,128)S(1)}, s32[3,128]{1,0:T(4,128)}, u32[]{:S(2)}) copy-start(s32[3,128]{1,0:T(4,128)} %pattern_ref.17) | copy-start | bytes 4612
  5.0 109.0 %collective-permute-start.8 = (f32[1160,128]{1,0:T(8,128)S(1)}, f32[1160,128]{1,0:T(8,128)S(1)}, u32[]{:S(2)}, u32[]{:S(2)}) collective-permute-start(f32[1160,128]{1,0:T(8,128)S(1)} %get-tuple-element.50), channel_id=1, source_target_pairs={{1,2},{3,4},{5,6},{7,8},{9,10},{11,12},{13,14},{15,16},{17,18},{19... | collective-permute-start | bytes 1781768 | tf_op jit(solution)/shard_map/ppermute | solution.py:500
  11.1 102.9 %collective-permute-start.7 = (f32[1160,128]{1,0:T(8,128)S(1)}, f32[1160,128]{1,0:T(8,128)S(1)}, u32[]{:S(2)}, u32[]{:S(2)}) collective-permute-start(f32[1160,128]{1,0:T(8,128)S(1)} %get-tuple-element.50), channel_id=1, source_target_pairs={{0,1},{1,0},{2,3},{3,2},{4,5},{5,4},{6,7},{7,6},{8,9},{9,8},{10,11... | collective-permute-start | bytes 1781768 | tf_op jit(solution)/shard_map/ppermute | solution.py:501
  13.0 43.3 %collective-permute-start.4 = (f32[248,384]{1,0:T(8,128)S(1)}, f32[248,384]{1,0:T(8,128)S(1)}, u32[]{:S(2)}, u32[]{:S(2)}) collective-permute-start(f32[248,384]{1,0:T(8,128)S(1)} %get-tuple-element.40), channel_id=1, source_target_pairs={{0,8},{8,16},{16,24},{24,32},{32,40},{40,48},{48,56},{56,64},{64,7... | collective-permute-start | bytes 1142792 | tf_op jit(solution)/shard_map/ppermute | solution.py:489
  14.9 47.4 %collective-permute-start.5 = (f32[248,384]{1,0:T(8,128)S(1)}, f32[248,384]{1,0:T(8,128)S(1)}, u32[]{:S(2)}, u32[]{:S(2)}) collective-permute-start(f32[248,384]{1,0:T(8,128)S(1)} %get-tuple-element.41), channel_id=1, source_target_pairs={{8,0},{16,8},{24,16},{32,24},{40,32},{48,40},{56,48},{64,56},{72,6... | collective-permute-start | bytes 1142792 | tf_op jit(solution)/shard_map/ppermute | solution.py:489
  23.6 20.6 %copy-start.14 = (s32[3,128]{1,0:T(4,128)S(1)}, s32[3,128]{1,0:T(4,128)}, u32[]{:S(2)}) copy-start(s32[3,128]{1,0:T(4,128)} %targets_ref.9) | copy-start | bytes 4612
  23.7 9.6 %collective-permute-start = (f32[64,128]{1,0:T(8,128)S(1)}, f32[64,128]{1,0:T(8,128)S(1)}, u32[]{:S(2)}, u32[]{:S(2)}) collective-permute-start(f32[64,128]{1,0:T(8,128)S(1)} %get-tuple-element.35.change_ref), channel_id=1, source_target_pairs={{1,2},{3,4},{5,6},{7,8},{9,10},{11,12},{13,14},{15,16},{17,18},{19... | collective-permute-start | bytes 98312 | tf_op jit(solution)/shard_map/ppermute | solution.py:484
  33.2 29.1 %copy-start.9 = (bf16[3,6,6,1024]{3,2,1,0:T(8,128)(2,1)S(1)}, bf16[3,6,6,1024]{3,2,1,0:T(8,128)(2,1)}, u32[]{:S(2)}) copy-start(bf16[3,6,6,1024]{3,2,1,0:T(8,128)(2,1)} %blocks_ref.3) | copy-start | bytes 663556
  33.2 29.1 %copy-start.12 = (s32[3,1024]{1,0:T(4,128)S(1)}, s32[3,1024]{1,0:T(4,128)}, u32[]{:S(2)}) copy-start(s32[3,1024]{1,0:T(4,128)} %pattern_ref.12) | copy-start | bytes 36868
  34.7 29.1 %copy-start.2 = (bf16[3,6,24,1024]{3,2,1,0:T(8,128)(2,1)S(1)}, bf16[3,6,24,1024]{3,2,1,0:T(8,128)(2,1)}, u32[]{:S(2)}) copy-start(bf16[3,6,24,1024]{3,2,1,0:T(8,128)(2,1)} %section_ref.7) | copy-start | bytes 2654212
  34.7 9.6 %collective-permute-start.1 = (f32[64,128]{1,0:T(8,128)S(1)}, f32[64,128]{1,0:T(8,128)S(1)}, u32[]{:S(2)}, u32[]{:S(2)}) collective-permute-start(f32[64,128]{1,0:T(8,128)S(1)} %shard_map.92), channel_id=1, source_target_pairs={{1,2},{3,4},{5,6},{7,8},{9,10},{11,12},{13,14},{15,16},{17,18},{19... | collective-permute-start | bytes 98312 | tf_op jit(solution)/shard_map/ppermute | solution.py:484
  44.3 61.0 %copy-start.7 = (f32[24,1536]{1,0:T(8,128)S(1)}, f32[24,1536]{1,0:T(8,128)}, u32[]{:S(2)}) copy-start(f32[24,1536]{1,0:T(8,128)} %top_inverse_ref.3) | copy-start | bytes 442372
  45.9 68.1 %copy-start.1 = (bf16[3,64,64,128]{3,2,1,0:T(8,128)(2,1)S(1)}, bf16[3,64,64,128]{3,2,1,0:T(8,128)(2,1)}, u32[]{:S(2)}) copy-start(bf16[3,64,64,128]{3,2,1,0:T(8,128)(2,1)} %matrix_ref.15) | copy-start | bytes 9437188
  54.4 8.7 %collective-permute-start.2 = (f32[4,8,128]{2,1,0:T(8,128)S(1)}, f32[4,8,128]{2,1,0:T(8,128)S(1)}, u32[]{:S(2)}, u32[]{:S(2)}) collective-permute-start(f32[4,8,128]{2,1,0:T(8,128)S(1)} %get-tuple-element.38), channel_id=1, source_target_pairs={{0,8},{8,16},{16,24},{24,32},{32,40},{40,48},{48,56},{56,64},{64,7... | collective-permute-start | bytes 49160 | tf_op jit(solution)/shard_map/ppermute | solution.py:489
  56.3 7.5 %collective-permute-start.3 = (f32[4,8,128]{2,1,0:T(8,128)S(1)}, f32[4,8,128]{2,1,0:T(8,128)S(1)}, u32[]{:S(2)}, u32[]{:S(2)}) collective-permute-start(f32[4,8,128]{2,1,0:T(8,128)S(1)} %get-tuple-element.39), channel_id=1, source_target_pairs={{8,0},{16,8},{24,16},{32,24},{40,32},{48,40},{56,48},{64,56},{72,6... | collective-permute-start | bytes 49160 | tf_op jit(solution)/shard_map/ppermute | solution.py:489
  106.3 7.7 %collective-permute-start.6 = (f32[3,8,128]{2,1,0:T(8,128)S(1)}, f32[3,8,128]{2,1,0:T(8,128)S(1)}, u32[]{:S(2)}, u32[]{:S(2)}) collective-permute-start(f32[3,8,128]{2,1,0:T(8,128)S(1)} %get-tuple-element.48), channel_id=1, source_target_pairs={{0,8},{1,9},{2,10},{8,16},{9,17},{10,18},{16,24},{17,25},{18,26},{... | collective-permute-start | bytes 36872 | tf_op jit(solution)/shard_map/ppermute | solution.py:535
  118.2 9.5 %collective-permute-start.9 = (f32[64,128]{1,0:T(8,128)S(1)}, f32[64,128]{1,0:T(8,128)S(1)}, u32[]{:S(2)}, u32[]{:S(2)}) collective-permute-start(f32[64,128]{1,0:T(8,128)S(1)} %get-tuple-element.51), channel_id=1, source_target_pairs={{1,2},{3,4},{5,6},{7,8},{9,10},{11,12},{13,14},{15,16},{17,18},{19... | collective-permute-start | bytes 98312 | tf_op jit(solution)/shard_map/ppermute | solution.py:484
  129.1 9.5 %collective-permute-start.10 = (f32[64,128]{1,0:T(8,128)S(1)}, f32[64,128]{1,0:T(8,128)S(1)}, u32[]{:S(2)}, u32[]{:S(2)}) collective-permute-start(f32[64,128]{1,0:T(8,128)S(1)} %shard_map.100), channel_id=1, source_target_pairs={{1,2},{3,4},{5,6},{7,8},{9,10},{11,12},{13,14},{15,16},{17,18},{19... | collective-permute-start | bytes 98312 | tf_op jit(solution)/shard_map/ppermute | solution.py:484
  140.0 9.5 %collective-permute-start.11 = (f32[64,128]{1,0:T(8,128)S(1)}, f32[64,128]{1,0:T(8,128)S(1)}, u32[]{:S(2)}, u32[]{:S(2)}) collective-permute-start(f32[64,128]{1,0:T(8,128)S(1)} %get-tuple-element.53), channel_id=1, source_target_pairs={{1,2},{3,4},{5,6},{7,8},{9,10},{11,12},{13,14},{15,16},{17,18},{19... | collective-permute-start | bytes 98312 | tf_op jit(solution)/shard_map/ppermute | solution.py:484
  150.8 9.5 %collective-permute-start.12 = (f32[64,128]{1,0:T(8,128)S(1)}, f32[64,128]{1,0:T(8,128)S(1)}, u32[]{:S(2)}, u32[]{:S(2)}) collective-permute-start(f32[64,128]{1,0:T(8,128)S(1)} %shard_map.102), channel_id=1, source_target_pairs={{1,2},{3,4},{5,6},{7,8},{9,10},{11,12},{13,14},{15,16},{17,18},{19... | collective-permute-start | bytes 98312 | tf_op jit(solution)/shard_map/ppermute | solution.py:484
  170.2 8.0 %collective-permute-start.13 = (f32[4,8,128]{2,1,0:T(8,128)S(1)}, f32[4,8,128]{2,1,0:T(8,128)S(1)}, u32[]{:S(2)}, u32[]{:S(2)}) collective-permute-start(f32[4,8,128]{2,1,0:T(8,128)S(1)} %get-tuple-element.56), channel_id=1, source_target_pairs={{0,8},{8,16},{16,24},{24,32},{32,40},{40,48},{48,56},{56,64},{64,7... | collective-permute-start | bytes 49160 | tf_op jit(solution)/shard_map/ppermute | solution.py:489
  172.1 7.5 %collective-permute-start.14 = (f32[4,8,128]{2,1,0:T(8,128)S(1)}, f32[4,8,128]{2,1,0:T(8,128)S(1)}, u32[]{:S(2)}, u32[]{:S(2)}) collective-permute-start(f32[4,8,128]{2,1,0:T(8,128)S(1)} %get-tuple-element.57), channel_id=1, source_target_pairs={{8,0},{16,8},{24,16},{32,24},{40,32},{48,40},{56,48},{64,56},{72,6... | collective-permute-start | bytes 49160 | tf_op jit(solution)/shard_map/ppermute | solution.py:489
  213.5 7.7 %collective-permute-start.15 = (f32[3,8,128]{2,1,0:T(8,128)S(1)}, f32[3,8,128]{2,1,0:T(8,128)S(1)}, u32[]{:S(2)}, u32[]{:S(2)}) collective-permute-start(f32[3,8,128]{2,1,0:T(8,128)S(1)} %get-tuple-element.61), channel_id=1, source_target_pairs={{0,8},{1,9},{2,10},{8,16},{9,17},{10,18},{16,24},{17,25},{18,26},{... | collective-permute-start | bytes 36872 | tf_op jit(solution)/shard_map/ppermute | solution.py:535
  225.4 9.5 %collective-permute-start.16 = (f32[64,128]{1,0:T(8,128)S(1)}, f32[64,128]{1,0:T(8,128)S(1)}, u32[]{:S(2)}, u32[]{:S(2)}) collective-permute-start(f32[64,128]{1,0:T(8,128)S(1)} %get-tuple-element.63), channel_id=1, source_target_pairs={{1,2},{3,4},{5,6},{7,8},{9,10},{11,12},{13,14},{15,16},{17,18},{19... | collective-permute-start | bytes 98312 | tf_op jit(solution)/shard_map/ppermute | solution.py:484
  (8 other events, 27.5 us)

commit v3 on v2

--- a/solution.py
+++ b/solution.py
@@ -78,10 +78,33 @@
     ext[2 * parity] = odd_ref[...]
 
 
-def fine_product(where_ref, matrix_ref, pattern_ref, ext, picked, out):
+def product_rows(matrix_ref, ks, picked, out, before=None):
+    rows = out.shape[0]
+
+    def group(g, carry):
+        part = pl.ds(pl.multiple_of(g * SUB, SUB), SUB)
+        terms = []
+        for p in range(SUB):
+            total = None
+            for k in ks:
+                block = matrix_ref[k, g * SUB + p].astype(F32)
+                product = jnp.sum((block * picked[k][...]).reshape(rows // SUB, SUB, LANES), axis=0)
+                total = product if total is None else total + product
+            terms.append(total)
+        value = fold_rows(terms)
+        out[part, :] = value if before is None else value + before[part, :]
+        return carry
+
+    lax.fori_loop(0, rows // SUB, group, 0)
+
+
+def own_body(matrix_ref, field_ref, out_ref):
+    product_rows(matrix_ref, (0,), [field_ref], out_ref)
+
+
+def fine_product(where_ref, matrix_ref, pattern_ref, ext, picked, out, before=None):
     rows = out.shape[0]
     base = where_ref[1]
-    picked[0] = ext[1]
     for k in (1, 2):
         target = pattern_ref[k : k + 1, :] - base
         lane = jnp.broadcast_to(target & (LANES - 1), (SUB, LANES))
@@ -89,21 +112,12 @@
         for t in range(rows // SUB):
             part = pl.ds(t * SUB, SUB)
             a, b, c = (take(ext[i, part, :], lane) for i in range(3))
-            picked[k, part, :] = jnp.where(block == 0, a, jnp.where(block == 1, b, c))
-
-    def group(g, carry):
-        terms = []
-        for p in range(SUB):
-            total = None
-            for k in range(3):
-                block = matrix_ref[k, g * SUB + p].astype(F32)
-                product = jnp.sum((block * picked[k]).reshape(rows // SUB, SUB, LANES), axis=0)
-                total = product if total is None else total + product
-            terms.append(total)
-        out[pl.ds(pl.multiple_of(g * SUB, SUB), SUB), :] = fold_rows(terms)
-        return carry
-
-    lax.fori_loop(0, rows // SUB, group, 0)
+            picked[k - 1, part, :] = jnp.where(block == 0, a, jnp.where(block == 1, b, c))
+
+    near = {1: picked.at[0], 2: picked.at[1]}
+    if before is None:
+        near[0] = ext.at[1]
+    product_rows(matrix_ref, sorted(near), near, out, before)
 
 
 def first_body(matrix_ref, source_ref, inverse_ref, field_ref):
@@ -120,24 +134,24 @@
         field_ref[part, :] = inverse * source_ref[part, :]
 
 
-def field_body(where_ref, pair_ref, odd_ref, matrix_ref, pattern_ref, source_ref, inverse_ref, change_ref, field_ref, ext, picked, out):
+def field_body(where_ref, pair_ref, odd_ref, own_ref, matrix_ref, pattern_ref, source_ref, inverse_ref, change_ref, field_ref, ext, picked, out):
     load_halo(where_ref, pair_ref, odd_ref, ext)
-    fine_product(where_ref, matrix_ref, pattern_ref, ext, picked, out)
+    fine_product(where_ref, matrix_ref, pattern_ref, ext, picked, out, own_ref)
     change = inverse_ref[...] * (source_ref[...] - out[...])
     change_ref[...] = change
     field_ref[...] = ext[1] + change
 
 
-def solution_body(where_ref, pair_ref, odd_ref, matrix_ref, pattern_ref, source_ref, inverse_ref, change_ref, field_ref, ext, picked, out):
+def solution_body(where_ref, pair_ref, odd_ref, own_ref, matrix_ref, pattern_ref, source_ref, inverse_ref, change_ref, field_ref, ext, picked, out):
     load_halo(where_ref, pair_ref, odd_ref, ext)
-    fine_product(where_ref, matrix_ref, pattern_ref, ext, picked, out)
+    fine_product(where_ref, matrix_ref, pattern_ref, ext, picked, out, own_ref)
     second = KEEP * change_ref[...] + FRESH * inverse_ref[...] * (source_ref[...] - out[...])
     field_ref[...] = ext[1] + second
 
 
-def restrict_body(where_ref, pair_ref, odd_ref, matrix_ref, pattern_ref, source_ref, prolong_ref, targets_ref, sums_ref, ext, picked, out):
+def restrict_body(where_ref, pair_ref, odd_ref, own_ref, matrix_ref, pattern_ref, source_ref, prolong_ref, targets_ref, sums_ref, ext, picked, out):
     load_halo(where_ref, pair_ref, odd_ref, ext)
-    fine_product(where_ref, matrix_ref, pattern_ref, ext, picked, out)
+    fine_product(where_ref, matrix_ref, pattern_ref, ext, picked, out, own_ref)
     residual = source_ref[...] - out[...]
     modes = prolong_ref.shape[1]
     rows = residual.shape[0]
@@ -235,7 +249,18 @@
     return fold_rows(terms)
 
 
-def gather_body(parts_ref, low_ref, all_ref, high_ref):
+def by_two(first, number, body):
+    def trip(i, carry):
+        body(first + 2 * i)
+        body(first + 2 * i + 1)
+        return carry
+
+    lax.fori_loop(0, number // 2, trip, 0)
+    if number % 2:
+        body(first + number - 1)
+
+
+def gather_body(parts_ref, ends_ref, all_ref):
     count = parts_ref.shape[0]
     blocks = []
     for b in range(-1, count + 1):
@@ -249,25 +274,27 @@
     for i, block in enumerate(blocks):
         all_ref[i] = block
     for i in range(SPILL):
-        low_ref[i] = blocks[i]
-        high_ref[i] = blocks[count + 2 - SPILL + i]
-
-
-def coarse_down_body(where_ref, all_ref, below_ref, above_ref, matrix_ref, offset_ref, inverse_ref, section_ref, rhs_ref, sol_ref, top_ref, field, other):
+        ends_ref[i] = blocks[i]
+        ends_ref[SPILL + i] = blocks[count + 2 - SPILL + i]
+
+
+def coarse_down_body(where_ref, all_ref, even_ref, odd_ref, matrix_ref, offset_ref, inverse_ref, section_ref, rhs_ref, sol_ref, top_ref, field, other):
     total = matrix_ref.shape[0]
     count = total - 2 * EXT
     modes = matrix_ref.shape[2]
     width = section_ref.shape[2]
     zero = jnp.zeros((SUB, LANES), F32)
+    parity = where_ref[6]
     for b in range(total):
         terms = []
         at = b - (EXT - 1)
         if 0 <= at < count + 2:
             terms.append(all_ref[at])
         if b < SPILL:
-            terms.append(below_ref[b])
+            terms.append(jnp.where(parity == 0, odd_ref[SPILL + b], even_ref[1 - parity, SPILL + b]))
         if b >= total - SPILL:
-            terms.append(above_ref[b - (total - SPILL)])
+            i = b - (total - SPILL)
+            terms.append(jnp.where(parity == 0, even_ref[1 - parity, i], odd_ref[i]))
         value = sum(terms[1:], terms[0])
         rhs_ref[b] = value
         field[b + 1] = inverse_ref[b] * value
@@ -275,28 +302,29 @@
         field[edge] = zero
         other[edge] = zero
 
-    def first(b, carry):
+    def first(b):
         start = field[b + 1]
         second = KEEP * start + FRESH * inverse_ref[b] * (rhs_ref[b] - coarse_product(matrix_ref, offset_ref, field, b))
         other[b + 1] = start + second
         sol_ref[b] = start + second
-        return carry
-
-    lax.fori_loop(0, total, first, 0)
+
+    by_two(EXT - 1, count + 2, first)
 
     def down(i, carry):
-        b = i + EXT
-        residual = rhs_ref[b] - coarse_product(matrix_ref, offset_ref, other, b)
-        cols = pl.ds(pl.multiple_of(i * LANES, LANES), LANES)
-        out = []
-        for k in range(3):
-            value = carry[k]
-            for p in range(modes):
-                value = value + section_ref[k, p, :, cols].astype(F32) * residual[p : p + 1, :]
-            out.append(value)
-        return tuple(out)
-
-    sums = lax.fori_loop(0, count, down, tuple(jnp.zeros((width, LANES), F32) for _ in range(3)))
+        for j in range(2):
+            b = 2 * i + j + EXT
+            residual = rhs_ref[b] - coarse_product(matrix_ref, offset_ref, other, b)
+            cols = pl.ds(pl.multiple_of((2 * i + j) * LANES, LANES), LANES)
+            out = []
+            for k in range(3):
+                value = carry[k]
+                for p in range(modes):
+                    value = value + section_ref[k, p, :, cols].astype(F32) * residual[p : p + 1, :]
+                out.append(value)
+            carry = out
+        return tuple(carry)
+
+    sums = lax.fori_loop(0, count // 2, down, tuple(jnp.zeros((width, LANES), F32) for _ in range(3)))
     stacked = jnp.concatenate(list(sums) + [jnp.zeros((LANES - 3 * width, LANES), F32)], axis=0)
     ones = jnp.ones((16, LANES), BF16)
     row = sum(lanes_dot(ones, part) for part in split3(stacked))
@@ -338,7 +366,7 @@
         column[side * width : (side + 1) * width, :] = jnp.broadcast_to(answers[side], (width, LANES))
     zero = jnp.zeros((SUB, LANES), F32)
 
-    def correct(b, carry):
+    def correct(b):
         cols = pl.ds(pl.multiple_of(b * LANES, LANES), LANES)
         terms = []
         for p in range(SUB):
@@ -348,9 +376,8 @@
             else:
                 terms.append(zero)
         field_ref[b] = sol_ref[b + EXT] + fold_rows(terms)
-        return carry
-
-    lax.fori_loop(0, count, correct, 0)
+
+    by_two(0, count, correct)
     start = jnp.where(where_ref[5] > 0, count - EXT, 0)
     for i in range(EXT):
         edge_ref[i] = field_ref[start + i]
@@ -397,20 +424,19 @@
         field[edge] = zero
         other[edge] = zero
 
-    def smooth_first(b, carry):
+    def smooth_first(b):
         change = inverse_ref[b] * (rhs_ref[b] - coarse_product(matrix_ref, offset_ref, field, b))
         final[b] = change
         other[b + 1] = field[b + 1] + change
-        return carry
-
-    lax.fori_loop(0, total, smooth_first, 0)
-
-    def smooth_second(b, carry):
+
+    middle = where_ref[3] + EXT
+    by_two(middle - 3, 7, smooth_first)
+
+    def smooth_second(b):
         second = KEEP * final[b] + FRESH * inverse_ref[b] * (rhs_ref[b] - coarse_product(matrix_ref, offset_ref, other, b))
         final[b] = other[b + 1] + second
-        return carry
-
-    lax.fori_loop(EXT - 2, EXT + count + 2, smooth_second, 0)
+
+    by_two(middle - 2, 5, smooth_second)
     load_halo(where_ref, pair_ref, odd_ref, ext)
     rows = ext.shape[1]
     parity = where_ref[0]
@@ -470,7 +496,7 @@
     device = section * secs + place
     roll = ((section + LANES - 1) * width) % LANES
     from_left = (place < secs // 2).astype(jnp.int32)
-    where = jnp.stack([place % 2, device * own, section * section_rows, place, roll, from_left]).astype(jnp.int32)
+    where = jnp.stack([place % 2, device * own, section * section_rows, place, roll, from_left, section % 2]).astype(jnp.int32)
 
     prolong = jnp.transpose(fine_prolong, (0, 2, 1, 3))
     odd_swap = [(i, i + 1) for i in range(1, devices - 1, 2)] + [(i + 1, i) for i in range(1, devices - 1, 2)]
@@ -480,22 +506,28 @@
     edge_moves = [(s * secs + c, (s + 1) * secs + c) for s in range(slabs - 1) for c in reach]
     edge_moves += [((s + 1) * secs + secs - 1 - c, s * secs + secs - 1 - c) for s in range(slabs - 1) for c in reach]
 
+    slab_odd = [(i, i + 1) for i in range(1, slabs - 1, 2)] + [(i + 1, i) for i in range(1, slabs - 1, 2)]
+    slab_pairs = [[2 * i, 2 * i + 1] for i in range(slabs // 2)]
+
     def nearby(field):
         odd = lax.ppermute(field, both, odd_swap)
         pair = lax.all_gather(field, "sec", axis_index_groups=pairs, axis=0)
-        return pair, odd
+        return pair, odd, call(own_body, [fine], [VMEM] * 2)(fine_blocks, field)[0]
 
     def beside(value, step):
         return lax.ppermute(value, "slab", [(i, i + step) for i in range(max(0, -step), min(slabs, slabs - step))])
 
     fine = struct(rows, own)
-    work = [pltpu.VMEM((3, rows, own), F32), pltpu.VMEM((3, rows, own), F32), pltpu.VMEM((rows, own), F32)]
+    work = [pltpu.VMEM((3, rows, own), F32), pltpu.VMEM((2, rows, own), F32), pltpu.VMEM((rows, own), F32)]
     inverse, start = call(first_body, [fine, fine], [VMEM] * 2)(fine_blocks, source)
 
+    first_near = nearby(start)
+    held = lax.optimization_barrier((first_near[0], coarse_blocks, coarse_pattern, coarsest_inverse, prolong, prolong_pattern))
     side = struct(3 * modes * SUB + SUB + width * (coarsest_inverse.shape[1] // halo), halo)
     low, high, fine_pack = call(pack_body, [side, side, struct(3 * modes * rows + SUB, own)], [SMEM] + [VMEM] * 5)(
-        where, coarse_blocks, coarse_pattern, coarsest_inverse, prolong, prolong_pattern
+        where, *held[1:]
     )
+    first_near = (held[0], *first_near[1:])
     left_data, right_data = beside(high, 1), beside(low, -1)
     odd_prolong = lax.ppermute(fine_pack, both, odd_swap)
     even_prolong = lax.ppermute(fine_pack, both, even_swap)
@@ -506,25 +538,26 @@
     )(where, left_data, right_data, coarse_blocks, coarse_pattern)
 
     def step(body, outs, near, *rest):
-        return call(body, outs, [SMEM] + [VMEM] * (4 + len(rest)), work)(where, *near, fine_blocks, fine_pattern, *rest)
+        return call(body, outs, [SMEM] + [VMEM] * (5 + len(rest)), work)(where, *near, fine_blocks, fine_pattern, *rest)
 
     coarse = struct(blocks, SUB, LANES)
-    ends = struct(SPILL, SUB, LANES)
     line = pltpu.VMEM((blocks + 2, SUB, LANES), F32)
     for cycle in range(CYCLES):
         if cycle == 0:
-            change = field = start
+            change, near = start, first_near
         else:
             change, field = step(field_body, [fine, fine], nearby(solution), source, inverse)
-        solution = step(solution_body, [fine], nearby(field), source, inverse, change)[0]
+            near = nearby(field)
+        solution = step(solution_body, [fine], near, source, inverse, change)[0]
         near = nearby(solution)
         sums = step(restrict_body, [struct(secs, SUB, 3 * LANES)], near, source, prolong, prolong_pattern)[0]
         parts = lax.all_to_all(sums, "sec", 0, 0, tiled=True)
-        low, everything, high = call(gather_body, [ends, struct(secs + 2, SUB, LANES), ends], [VMEM])(parts)
-        below, above = beside(high, 1), beside(low, -1)
+        ends, everything = call(gather_body, [struct(2 * SPILL, SUB, LANES), struct(secs + 2, SUB, LANES)], [VMEM])(parts)
+        odd = lax.ppermute(ends, "slab", slab_odd)
+        even = lax.all_gather(ends, "slab", axis_index_groups=slab_pairs, axis=0)
         rhs, coarse_sol, top = call(
             coarse_down_body, [coarse, coarse, struct(slabs, LANES)], [SMEM] + [VMEM] * 7, [line, line]
-        )(where, everything, below, above, matrix, offset, coarse_inverse, section_prolong)
+        )(where, everything, even, odd, matrix, offset, coarse_inverse, section_prolong)
         tops = lax.all_to_all(top, "slab", 0, 0, tiled=True)
         middle, edge = call(
             top_body,
@@ -534,7 +567,7 @@
         )(where, tops, left_data, coarsest_inverse, right_data, coarse_sol, section_prolong)
         edge = lax.ppermute(edge, both, edge_moves)
         change, field = call(up_body, [fine, fine], [SMEM] + [VMEM] * 16, [line, line, line] + work)(
-            where, middle, edge, rhs, matrix, offset, coarse_inverse, *near, prolong, even_prolong, odd_prolong, prolong_pattern, fine_blocks, fine_pattern, source, inverse
+            where, middle, edge, rhs, matrix, offset, coarse_inverse, *near[:2], prolong, even_prolong, odd_prolong, prolong_pattern, fine_blocks, fine_pattern, source, inverse
         )
         solution = step(solution_body, [fine], nearby(field), source, inverse, change)[0]
     return solution

time: 238 us -> 224 us (0.941)
  Pallas kernels: 29.1 us -> 23.9 us
  waiting for transfers between devices: 48.1 us -> 43.4 us
  starting transfers between devices: 53.9 us -> 50.4 us
    ppermute x6 -> x2, starting transfers between devices: 23.9 us -> 7.95 us  [beside(): lax.ppermute(value, 'slab', [(i, i + step) for i in range(max(0, -step),...]
    all_gather x0 -> x2, blocking collectives: none -> 9.18 us  [shards(): even = lax.all_gather(ends, 'slab', axis_index_groups=slab_pairs, axis=0)]
    ppermute x0 -> x2, starting transfers between devices: none -> 8.31 us  [shards(): odd = lax.ppermute(ends, 'slab', slab_odd)]
    all_to_all x2, blocking collectives: 68.1 us -> 60.3 us  [shards(): tops = lax.all_to_all(top, 'slab', 0, 0, tiled=True)]
    ppermute x7, waiting for transfers between devices: 35.5 us -> 31.5 us  [nearby(): odd = lax.ppermute(field, both, odd_swap)]
    ppermute x7, starting transfers between devices: 17.2 us -> 20.9 us  [nearby(): odd = lax.ppermute(field, both, odd_swap)]
    pallas_call x2, Pallas kernels: 8.4 us -> 4.81 us  [shards(): call(up_body, [fine, fine], [SMEM] + [VMEM] * 16, [line, line, line] + work)]
    unnamed x30 -> x28, local copies, waits for them, and re-layouts: 6.91 us -> 5.53 us
  transfers between devices with their start and end apart: 17 -> 15, of which waited for: 11 -> 9; matrix products, arithmetic and copies ran while one was open for 0% -> 0% of each run, Pallas kernels for 3% -> 4%
where the time goes in v3:
time: 224 us; the launch traced here: 223 us
  blocking collectives  99.8 us (45%)
  starting transfers between devices  50.4 us (22%)
  waiting for transfers between devices  43.4 us (19%)
  Pallas kernels  23.9 us (11%)
  local copies, waits for them, and re-layouts  5.62 us (3%)
    all_to_all x2, blocking collectives, shards(): tops = lax.all_to_all(top, 'slab', 0, 0, tiled=True)  60.3 us
    ppermute x7, waiting for transfers between devices, nearby(): odd = lax.ppermute(field, both, odd_swap)  31.5 us
    ppermute x7, starting transfers between devices, nearby(): odd = lax.ppermute(field, both, odd_swap)  20.9 us
    all_to_all x2, blocking collectives, shards(): parts = lax.all_to_all(sums, 'sec', 0, 0, tiled=True)  16.5 us
    all_gather x7, blocking collectives, nearby(): pair = lax.all_gather(field, 'sec', axis_index_groups=pairs, axis=0)  13.9 us
    ppermute x2, waiting for transfers between devices, shards(): edge = lax.ppermute(edge, both, edge_moves)  10.5 us
    pallas_call x7, Pallas kernels, step(): call(body, outs, [SMEM] + [VMEM] * (5 + len(rest)), work)  9.56 us
    all_gather x2, blocking collectives, shards(): even = lax.all_gather(ends, 'slab', axis_index_groups=slab_pairs, axis=0)  9.18 us
  transfers between devices with their start and end apart: 15, of which 9 were waited for; matrix products, arithmetic and copies ran while one was open for 0% of the time, Pallas kernels for 4%

profile of v3, /device:TPU:32, one launch (start us, length us, event | category | flops | bytes accessed | tf_op | source)
XLA Modules:
  0.0 223.4 jit_solution(13300764839556015357)
XLA Ops:
  8.3 6.4 %collective-permute-start.7 = (f32[1160,128]{1,0:T(8,128)S(1)}, f32[1160,128]{1,0:T(8,128)S(1)}, u32[]{:S(2)}, u32[]{:S(2)}) collective-permute-start(f32[1160,128]{1,0:T(8,128)S(1)} %get-tuple-element.59), channel_id=1, source_target_pairs={{1,2},{3,4},{5,6},{7,8},{9,10},{11,12},{13,14},{15,16},{17,18},{19... | collective-permute-start | bytes 1781768 | tf_op jit(solution)/shard_map/ppermute | solution.py:532
  18.6 6.0 %collective-permute-start.4 = (f32[248,384]{1,0:T(8,128)S(1)}, f32[248,384]{1,0:T(8,128)S(1)}, u32[]{:S(2)}, u32[]{:S(2)}) collective-permute-start(f32[248,384]{1,0:T(8,128)S(1)} %get-tuple-element.50), channel_id=1, source_target_pairs={{8,0},{16,8},{24,16},{32,24},{40,32},{48,40},{56,48},{64,56},{72,6... | collective-permute-start | bytes 1142792 | tf_op jit(solution)/shard_map/ppermute | solution.py:518
  26.9 7.2 %collective-permute-done.odd_ref = f32[64,128]{1,0:T(8,128)S(1)} collective-permute-done((f32[64,128]{1,0:T(8,128)S(1)}, f32[64,128]{1,0:T(8,128)S(1)}, u32[]{:S(2)}, u32[]{:S(2)}) %collective-permute-start) | collective-permute-done | bytes 32800 | tf_op jit(solution)/shard_map/ppermute | solution.py:513
  35.3 7.5 %collective-permute-start.1 = (f32[64,128]{1,0:T(8,128)S(1)}, f32[64,128]{1,0:T(8,128)S(1)}, u32[]{:S(2)}, u32[]{:S(2)}) collective-permute-start(f32[64,128]{1,0:T(8,128)S(1)} %shard_map.93.field_ref), channel_id=1, source_target_pairs={{1,2},{3,4},{5,6},{7,8},{9,10},{11,12},{13,14},{15,16},{17,18},{19... | collective-permute-start | bytes 98312 | tf_op jit(solution)/shard_map/ppermute | solution.py:513
  46.6 8.3 %all_to_all.32.parts_ref = f32[8,8,384]{2,1,0:T(8,128)S(1)} all-to-all(f32[8,8,384]{2,1,0:T(8,128)S(1)} %shard_map.95), channel_id=1, replica_groups=mesh['slab'=64,'sec'=8] {'sec'}, dimensions={0} | all-to-all | bytes 196608 | tf_op jit(solution)/shard_map/all_to_all | solution.py:554
  54.9 6.4 %collective-permute-start.2 = (f32[8,8,128]{2,1,0:T(8,128)S(1)}, f32[8,8,128]{2,1,0:T(8,128)S(1)}, u32[]{:S(2)}, u32[]{:S(2)}) collective-permute-start(f32[8,8,128]{2,1,0:T(8,128)S(1)} %get-tuple-element.43), channel_id=1, source_target_pairs={{8,16},{24,32},{40,48},{56,64},{72,80},{88,96},{104,112},{120,128}... | collective-permute-start | bytes 98312 | tf_op jit(solution)/shard_map/ppermute | solution.py:556
  61.3 4.6 %all-gather.2 = f32[16,8,128]{2,1,0:T(8,128)S(1)} all-gather(f32[8,8,128]{2,1,0:T(8,128)S(1)} %get-tuple-element.43), channel_id=4, replica_groups={{0,8},{16,24},{32,40},{48,56},{64,72},{80,88},{96,104},{112,120},{128,1..., dimensions={0}, use_global_device_ids=true | all-gather | bytes 98304 | tf_op jit(solution)/shard_map/all_gather | solution.py:557
  68.7 33.4 %all_to_all.33 = f32[64,1,128]{2,1,0:T(1,128)S(1)} all-to-all(f32[64,1,128]{2,1,0:T(1,128)S(1)} %bitcast.43), channel_id=1, replica_groups=mesh['slab'=64,'sec'=8] {'slab'}, dimensions={0} | all-to-all | bytes 65536 | tf_op jit(solution)/shard_map/all_to_all | solution.py:561
  103.0 2.5 %collective-permute-start.5 = (f32[3,8,128]{2,1,0:T(8,128)S(1)}, f32[3,8,128]{2,1,0:T(8,128)S(1)}, u32[]{:S(2)}, u32[]{:S(2)}) collective-permute-start(f32[3,8,128]{2,1,0:T(8,128)S(1)} %get-tuple-element.57), channel_id=1, source_target_pairs={{0,8},{1,9},{2,10},{8,16},{9,17},{10,18},{16,24},{17,25},{18,26},{... | collective-permute-start | bytes 36872 | tf_op jit(solution)/shard_map/ppermute | solution.py:568
  105.5 5.2 %collective-permute-done.5.edge_ref = f32[3,8,128]{2,1,0:T(8,128)S(1)} collective-permute-done((f32[3,8,128]{2,1,0:T(8,128)S(1)}, f32[3,8,128]{2,1,0:T(8,128)S(1)}, u32[]{:S(2)}, u32[]{:S(2)}) %collective-permute-start.5) | collective-permute-done | bytes 12320 | tf_op jit(solution)/shard_map/ppermute | solution.py:568
  110.7 2.4 %shard_map.101 = (f32[64,128]{1,0:T(8,128)S(1)}, f32[64,128]{1,0:T(8,128)S(1)}) custom-call(s32[7]{0:T(128)S(1)} %stack.35.where_ref, f32[8,8,128]{2,1,0:T(8,128)S(1)} %get-tuple-element.56.middle_ref, f32[3,8,128]{2,1,0:T(8,128)S(1)} %collective-permute-done.5.edge_ref, f32[14,8,128]{2,1,0:T(8,128)S(1)} %get-tuple-element.58.rhs_ref, ...), custom_call_target="tpu_custom_call" | custom-call | flops 1048576 | bytes 1048576 | tf_op jit(solution)/shard_map/pallas_call | solution.py:569
  117.6 5.0 %collective-permute-done.8.odd_ref = f32[64,128]{1,0:T(8,128)S(1)} collective-permute-done((f32[64,128]{1,0:T(8,128)S(1)}, f32[64,128]{1,0:T(8,128)S(1)}, u32[]{:S(2)}, u32[]{:S(2)}) %collective-permute-start.8) | collective-permute-done | bytes 32800 | tf_op jit(solution)/shard_map/ppermute | solution.py:513
  123.8 2.5 %collective-permute-start.9 = (f32[64,128]{1,0:T(8,128)S(1)}, f32[64,128]{1,0:T(8,128)S(1)}, u32[]{:S(2)}, u32[]{:S(2)}) collective-permute-start(f32[64,128]{1,0:T(8,128)S(1)} %shard_map.103.field_ref), channel_id=1, source_target_pairs={{1,2},{3,4},{5,6},{7,8},{9,10},{11,12},{13,14},{15,16},{17,18},{19... | collective-permute-start | bytes 98312 | tf_op jit(solution)/shard_map/ppermute | solution.py:513
  128.5 4.8 %collective-permute-done.9.odd_ref = f32[64,128]{1,0:T(8,128)S(1)} collective-permute-done((f32[64,128]{1,0:T(8,128)S(1)}, f32[64,128]{1,0:T(8,128)S(1)}, u32[]{:S(2)}, u32[]{:S(2)}) %collective-permute-start.9) | collective-permute-done | bytes 32800 | tf_op jit(solution)/shard_map/ppermute | solution.py:513
  134.5 2.5 %collective-permute-start.10 = (f32[64,128]{1,0:T(8,128)S(1)}, f32[64,128]{1,0:T(8,128)S(1)}, u32[]{:S(2)}, u32[]{:S(2)}) collective-permute-start(f32[64,128]{1,0:T(8,128)S(1)} %get-tuple-element.62.field_ref), channel_id=1, source_target_pairs={{1,2},{3,4},{5,6},{7,8},{9,10},{11,12},{13,14},{15,16},{17,18},{19... | collective-permute-start | bytes 98312 | tf_op jit(solution)/shard_map/ppermute | solution.py:513
  139.2 4.8 %collective-permute-done.10.odd_ref = f32[64,128]{1,0:T(8,128)S(1)} collective-permute-done((f32[64,128]{1,0:T(8,128)S(1)}, f32[64,128]{1,0:T(8,128)S(1)}, u32[]{:S(2)}, u32[]{:S(2)}) %collective-permute-start.10) | collective-permute-done | bytes 32800 | tf_op jit(solution)/shard_map/ppermute | solution.py:513
  145.2 2.5 %collective-permute-start.11 = (f32[64,128]{1,0:T(8,128)S(1)}, f32[64,128]{1,0:T(8,128)S(1)}, u32[]{:S(2)}, u32[]{:S(2)}) collective-permute-start(f32[64,128]{1,0:T(8,128)S(1)} %shard_map.107.field_ref), channel_id=1, source_target_pairs={{1,2},{3,4},{5,6},{7,8},{9,10},{11,12},{13,14},{15,16},{17,18},{19... | collective-permute-start | bytes 98312 | tf_op jit(solution)/shard_map/ppermute | solution.py:513
  149.9 4.8 %collective-permute-done.11.odd_ref = f32[64,128]{1,0:T(8,128)S(1)} collective-permute-done((f32[64,128]{1,0:T(8,128)S(1)}, f32[64,128]{1,0:T(8,128)S(1)}, u32[]{:S(2)}, u32[]{:S(2)}) %collective-permute-start.11) | collective-permute-done | bytes 32800 | tf_op jit(solution)/shard_map/ppermute | solution.py:513
  156.1 8.2 %all_to_all.34.parts_ref = f32[8,8,384]{2,1,0:T(8,128)S(1)} all-to-all(f32[8,8,384]{2,1,0:T(8,128)S(1)} %shard_map.109), channel_id=1, replica_groups=mesh['slab'=64,'sec'=8] {'sec'}, dimensions={0} | all-to-all | bytes 196608 | tf_op jit(solution)/shard_map/all_to_all | solution.py:554
  166.2 4.6 %all-gather.7 = f32[16,8,128]{2,1,0:T(8,128)S(1)} all-gather(f32[8,8,128]{2,1,0:T(8,128)S(1)} %get-tuple-element.65), channel_id=9, replica_groups={{0,8},{16,24},{32,40},{48,56},{64,72},{80,88},{96,104},{112,120},{128,1..., dimensions={0}, use_global_device_ids=true | all-gather | bytes 98304 | tf_op jit(solution)/shard_map/all_gather | solution.py:557
  174.2 26.9 %all_to_all.35 = f32[64,1,128]{2,1,0:T(1,128)S(1)} all-to-all(f32[64,1,128]{2,1,0:T(1,128)S(1)} %bitcast.44), channel_id=1, replica_groups=mesh['slab'=64,'sec'=8] {'slab'}, dimensions={0} | all-to-all | bytes 65536 | tf_op jit(solution)/shard_map/all_to_all | solution.py:561
  202.0 2.4 %collective-permute-start.13 = (f32[3,8,128]{2,1,0:T(8,128)S(1)}, f32[3,8,128]{2,1,0:T(8,128)S(1)}, u32[]{:S(2)}, u32[]{:S(2)}) collective-permute-start(f32[3,8,128]{2,1,0:T(8,128)S(1)} %get-tuple-element.69), channel_id=1, source_target_pairs={{0,8},{1,9},{2,10},{8,16},{9,17},{10,18},{16,24},{17,25},{18,26},{... | collective-permute-start | bytes 36872 | tf_op jit(solution)/shard_map/ppermute | solution.py:568
  204.5 5.3 %collective-permute-done.13.edge_ref = f32[3,8,128]{2,1,0:T(8,128)S(1)} collective-permute-done((f32[3,8,128]{2,1,0:T(8,128)S(1)}, f32[3,8,128]{2,1,0:T(8,128)S(1)}, u32[]{:S(2)}, u32[]{:S(2)}) %collective-permute-start.13) | collective-permute-done | bytes 12320 | tf_op jit(solution)/shard_map/ppermute | solution.py:568
  216.6 5.0 %collective-permute-done.14.odd_ref = f32[64,128]{1,0:T(8,128)S(1)} collective-permute-done((f32[64,128]{1,0:T(8,128)S(1)}, f32[64,128]{1,0:T(8,128)S(1)}, u32[]{:S(2)}, u32[]{:S(2)}) %collective-permute-start.14) | collective-permute-done | bytes 32800 | tf_op jit(solution)/shard_map/ppermute | solution.py:513
  (73 shorter events, 53.9 us)
Async XLA Ops:
  0.0 4.8 %copy-start.13 = (s32[3,128]{1,0:T(4,128)S(1)}, s32[3,128]{1,0:T(4,128)}, u32[]{:S(2)}) copy-start(s32[3,128]{1,0:T(4,128)} %targets_ref.8) | copy-start | bytes 4612
  0.0 4.8 %copy-start.12 = (s32[3,1024]{1,0:T(4,128)S(1)}, s32[3,1024]{1,0:T(4,128)}, u32[]{:S(2)}) copy-start(s32[3,1024]{1,0:T(4,128)} %pattern_ref.11) | copy-start | bytes 36868
  2.7 23.9 %copy-start.1 = (bf16[3,64,64,128]{3,2,1,0:T(8,128)(2,1)S(1)}, bf16[3,64,64,128]{3,2,1,0:T(8,128)(2,1)}, u32[]{:S(2)}) copy-start(bf16[3,64,64,128]{3,2,1,0:T(8,128)(2,1)} %matrix_ref.29) | copy-start | bytes 9437188
  2.7 31.4 %copy-start.6 = (f32[64,128]{1,0:T(8,128)S(1)}, f32[64,128]{1,0:T(8,128)}, u32[]{:S(2)}) copy-start(f32[64,128]{1,0:T(8,128)} %source_ref.19) | copy-start | bytes 98308
  2.7 31.4 %copy-start.11 = (s32[3,128]{1,0:T(4,128)S(1)}, s32[3,128]{1,0:T(4,128)}, u32[]{:S(2)}) copy-start(s32[3,128]{1,0:T(4,128)} %pattern_ref.16) | copy-start | bytes 4612
  8.3 102.5 %collective-permute-start.7 = (f32[1160,128]{1,0:T(8,128)S(1)}, f32[1160,128]{1,0:T(8,128)S(1)}, u32[]{:S(2)}, u32[]{:S(2)}) collective-permute-start(f32[1160,128]{1,0:T(8,128)S(1)} %get-tuple-element.59), channel_id=1, source_target_pairs={{1,2},{3,4},{5,6},{7,8},{9,10},{11,12},{13,14},{15,16},{17,18},{19... | collective-permute-start | bytes 1781768 | tf_op jit(solution)/shard_map/ppermute | solution.py:532
  14.7 96.0 %collective-permute-start.6 = (f32[1160,128]{1,0:T(8,128)S(1)}, f32[1160,128]{1,0:T(8,128)S(1)}, u32[]{:S(2)}, u32[]{:S(2)}) collective-permute-start(f32[1160,128]{1,0:T(8,128)S(1)} %get-tuple-element.59), channel_id=1, source_target_pairs={{0,1},{1,0},{2,3},{3,2},{4,5},{5,4},{6,7},{7,6},{8,9},{9,8},{10,11... | collective-permute-start | bytes 1781768 | tf_op jit(solution)/shard_map/ppermute | solution.py:533
  16.6 49.3 %collective-permute-start.3 = (f32[248,384]{1,0:T(8,128)S(1)}, f32[248,384]{1,0:T(8,128)S(1)}, u32[]{:S(2)}, u32[]{:S(2)}) collective-permute-start(f32[248,384]{1,0:T(8,128)S(1)} %get-tuple-element.49), channel_id=1, source_target_pairs={{0,8},{8,16},{16,24},{24,32},{32,40},{40,48},{48,56},{56,64},{64,7... | collective-permute-start | bytes 1142792 | tf_op jit(solution)/shard_map/ppermute | solution.py:518
  18.6 47.4 %collective-permute-start.4 = (f32[248,384]{1,0:T(8,128)S(1)}, f32[248,384]{1,0:T(8,128)S(1)}, u32[]{:S(2)}, u32[]{:S(2)}) collective-permute-start(f32[248,384]{1,0:T(8,128)S(1)} %get-tuple-element.50), channel_id=1, source_target_pairs={{8,0},{16,8},{24,16},{32,24},{40,32},{48,40},{56,48},{64,56},{72,6... | collective-permute-start | bytes 1142792 | tf_op jit(solution)/shard_map/ppermute | solution.py:518
  24.6 9.5 %collective-permute-start = (f32[64,128]{1,0:T(8,128)S(1)}, f32[64,128]{1,0:T(8,128)S(1)}, u32[]{:S(2)}, u32[]{:S(2)}) collective-permute-start(f32[64,128]{1,0:T(8,128)S(1)} %get-tuple-element.39.field_ref.change_ref), channel_id=1, source_target_pairs={{1,2},{3,4},{5,6},{7,8},{9,10},{11,12},{13,14},{15,16},{17,18},{19... | collective-permute-start | bytes 98312 | tf_op jit(solution)/shard_map/ppermute | solution.py:513
  35.3 30.7 %copy-start.10 = (bf16[3,6,6,1024]{3,2,1,0:T(8,128)(2,1)S(1)}, bf16[3,6,6,1024]{3,2,1,0:T(8,128)(2,1)}, u32[]{:S(2)}) copy-start(bf16[3,6,6,1024]{3,2,1,0:T(8,128)(2,1)} %blocks_ref.2) | copy-start | bytes 663556
  35.3 9.9 %collective-permute-start.1 = (f32[64,128]{1,0:T(8,128)S(1)}, f32[64,128]{1,0:T(8,128)S(1)}, u32[]{:S(2)}, u32[]{:S(2)}) collective-permute-start(f32[64,128]{1,0:T(8,128)S(1)} %shard_map.93.field_ref), channel_id=1, source_target_pairs={{1,2},{3,4},{5,6},{7,8},{9,10},{11,12},{13,14},{15,16},{17,18},{19... | collective-permute-start | bytes 98312 | tf_op jit(solution)/shard_map/ppermute | solution.py:513
  43.1 23.5 %copy-start.2 = (bf16[3,6,24,1024]{3,2,1,0:T(8,128)(2,1)S(1)}, bf16[3,6,24,1024]{3,2,1,0:T(8,128)(2,1)}, u32[]{:S(2)}) copy-start(bf16[3,6,24,1024]{3,2,1,0:T(8,128)(2,1)} %section_ref.7) | copy-start | bytes 2654212
  45.1 56.9 %copy-start.8 = (f32[24,1536]{1,0:T(8,128)S(1)}, f32[24,1536]{1,0:T(8,128)}, u32[]{:S(2)}) copy-start(f32[24,1536]{1,0:T(8,128)} %top_inverse_ref.3) | copy-start | bytes 442372
  46.6 64.1 %copy-start.4 = (bf16[3,64,6,128]{3,1,2,0:T(8,128)(2,1)S(1)}, bf16[3,64,6,128]{3,1,2,0:T(8,128)(2,1)}, u32[]{:S(2)}) copy-start(bf16[3,64,6,128]{3,1,2,0:T(8,128)(2,1)} %param.12) | copy-start | bytes 884740
  54.9 11.7 %collective-permute-start.2 = (f32[8,8,128]{2,1,0:T(8,128)S(1)}, f32[8,8,128]{2,1,0:T(8,128)S(1)}, u32[]{:S(2)}, u32[]{:S(2)}) collective-permute-start(f32[8,8,128]{2,1,0:T(8,128)S(1)} %get-tuple-element.43), channel_id=1, source_target_pairs={{8,16},{24,32},{40,48},{56,64},{72,80},{88,96},{104,112},{120,128}... | collective-permute-start | bytes 98312 | tf_op jit(solution)/shard_map/ppermute | solution.py:556
  103.0 7.7 %collective-permute-start.5 = (f32[3,8,128]{2,1,0:T(8,128)S(1)}, f32[3,8,128]{2,1,0:T(8,128)S(1)}, u32[]{:S(2)}, u32[]{:S(2)}) collective-permute-start(f32[3,8,128]{2,1,0:T(8,128)S(1)} %get-tuple-element.57), channel_id=1, source_target_pairs={{0,8},{1,9},{2,10},{8,16},{9,17},{10,18},{16,24},{17,25},{18,26},{... | collective-permute-start | bytes 36872 | tf_op jit(solution)/shard_map/ppermute | solution.py:568
  113.2 9.5 %collective-permute-start.8 = (f32[64,128]{1,0:T(8,128)S(1)}, f32[64,128]{1,0:T(8,128)S(1)}, u32[]{:S(2)}, u32[]{:S(2)}) collective-permute-start(f32[64,128]{1,0:T(8,128)S(1)} %get-tuple-element.60.field_ref), channel_id=1, source_target_pairs={{1,2},{3,4},{5,6},{7,8},{9,10},{11,12},{13,14},{15,16},{17,18},{19... | collective-permute-start | bytes 98312 | tf_op jit(solution)/shard_map/ppermute | solution.py:513
  123.8 9.5 %collective-permute-start.9 = (f32[64,128]{1,0:T(8,128)S(1)}, f32[64,128]{1,0:T(8,128)S(1)}, u32[]{:S(2)}, u32[]{:S(2)}) collective-permute-start(f32[64,128]{1,0:T(8,128)S(1)} %shard_map.103.field_ref), channel_id=1, source_target_pairs={{1,2},{3,4},{5,6},{7,8},{9,10},{11,12},{13,14},{15,16},{17,18},{19... | collective-permute-start | bytes 98312 | tf_op jit(solution)/shard_map/ppermute | solution.py:513
  134.5 9.5 %collective-permute-start.10 = (f32[64,128]{1,0:T(8,128)S(1)}, f32[64,128]{1,0:T(8,128)S(1)}, u32[]{:S(2)}, u32[]{:S(2)}) collective-permute-start(f32[64,128]{1,0:T(8,128)S(1)} %get-tuple-element.62.field_ref), channel_id=1, source_target_pairs={{1,2},{3,4},{5,6},{7,8},{9,10},{11,12},{13,14},{15,16},{17,18},{19... | collective-permute-start | bytes 98312 | tf_op jit(solution)/shard_map/ppermute | solution.py:513
  145.2 9.5 %collective-permute-start.11 = (f32[64,128]{1,0:T(8,128)S(1)}, f32[64,128]{1,0:T(8,128)S(1)}, u32[]{:S(2)}, u32[]{:S(2)}) collective-permute-start(f32[64,128]{1,0:T(8,128)S(1)} %shard_map.107.field_ref), channel_id=1, source_target_pairs={{1,2},{3,4},{5,6},{7,8},{9,10},{11,12},{13,14},{15,16},{17,18},{19... | collective-permute-start | bytes 98312 | tf_op jit(solution)/shard_map/ppermute | solution.py:513
  164.3 7.9 %collective-permute-start.12 = (f32[8,8,128]{2,1,0:T(8,128)S(1)}, f32[8,8,128]{2,1,0:T(8,128)S(1)}, u32[]{:S(2)}, u32[]{:S(2)}) collective-permute-start(f32[8,8,128]{2,1,0:T(8,128)S(1)} %get-tuple-element.65), channel_id=1, source_target_pairs={{8,16},{24,32},{40,48},{56,64},{72,80},{88,96},{104,112},{120,128}... | collective-permute-start | bytes 98312 | tf_op jit(solution)/shard_map/ppermute | solution.py:556
  202.0 7.7 %collective-permute-start.13 = (f32[3,8,128]{2,1,0:T(8,128)S(1)}, f32[3,8,128]{2,1,0:T(8,128)S(1)}, u32[]{:S(2)}, u32[]{:S(2)}) collective-permute-start(f32[3,8,128]{2,1,0:T(8,128)S(1)} %get-tuple-element.69), channel_id=1, source_target_pairs={{0,8},{1,9},{2,10},{8,16},{9,17},{10,18},{16,24},{17,25},{18,26},{... | collective-permute-start | bytes 36872 | tf_op jit(solution)/shard_map/ppermute | solution.py:568
  212.1 9.5 %collective-permute-start.14 = (f32[64,128]{1,0:T(8,128)S(1)}, f32[64,128]{1,0:T(8,128)S(1)}, u32[]{:S(2)}, u32[]{:S(2)}) collective-permute-start(f32[64,128]{1,0:T(8,128)S(1)} %get-tuple-element.71.field_ref), channel_id=1, source_target_pairs={{1,2},{3,4},{5,6},{7,8},{9,10},{11,12},{13,14},{15,16},{17,18},{19... | collective-permute-start | bytes 98312 | tf_op jit(solution)/shard_map/ppermute | solution.py:513
  (5 other events, 5.5 us)

commit v4 on v3

--- a/solution.py
+++ b/solution.py
@@ -10,7 +10,8 @@
 FRESH = 8.0 / 7.0
 LANES = 128
 SUB = 8
-EXT = 3
+EXT = 4
+FAR = 3
 SPILL = EXT + 1
 F32 = jnp.float32
 BF16 = jnp.bfloat16
@@ -176,7 +177,7 @@
         sums_ref[i] = sums
 
 
-def pack_body(where_ref, blocks_ref, pattern_ref, top_ref, prolong_ref, targets_ref, low_ref, high_ref, fine_ref):
+def pack_body(where_ref, blocks_ref, pattern_ref, top_ref, low_ref, high_ref):
     modes = blocks_ref.shape[1]
     total = blocks_ref.shape[3]
     halo = low_ref.shape[1]
@@ -193,15 +194,26 @@
             offset = pattern_ref[k + 1 : k + 2, cols] - (where_ref[2] + at) - column
             out[row + k : row + k + 1, :] = offset.astype(F32)
         row += SUB
-        for i in range(top_ref.shape[1] // halo):
-            out[row + i * width : row + (i + 1) * width, :] = top_ref[:, i * halo : (i + 1) * halo]
-    rows = prolong_ref.shape[2]
+        for i in range(pl.cdiv(top_ref.shape[1], halo)):
+            part = top_ref[:, i * halo : (i + 1) * halo]
+            out[row + i * width : row + (i + 1) * width, 0 : part.shape[1]] = part
+
+
+def pack_prolong_body(where_ref, prolong_ref, targets_ref, section_ref, fine_ref, far_ref):
+    modes, rows = prolong_ref.shape[1:3]
+    width, total = section_ref.shape[2:]
     for k in range(3):
         for m in range(modes):
             at = (k * modes + m) * rows
             fine_ref[at : at + rows, :] = prolong_ref[k, m].astype(F32)
         at = 3 * modes * rows + k
         fine_ref[at : at + 1, :] = targets_ref[k : k + 1, :].astype(F32)
+    reach = far_ref.shape[1]
+    cols = pl.ds(pl.multiple_of(where_ref[5] * (total - reach), LANES), reach)
+    for k in range(3):
+        for p in range(modes):
+            at = (k * modes + p) * width
+            far_ref[at : at + width, :] = section_ref[k, p, :, cols].astype(F32)
 
 
 def setup_body(where_ref, left_ref, right_ref, blocks_ref, pattern_ref, matrix_ref, offset_ref, inverse_ref):
@@ -308,7 +320,7 @@
         other[b + 1] = start + second
         sol_ref[b] = start + second
 
-    by_two(EXT - 1, count + 2, first)
+    by_two(EXT - FAR, count + 2 * FAR, first)
 
     def down(i, carry):
         for j in range(2):
@@ -331,8 +343,7 @@
     top_ref[...] = jnp.broadcast_to(pltpu.roll(row, where_ref[4], 1)[0:1], top_ref.shape)
 
 
-def top_body(where_ref, parts_ref, left_ref, top_inverse_ref, right_ref, sol_ref, section_ref, field_ref, edge_ref, column):
-    count, modes, width = section_ref.shape[3] // LANES, section_ref.shape[1], section_ref.shape[2]
+def top_answers(parts_ref, rows_of, width, column, slots):
     sections = parts_ref.shape[0]
     chunk_count = sections * width // LANES
     sub = lax.broadcasted_iota(jnp.int32, (SUB, LANES), 0)
@@ -347,46 +358,26 @@
             term = jnp.where(chunk == q, value, 0.0)
             chunks[q] = term if chunks[q] is None else chunks[q] + term
     chunks = [jnp.sum(c, axis=0, keepdims=True) for c in chunks]
-    halo = left_ref.shape[1]
-    at_top = 3 * modes * SUB + SUB
-    answers = []
-    for side in range(3):
+    for i, places in enumerate(slots):
         total = None
         for q in range(chunk_count):
-            if side == 1:
-                part = top_inverse_ref[:, q * LANES : (q + 1) * LANES]
-            else:
-                ref = left_ref if side == 0 else right_ref
-                i, at = divmod(q * LANES, halo)
-                part = ref[pl.ds(at_top + i * width, width), pl.ds(at, LANES)]
-            term = part * chunks[q]
+            term = rows_of(i, q) * chunks[q]
             total = term if total is None else total + term
-        answers.append(jnp.sum(total, axis=1, keepdims=True))
-    for side in range(3):
-        column[side * width : (side + 1) * width, :] = jnp.broadcast_to(answers[side], (width, LANES))
-    zero = jnp.zeros((SUB, LANES), F32)
-
-    def correct(b):
-        cols = pl.ds(pl.multiple_of(b * LANES, LANES), LANES)
-        terms = []
-        for p in range(SUB):
-            if p < modes:
-                value = sum(section_ref[k, p, :, cols].astype(F32) * column[k * width : (k + 1) * width, :] for k in range(3))
-                terms.append(jnp.sum(value.reshape(width // SUB, SUB, LANES), axis=0))
-            else:
-                terms.append(zero)
-        field_ref[b] = sol_ref[b + EXT] + fold_rows(terms)
-
-    by_two(0, count, correct)
-    start = jnp.where(where_ref[5] > 0, count - EXT, 0)
-    for i in range(EXT):
-        edge_ref[i] = field_ref[start + i]
+        answer = jnp.broadcast_to(jnp.sum(total, axis=1, keepdims=True), (width, LANES))
+        for place in places:
+            column[place * width : (place + 1) * width, :] = answer
 
 
 def up_body(
     where_ref,
-    middle_ref,
-    edge_ref,
+    parts_ref,
+    left_ref,
+    top_inverse_ref,
+    right_ref,
+    far_top_ref,
+    section_ref,
+    far_ref,
+    sol_ref,
     rhs_ref,
     matrix_ref,
     offset_ref,
@@ -403,6 +394,7 @@
     fine_inverse_ref,
     change_ref,
     field_ref,
+    column,
     field,
     other,
     final,
@@ -414,22 +406,52 @@
     count = total - 2 * EXT
     modes = matrix_ref.shape[2]
     zero = jnp.zeros((SUB, LANES), F32)
-    from_left = where_ref[5] > 0
-    for i in range(EXT):
-        field[1 + i] = jnp.where(from_left, edge_ref[i], 0.0)
-        field[1 + EXT + count + i] = jnp.where(from_left, 0.0, edge_ref[i])
-    for i in range(count):
-        field[1 + EXT + i] = middle_ref[i]
-    for edge in (0, total + 1):
-        field[edge] = zero
-        other[edge] = zero
+    width = section_ref.shape[2]
+    halo = left_ref.shape[1]
+    at_top = 3 * modes * SUB + SUB
+
+    def rows_of(i, q):
+        if i in (1, 3):
+            return (top_inverse_ref if i == 1 else far_top_ref)[:, q * LANES : (q + 1) * LANES]
+        chunk, at = divmod(q * LANES, halo)
+        return (left_ref if i == 0 else right_ref)[pl.ds(at_top + chunk * width, width), pl.ds(at, LANES)]
+
+    top_answers(parts_ref, rows_of, width, column, [(1,), (2,), (3,), (0, 4)])
+
+    def corrected(b, slot, section_of):
+        terms = []
+        for p in range(SUB):
+            if p < modes:
+                value = sum(section_of(k, p) * column[(slot + k) * width : (slot + k + 1) * width, :] for k in range(3))
+                terms.append(jnp.sum(value.reshape(width // SUB, SUB, LANES), axis=0))
+            else:
+                terms.append(zero)
+        field[b + 1] = sol_ref[b] + fold_rows(terms)
+
+    def far_block(slot, first):
+        def body(b, carry):
+            cols = pl.ds(pl.multiple_of((b - first) * LANES, LANES), LANES)
+            corrected(b, slot, lambda k, p: far_ref[pl.ds((k * modes + p) * width, width), cols])
+            return carry
+
+        return body
+
+    def own_block(b, carry):
+        cols = pl.ds(pl.multiple_of((b - EXT) * LANES, LANES), LANES)
+        corrected(b, 1, lambda k, p: section_ref[k, p, :, cols].astype(F32))
+        return carry
+
+    middle = where_ref[3] + EXT
+    low, high = middle - FAR, middle + FAR + 1
+    lax.fori_loop(low, jnp.minimum(high, EXT), far_block(0, EXT - FAR), 0)
+    lax.fori_loop(jnp.maximum(low, EXT), jnp.minimum(high, EXT + count), own_block, 0)
+    lax.fori_loop(jnp.maximum(low, EXT + count), high, far_block(2, EXT + count), 0)
 
     def smooth_first(b):
         change = inverse_ref[b] * (rhs_ref[b] - coarse_product(matrix_ref, offset_ref, field, b))
         final[b] = change
         other[b + 1] = field[b + 1] + change
 
-    middle = where_ref[3] + EXT
     by_two(middle - 3, 7, smooth_first)
 
     def smooth_second(b):
@@ -502,9 +524,12 @@
     odd_swap = [(i, i + 1) for i in range(1, devices - 1, 2)] + [(i + 1, i) for i in range(1, devices - 1, 2)]
     even_swap = [(i, i ^ 1) for i in range(devices)]
     pairs = [[2 * i, 2 * i + 1] for i in range(secs // 2)]
-    reach = [c for c in range(secs // 2) if c < EXT]
-    edge_moves = [(s * secs + c, (s + 1) * secs + c) for s in range(slabs - 1) for c in reach]
-    edge_moves += [((s + 1) * secs + secs - 1 - c, s * secs + secs - 1 - c) for s in range(slabs - 1) for c in reach]
+    reach = [c for c in range(secs // 2) if c < FAR]
+
+    def one_sided(value, step):
+        moves = [(s * secs + c, (s + step) * secs + c) for s in range(slabs - step) for c in reach]
+        moves += [((s + step) * secs + secs - 1 - c, s * secs + secs - 1 - c) for s in range(slabs - step) for c in reach]
+        return lax.ppermute(value, both, moves)
 
     slab_odd = [(i, i + 1) for i in range(1, slabs - 1, 2)] + [(i + 1, i) for i in range(1, slabs - 1, 2)]
     slab_pairs = [[2 * i, 2 * i + 1] for i in range(slabs // 2)]
@@ -521,22 +546,12 @@
     work = [pltpu.VMEM((3, rows, own), F32), pltpu.VMEM((2, rows, own), F32), pltpu.VMEM((rows, own), F32)]
     inverse, start = call(first_body, [fine, fine], [VMEM] * 2)(fine_blocks, source)
 
-    first_near = nearby(start)
-    held = lax.optimization_barrier((first_near[0], coarse_blocks, coarse_pattern, coarsest_inverse, prolong, prolong_pattern))
-    side = struct(3 * modes * SUB + SUB + width * (coarsest_inverse.shape[1] // halo), halo)
-    low, high, fine_pack = call(pack_body, [side, side, struct(3 * modes * rows + SUB, own)], [SMEM] + [VMEM] * 5)(
-        where, *held[1:]
-    )
-    first_near = (held[0], *first_near[1:])
+    near = nearby(start)
+    pair, *held = lax.optimization_barrier((near[0], coarse_blocks, coarse_pattern, coarsest_inverse))
+    near = (pair, *near[1:])
+    side = struct(3 * modes * SUB + SUB + width * pl.cdiv(coarsest_inverse.shape[1], halo), halo)
+    low, high = call(pack_body, [side, side], [SMEM] + [VMEM] * 3)(where, *held)
     left_data, right_data = beside(high, 1), beside(low, -1)
-    odd_prolong = lax.ppermute(fine_pack, both, odd_swap)
-    even_prolong = lax.ppermute(fine_pack, both, even_swap)
-    matrix, offset, coarse_inverse = call(
-        setup_body,
-        [struct(blocks, 3, modes, SUB, LANES), struct(blocks, SUB, LANES, dtype=jnp.int32), struct(blocks, SUB, LANES)],
-        [SMEM] + [VMEM] * 4,
-    )(where, left_data, right_data, coarse_blocks, coarse_pattern)
-
     def step(body, outs, near, *rest):
         return call(body, outs, [SMEM] + [VMEM] * (5 + len(rest)), work)(where, *near, fine_blocks, fine_pattern, *rest)
 
@@ -544,12 +559,30 @@
     line = pltpu.VMEM((blocks + 2, SUB, LANES), F32)
     for cycle in range(CYCLES):
         if cycle == 0:
-            change, near = start, first_near
+            change = start
         else:
             change, field = step(field_body, [fine, fine], nearby(solution), source, inverse)
             near = nearby(field)
         solution = step(solution_body, [fine], near, source, inverse, change)[0]
+        if cycle == 0:
+            solution, left_data, right_data = lax.optimization_barrier((solution, left_data, right_data))
+            matrix, offset, coarse_inverse = call(
+                setup_body,
+                [struct(blocks, 3, modes, SUB, LANES), struct(blocks, SUB, LANES, dtype=jnp.int32), struct(blocks, SUB, LANES)],
+                [SMEM] + [VMEM] * 4,
+            )(where, left_data, right_data, coarse_blocks, coarse_pattern)
         near = nearby(solution)
+        if cycle == 0:
+            pair, *held = lax.optimization_barrier((near[0], prolong, prolong_pattern, section_prolong, coarsest_inverse))
+            near = (pair, *near[1:])
+            fine_pack, far = call(
+                pack_prolong_body,
+                [struct(3 * modes * rows + SUB, own), struct(3 * modes * width, FAR * LANES)],
+                [SMEM] + [VMEM] * 3,
+            )(where, *held[:3])
+            far_sections, far_top = one_sided(far, 1), one_sided(held[3], 2)
+            odd_prolong = lax.ppermute(fine_pack, both, odd_swap)
+            even_prolong = lax.ppermute(fine_pack, both, even_swap)
         sums = step(restrict_body, [struct(secs, SUB, 3 * LANES)], near, source, prolong, prolong_pattern)[0]
         parts = lax.all_to_all(sums, "sec", 0, 0, tiled=True)
         ends, everything = call(gather_body, [struct(2 * SPILL, SUB, LANES), struct(secs + 2, SUB, LANES)], [VMEM])(parts)
@@ -558,16 +591,17 @@
         rhs, coarse_sol, top = call(
             coarse_down_body, [coarse, coarse, struct(slabs, LANES)], [SMEM] + [VMEM] * 7, [line, line]
         )(where, everything, even, odd, matrix, offset, coarse_inverse, section_prolong)
+        if cycle == 0:
+            top, far_sections, far_top, odd_prolong, even_prolong = lax.optimization_barrier(
+                (top, far_sections, far_top, odd_prolong, even_prolong)
+            )
         tops = lax.all_to_all(top, "slab", 0, 0, tiled=True)
-        middle, edge = call(
-            top_body,
-            [struct(count, SUB, LANES), struct(EXT, SUB, LANES)],
-            [SMEM] + [VMEM] * 6,
-            [pltpu.VMEM((3 * width, LANES), F32)],
-        )(where, tops, left_data, coarsest_inverse, right_data, coarse_sol, section_prolong)
-        edge = lax.ppermute(edge, both, edge_moves)
-        change, field = call(up_body, [fine, fine], [SMEM] + [VMEM] * 16, [line, line, line] + work)(
-            where, middle, edge, rhs, matrix, offset, coarse_inverse, *near[:2], prolong, even_prolong, odd_prolong, prolong_pattern, fine_blocks, fine_pattern, source, inverse
+        change, field = call(
+            up_body, [fine, fine], [SMEM] + [VMEM] * 22, [pltpu.VMEM((5 * width, LANES), F32), line, line, line] + work
+        )(
+            *(where, tops, left_data, coarsest_inverse, right_data, far_top, section_prolong, far_sections, coarse_sol, rhs),
+            *(matrix, offset, coarse_inverse, *near[:2], prolong, even_prolong, odd_prolong, prolong_pattern),
+            *(fine_blocks, fine_pattern, source, inverse),
         )
         solution = step(solution_body, [fine], nearby(field), source, inverse, change)[0]
     return solution

time: 224 us -> 214 us (0.955)
  waiting for transfers between devices: 43.4 us -> 35.2 us
  starting transfers between devices: 50.4 us -> 48.1 us
    ppermute x2, waiting for transfers between devices: 10.5 us -> 0.01 us  [one_sided(): return lax.ppermute(value, both, moves)]
    ppermute x7, starting transfers between devices: 20.9 us -> 17.7 us  [nearby(): odd = lax.ppermute(field, both, odd_swap)]
    all_to_all x2, blocking collectives: 16.5 us -> 19.5 us  [shards(): parts = lax.all_to_all(sums, 'sec', 0, 0, tiled=True)]
    unnamed x28 -> x26, local copies, waits for them, and re-layouts: 5.53 us -> 4.58 us
    pallas_call x5 -> x4, Pallas kernels: 7.39 us -> 6.85 us  [the longest x2 5.63 us: shards(): call(up_body, [fine, fine], [SMEM] + [VMEM] * 22, [pltpu.VMEM((5 * width,...]
  transfers between devices with their start and end apart: 15 -> 15, of which waited for: 9 -> 8; matrix products, arithmetic and copies ran while one was open for 0% -> 0% of each run, Pallas kernels for 4% -> 4%
where the time goes in v4:
time: 214 us
  blocking collectives  101 us (47%)
  starting transfers between devices  48.1 us (22%)
  waiting for transfers between devices  35.2 us (16%)
  Pallas kernels  23.8 us (11%)
  local copies, waits for them, and re-layouts  4.66 us (2%)
    all_to_all x2, blocking collectives, shards(): tops = lax.all_to_all(top, 'slab', 0, 0, tiled=True)  58.8 us
    ppermute x7, waiting for transfers between devices, nearby(): odd = lax.ppermute(field, both, odd_swap)  33.7 us
    all_to_all x2, blocking collectives, shards(): parts = lax.all_to_all(sums, 'sec', 0, 0, tiled=True)  19.5 us
    ppermute x7, starting transfers between devices, nearby(): odd = lax.ppermute(field, both, odd_swap)  17.7 us
    all_gather x7, blocking collectives, nearby(): pair = lax.all_gather(field, 'sec', axis_index_groups=pairs, axis=0)  13.8 us
    pallas_call x7, Pallas kernels, step(): call(body, outs, [SMEM] + [VMEM] * (5 + len(rest)), work)  9.55 us
    all_gather x2, blocking collectives, shards(): even = lax.all_gather(ends, 'slab', axis_index_groups=slab_pairs, axis=0)  9.36 us
    ppermute x2, starting transfers between devices, beside(): lax.ppermute(value, 'slab', [(i, i + step) for i in range(max(0, -step),...  8.08 us
  transfers between devices with their start and end apart: 15, of which 8 were waited for; matrix products, arithmetic and copies ran while one was open for 0% of the time, Pallas kernels for 4%

profile of v4, /device:TPU:32, one launch (start us, length us, event | category | flops | bytes accessed | tf_op | source)
XLA Modules:
  0.0 213.6 jit_solution(9752623097026842059)
XLA Ops:
  7.3 3.4 %collective-permute-start.1 = (f32[224,512]{1,0:T(8,128)S(1)}, f32[224,512]{1,0:T(8,128)S(1)}, u32[]{:S(2)}, u32[]{:S(2)}) collective-permute-start(f32[224,512]{1,0:T(8,128)S(1)} %get-tuple-element.53), channel_id=1, source_target_pairs={{0,8},{8,16},{16,24},{24,32},{32,40},{40,48},{48,56},{56,64},{64,7... | collective-permute-start | bytes 1376264 | tf_op jit(solution)/shard_map/ppermute | solution.py:543
  10.7 4.7 %collective-permute-start.2 = (f32[224,512]{1,0:T(8,128)S(1)}, f32[224,512]{1,0:T(8,128)S(1)}, u32[]{:S(2)}, u32[]{:S(2)}) collective-permute-start(f32[224,512]{1,0:T(8,128)S(1)} %get-tuple-element.54), channel_id=1, source_target_pairs={{8,0},{16,8},{24,16},{32,24},{40,32},{48,40},{56,48},{64,56},{72,6... | collective-permute-start | bytes 1376264 | tf_op jit(solution)/shard_map/ppermute | solution.py:543
  15.4 3.9 %collective-permute-start = (f32[64,128]{1,0:T(8,128)S(1)}, f32[64,128]{1,0:T(8,128)S(1)}, u32[]{:S(2)}, u32[]{:S(2)}) collective-permute-start(f32[64,128]{1,0:T(8,128)S(1)} %get-tuple-element.47.field_ref.change_ref), channel_id=1, source_target_pairs={{1,2},{3,4},{5,6},{7,8},{9,10},{11,12},{13,14},{15,16},{17,18},{19... | collective-permute-start | bytes 98312 | tf_op jit(solution)/shard_map/ppermute | solution.py:538
  19.6 6.6 %collective-permute-done.odd_ref = f32[64,128]{1,0:T(8,128)S(1)} collective-permute-done((f32[64,128]{1,0:T(8,128)S(1)}, f32[64,128]{1,0:T(8,128)S(1)}, u32[]{:S(2)}, u32[]{:S(2)}) %collective-permute-start) | collective-permute-done | bytes 32800 | tf_op jit(solution)/shard_map/ppermute | solution.py:538
  34.1 7.4 %collective-permute-start.7 = (f32[1160,128]{1,0:T(8,128)S(1)}, f32[1160,128]{1,0:T(8,128)S(1)}, u32[]{:S(2)}, u32[]{:S(2)}) collective-permute-start(f32[1160,128]{1,0:T(8,128)S(1)} %get-tuple-element.70), channel_id=1, source_target_pairs={{1,2},{3,4},{5,6},{7,8},{9,10},{11,12},{13,14},{15,16},{17,18},{19... | collective-permute-start | bytes 1781768 | tf_op jit(solution)/shard_map/ppermute | solution.py:584
  43.9 3.9 %collective-permute-start.6 = (f32[24,1536]{1,0:T(8,128)S(1)}, f32[24,1536]{1,0:T(8,128)S(1)}, u32[]{:S(2)}, u32[]{:S(2)}) collective-permute-start(f32[24,1536]{1,0:T(8,128)S(1)} %copy-done.7), channel_id=1, source_target_pairs={{0,16},{1,17},{2,18},{8,24},{9,25},{10,26},{16,32},{17,33},{18,34}... | collective-permute-start | bytes 442376 | tf_op jit(solution)/shard_map/ppermute | solution.py:532
  48.1 2.8 %collective-permute-done.3.odd_ref = f32[64,128]{1,0:T(8,128)S(1)} collective-permute-done((f32[64,128]{1,0:T(8,128)S(1)}, f32[64,128]{1,0:T(8,128)S(1)}, u32[]{:S(2)}, u32[]{:S(2)}) %collective-permute-start.3) | collective-permute-done | bytes 32800 | tf_op jit(solution)/shard_map/ppermute | solution.py:538
  52.4 11.3 %all_to_all.32.parts_ref = f32[8,8,384]{2,1,0:T(8,128)S(1)} all-to-all(f32[8,8,384]{2,1,0:T(8,128)S(1)} %shard_map.96), channel_id=1, replica_groups=mesh['slab'=64,'sec'=8] {'sec'}, dimensions={0} | all-to-all | bytes 196608 | tf_op jit(solution)/shard_map/all_to_all | solution.py:587
  63.7 5.1 %collective-permute-start.4 = (f32[10,8,128]{2,1,0:T(8,128)S(1)}, f32[10,8,128]{2,1,0:T(8,128)S(1)}, u32[]{:S(2)}, u32[]{:S(2)}) collective-permute-start(f32[10,8,128]{2,1,0:T(8,128)S(1)} %get-tuple-element.58), channel_id=1, source_target_pairs={{8,16},{24,32},{40,48},{56,64},{72,80},{88,96},{104,112},{120,128}... | collective-permute-start | bytes 122888 | tf_op jit(solution)/shard_map/ppermute | solution.py:589
  69.6 4.7 %all-gather.2 = f32[20,8,128]{2,1,0:T(8,128)S(1)} all-gather(f32[10,8,128]{2,1,0:T(8,128)S(1)} %get-tuple-element.58), channel_id=4, replica_groups={{0,8},{16,24},{32,40},{48,56},{64,72},{80,88},{96,104},{112,120},{128,1..., dimensions={0}, use_global_device_ids=true | all-gather | bytes 122880 | tf_op jit(solution)/shard_map/all_gather | solution.py:590
  76.6 33.1 %all_to_all.33 = f32[64,1,128]{2,1,0:T(1,128)S(1)} all-to-all(f32[64,1,128]{2,1,0:T(1,128)S(1)} %bitcast.43), channel_id=1, replica_groups=mesh['slab'=64,'sec'=8] {'slab'}, dimensions={0} | all-to-all | bytes 65536 | tf_op jit(solution)/shard_map/all_to_all | solution.py:598
  109.7 2.8 %shard_map.101 = (f32[64,128]{1,0:T(8,128)S(1)}, f32[64,128]{1,0:T(8,128)S(1)}) custom-call(s32[7]{0:T(128)S(1)} %stack.35.where_ref, f32[64,128]{1,0:T(8,128)S(1)} %bitcast.42, f32[224,512]{1,0:T(8,128)S(1)} %collective-permute-done.1.left_ref, f32[24,1536]{1,0:T(8,128)S(1)} %copy-done.7, f32[224,512]{1,0:T(8,128)S(1)} %collective-permute-done.2.right_ref, ...), custom_call_target="tpu_custom_call" | custom-call | flops 1048576 | bytes 1048576 | tf_op jit(solution)/shard_map/pallas_call | solution.py:599
  117.0 5.0 %collective-permute-done.9.odd_ref = f32[64,128]{1,0:T(8,128)S(1)} collective-permute-done((f32[64,128]{1,0:T(8,128)S(1)}, f32[64,128]{1,0:T(8,128)S(1)}, u32[]{:S(2)}, u32[]{:S(2)}) %collective-permute-start.9) | collective-permute-done | bytes 32800 | tf_op jit(solution)/shard_map/ppermute | solution.py:538
  123.2 2.5 %collective-permute-start.10 = (f32[64,128]{1,0:T(8,128)S(1)}, f32[64,128]{1,0:T(8,128)S(1)}, u32[]{:S(2)}, u32[]{:S(2)}) collective-permute-start(f32[64,128]{1,0:T(8,128)S(1)} %shard_map.103.field_ref), channel_id=1, source_target_pairs={{1,2},{3,4},{5,6},{7,8},{9,10},{11,12},{13,14},{15,16},{17,18},{19... | collective-permute-start | bytes 98312 | tf_op jit(solution)/shard_map/ppermute | solution.py:538
  127.9 4.8 %collective-permute-done.10.odd_ref = f32[64,128]{1,0:T(8,128)S(1)} collective-permute-done((f32[64,128]{1,0:T(8,128)S(1)}, f32[64,128]{1,0:T(8,128)S(1)}, u32[]{:S(2)}, u32[]{:S(2)}) %collective-permute-start.10) | collective-permute-done | bytes 32800 | tf_op jit(solution)/shard_map/ppermute | solution.py:538
  133.9 2.5 %collective-permute-start.11 = (f32[64,128]{1,0:T(8,128)S(1)}, f32[64,128]{1,0:T(8,128)S(1)}, u32[]{:S(2)}, u32[]{:S(2)}) collective-permute-start(f32[64,128]{1,0:T(8,128)S(1)} %get-tuple-element.80.field_ref), channel_id=1, source_target_pairs={{1,2},{3,4},{5,6},{7,8},{9,10},{11,12},{13,14},{15,16},{17,18},{19... | collective-permute-start | bytes 98312 | tf_op jit(solution)/shard_map/ppermute | solution.py:538
  138.5 4.8 %collective-permute-done.11.odd_ref = f32[64,128]{1,0:T(8,128)S(1)} collective-permute-done((f32[64,128]{1,0:T(8,128)S(1)}, f32[64,128]{1,0:T(8,128)S(1)}, u32[]{:S(2)}, u32[]{:S(2)}) %collective-permute-start.11) | collective-permute-done | bytes 32800 | tf_op jit(solution)/shard_map/ppermute | solution.py:538
  144.5 2.5 %collective-permute-start.12 = (f32[64,128]{1,0:T(8,128)S(1)}, f32[64,128]{1,0:T(8,128)S(1)}, u32[]{:S(2)}, u32[]{:S(2)}) collective-permute-start(f32[64,128]{1,0:T(8,128)S(1)} %shard_map.107.field_ref), channel_id=1, source_target_pairs={{1,2},{3,4},{5,6},{7,8},{9,10},{11,12},{13,14},{15,16},{17,18},{19... | collective-permute-start | bytes 98312 | tf_op jit(solution)/shard_map/ppermute | solution.py:538
  149.2 4.8 %collective-permute-done.12.odd_ref = f32[64,128]{1,0:T(8,128)S(1)} collective-permute-done((f32[64,128]{1,0:T(8,128)S(1)}, f32[64,128]{1,0:T(8,128)S(1)}, u32[]{:S(2)}, u32[]{:S(2)}) %collective-permute-start.12) | collective-permute-done | bytes 32800 | tf_op jit(solution)/shard_map/ppermute | solution.py:538
  155.4 8.2 %all_to_all.34.parts_ref = f32[8,8,384]{2,1,0:T(8,128)S(1)} all-to-all(f32[8,8,384]{2,1,0:T(8,128)S(1)} %shard_map.109), channel_id=1, replica_groups=mesh['slab'=64,'sec'=8] {'sec'}, dimensions={0} | all-to-all | bytes 196608 | tf_op jit(solution)/shard_map/all_to_all | solution.py:587
  165.5 4.7 %all-gather.7 = f32[20,8,128]{2,1,0:T(8,128)S(1)} all-gather(f32[10,8,128]{2,1,0:T(8,128)S(1)} %get-tuple-element.83), channel_id=9, replica_groups={{0,8},{16,24},{32,40},{48,56},{64,72},{80,88},{96,104},{112,120},{128,1..., dimensions={0}, use_global_device_ids=true | all-gather | bytes 122880 | tf_op jit(solution)/shard_map/all_gather | solution.py:590
  173.8 25.7 %all_to_all.35 = f32[64,1,128]{2,1,0:T(1,128)S(1)} all-to-all(f32[64,1,128]{2,1,0:T(1,128)S(1)} %bitcast.44), channel_id=1, replica_groups=mesh['slab'=64,'sec'=8] {'slab'}, dimensions={0} | all-to-all | bytes 65536 | tf_op jit(solution)/shard_map/all_to_all | solution.py:598
  199.5 2.8 %shard_map.112 = (f32[64,128]{1,0:T(8,128)S(1)}, f32[64,128]{1,0:T(8,128)S(1)}) custom-call(s32[7]{0:T(128)S(1)} %stack.35.where_ref, f32[64,128]{1,0:T(8,128)S(1)} %bitcast.41, f32[224,512]{1,0:T(8,128)S(1)} %collective-permute-done.1.left_ref, f32[24,1536]{1,0:T(8,128)S(1)} %copy-done.7, f32[224,512]{1,0:T(8,128)S(1)} %collective-permute-done.2.right_ref, ...), custom_call_target="tpu_custom_call" | custom-call | flops 1048576 | bytes 1048576 | tf_op jit(solution)/shard_map/pallas_call | solution.py:599
  206.8 5.0 %collective-permute-done.14.odd_ref = f32[64,128]{1,0:T(8,128)S(1)} collective-permute-done((f32[64,128]{1,0:T(8,128)S(1)}, f32[64,128]{1,0:T(8,128)S(1)}, u32[]{:S(2)}, u32[]{:S(2)}) %collective-permute-start.14) | collective-permute-done | bytes 32800 | tf_op jit(solution)/shard_map/ppermute | solution.py:538
  (70 shorter events, 50.4 us)
Async XLA Ops:
  0.0 4.8 %copy-start.11 = (s32[3,1024]{1,0:T(4,128)S(1)}, s32[3,1024]{1,0:T(4,128)}, u32[]{:S(2)}) copy-start(s32[3,1024]{1,0:T(4,128)} %pattern_ref.11) | copy-start | bytes 36868
  2.7 16.6 %copy-start.1 = (bf16[3,64,64,128]{3,2,1,0:T(8,128)(2,1)S(1)}, bf16[3,64,64,128]{3,2,1,0:T(8,128)(2,1)}, u32[]{:S(2)}) copy-start(bf16[3,64,64,128]{3,2,1,0:T(8,128)(2,1)} %matrix_ref.29) | copy-start | bytes 9437188
  2.7 23.6 %copy-start.5 = (f32[64,128]{1,0:T(8,128)S(1)}, f32[64,128]{1,0:T(8,128)}, u32[]{:S(2)}) copy-start(f32[64,128]{1,0:T(8,128)} %source_ref.19) | copy-start | bytes 98308
  2.7 23.6 %copy-start.10 = (s32[3,128]{1,0:T(4,128)S(1)}, s32[3,128]{1,0:T(4,128)}, u32[]{:S(2)}) copy-start(s32[3,128]{1,0:T(4,128)} %pattern_ref.16) | copy-start | bytes 4612
  7.3 20.2 %collective-permute-start.1 = (f32[224,512]{1,0:T(8,128)S(1)}, f32[224,512]{1,0:T(8,128)S(1)}, u32[]{:S(2)}, u32[]{:S(2)}) collective-permute-start(f32[224,512]{1,0:T(8,128)S(1)} %get-tuple-element.53), channel_id=1, source_target_pairs={{0,8},{8,16},{16,24},{24,32},{32,40},{40,48},{48,56},{56,64},{64,7... | collective-permute-start | bytes 1376264 | tf_op jit(solution)/shard_map/ppermute | solution.py:543
  10.7 18.6 %copy-start.2 = (bf16[3,6,24,1024]{3,2,1,0:T(8,128)(2,1)S(1)}, bf16[3,6,24,1024]{3,2,1,0:T(8,128)(2,1)}, u32[]{:S(2)}) copy-start(bf16[3,6,24,1024]{3,2,1,0:T(8,128)(2,1)} %section_ref.8) | copy-start | bytes 2654212
  10.7 18.6 %copy-start.3 = (bf16[3,64,6,128]{3,1,2,0:T(8,128)(2,1)S(1)}, bf16[3,64,6,128]{3,1,2,0:T(8,128)(2,1)}, u32[]{:S(2)}) copy-start(bf16[3,64,6,128]{3,1,2,0:T(8,128)(2,1)} %param.12) | copy-start | bytes 884740
  10.7 18.6 %copy-start.12 = (s32[3,128]{1,0:T(4,128)S(1)}, s32[3,128]{1,0:T(4,128)}, u32[]{:S(2)}) copy-start(s32[3,128]{1,0:T(4,128)} %targets_ref.8) | copy-start | bytes 4612
  10.7 16.7 %collective-permute-start.2 = (f32[224,512]{1,0:T(8,128)S(1)}, f32[224,512]{1,0:T(8,128)S(1)}, u32[]{:S(2)}, u32[]{:S(2)}) collective-permute-start(f32[224,512]{1,0:T(8,128)S(1)} %get-tuple-element.54), channel_id=1, source_target_pairs={{8,0},{16,8},{24,16},{32,24},{40,32},{48,40},{56,48},{64,56},{72,6... | collective-permute-start | bytes 1376264 | tf_op jit(solution)/shard_map/ppermute | solution.py:543
  15.4 10.8 %collective-permute-start = (f32[64,128]{1,0:T(8,128)S(1)}, f32[64,128]{1,0:T(8,128)S(1)}, u32[]{:S(2)}, u32[]{:S(2)}) collective-permute-start(f32[64,128]{1,0:T(8,128)S(1)} %get-tuple-element.47.field_ref.change_ref), channel_id=1, source_target_pairs={{1,2},{3,4},{5,6},{7,8},{9,10},{11,12},{13,14},{15,16},{17,18},{19... | collective-permute-start | bytes 98312 | tf_op jit(solution)/shard_map/ppermute | solution.py:538
  19.6 24.3 %copy-start.7 = (f32[24,1536]{1,0:T(8,128)S(1)}, f32[24,1536]{1,0:T(8,128)}, u32[]{:S(2)}) copy-start(f32[24,1536]{1,0:T(8,128)} %top_inverse_ref.3) | copy-start | bytes 442372
  30.0 46.6 %collective-permute-start.5 = (f32[432,384]{1,0:T(8,128)S(1)}, f32[432,384]{1,0:T(8,128)S(1)}, u32[]{:S(2)}, u32[]{:S(2)}) collective-permute-start(f32[432,384]{1,0:T(8,128)S(1)} %get-tuple-element.68), channel_id=1, source_target_pairs={{0,8},{1,9},{2,10},{8,16},{9,17},{10,18},{16,24},{17,25},{18,26},{... | collective-permute-start | bytes 1990664 | tf_op jit(solution)/shard_map/ppermute | solution.py:532
  31.9 37.0 %copy-start.9 = (bf16[3,6,6,1024]{3,2,1,0:T(8,128)(2,1)S(1)}, bf16[3,6,6,1024]{3,2,1,0:T(8,128)(2,1)}, u32[]{:S(2)}) copy-start(bf16[3,6,6,1024]{3,2,1,0:T(8,128)(2,1)} %blocks_ref.2) | copy-start | bytes 663556
  31.9 44.7 %collective-permute-start.8 = (f32[1160,128]{1,0:T(8,128)S(1)}, f32[1160,128]{1,0:T(8,128)S(1)}, u32[]{:S(2)}, u32[]{:S(2)}) collective-permute-start(f32[1160,128]{1,0:T(8,128)S(1)} %get-tuple-element.70), channel_id=1, source_target_pairs={{0,1},{1,0},{2,3},{3,2},{4,5},{5,4},{6,7},{7,6},{8,9},{9,8},{10,11... | collective-permute-start | bytes 1781768 | tf_op jit(solution)/shard_map/ppermute | solution.py:585
  34.1 42.5 %collective-permute-start.7 = (f32[1160,128]{1,0:T(8,128)S(1)}, f32[1160,128]{1,0:T(8,128)S(1)}, u32[]{:S(2)}, u32[]{:S(2)}) collective-permute-start(f32[1160,128]{1,0:T(8,128)S(1)} %get-tuple-element.70), channel_id=1, source_target_pairs={{1,2},{3,4},{5,6},{7,8},{9,10},{11,12},{13,14},{15,16},{17,18},{19... | collective-permute-start | bytes 1781768 | tf_op jit(solution)/shard_map/ppermute | solution.py:584
  41.5 9.5 %collective-permute-start.3 = (f32[64,128]{1,0:T(8,128)S(1)}, f32[64,128]{1,0:T(8,128)S(1)}, u32[]{:S(2)}, u32[]{:S(2)}) collective-permute-start(f32[64,128]{1,0:T(8,128)S(1)} %shard_map.93.field_ref), channel_id=1, source_target_pairs={{1,2},{3,4},{5,6},{7,8},{9,10},{11,12},{13,14},{15,16},{17,18},{19... | collective-permute-start | bytes 98312 | tf_op jit(solution)/shard_map/ppermute | solution.py:538
  43.9 32.6 %collective-permute-start.6 = (f32[24,1536]{1,0:T(8,128)S(1)}, f32[24,1536]{1,0:T(8,128)S(1)}, u32[]{:S(2)}, u32[]{:S(2)}) collective-permute-start(f32[24,1536]{1,0:T(8,128)S(1)} %copy-done.7), channel_id=1, source_target_pairs={{0,16},{1,17},{2,18},{8,24},{9,25},{10,26},{16,32},{17,33},{18,34}... | collective-permute-start | bytes 442376 | tf_op jit(solution)/shard_map/ppermute | solution.py:532
  63.7 10.6 %collective-permute-start.4 = (f32[10,8,128]{2,1,0:T(8,128)S(1)}, f32[10,8,128]{2,1,0:T(8,128)S(1)}, u32[]{:S(2)}, u32[]{:S(2)}) collective-permute-start(f32[10,8,128]{2,1,0:T(8,128)S(1)} %get-tuple-element.58), channel_id=1, source_target_pairs={{8,16},{24,32},{40,48},{56,64},{72,80},{88,96},{104,112},{120,128}... | collective-permute-start | bytes 122888 | tf_op jit(solution)/shard_map/ppermute | solution.py:589
  112.5 9.5 %collective-permute-start.9 = (f32[64,128]{1,0:T(8,128)S(1)}, f32[64,128]{1,0:T(8,128)S(1)}, u32[]{:S(2)}, u32[]{:S(2)}) collective-permute-start(f32[64,128]{1,0:T(8,128)S(1)} %get-tuple-element.78.field_ref), channel_id=1, source_target_pairs={{1,2},{3,4},{5,6},{7,8},{9,10},{11,12},{13,14},{15,16},{17,18},{19... | collective-permute-start | bytes 98312 | tf_op jit(solution)/shard_map/ppermute | solution.py:538
  123.2 9.5 %collective-permute-start.10 = (f32[64,128]{1,0:T(8,128)S(1)}, f32[64,128]{1,0:T(8,128)S(1)}, u32[]{:S(2)}, u32[]{:S(2)}) collective-permute-start(f32[64,128]{1,0:T(8,128)S(1)} %shard_map.103.field_ref), channel_id=1, source_target_pairs={{1,2},{3,4},{5,6},{7,8},{9,10},{11,12},{13,14},{15,16},{17,18},{19... | collective-permute-start | bytes 98312 | tf_op jit(solution)/shard_map/ppermute | solution.py:538
  133.9 9.5 %collective-permute-start.11 = (f32[64,128]{1,0:T(8,128)S(1)}, f32[64,128]{1,0:T(8,128)S(1)}, u32[]{:S(2)}, u32[]{:S(2)}) collective-permute-start(f32[64,128]{1,0:T(8,128)S(1)} %get-tuple-element.80.field_ref), channel_id=1, source_target_pairs={{1,2},{3,4},{5,6},{7,8},{9,10},{11,12},{13,14},{15,16},{17,18},{19... | collective-permute-start | bytes 98312 | tf_op jit(solution)/shard_map/ppermute | solution.py:538
  144.5 9.5 %collective-permute-start.12 = (f32[64,128]{1,0:T(8,128)S(1)}, f32[64,128]{1,0:T(8,128)S(1)}, u32[]{:S(2)}, u32[]{:S(2)}) collective-permute-start(f32[64,128]{1,0:T(8,128)S(1)} %shard_map.107.field_ref), channel_id=1, source_target_pairs={{1,2},{3,4},{5,6},{7,8},{9,10},{11,12},{13,14},{15,16},{17,18},{19... | collective-permute-start | bytes 98312 | tf_op jit(solution)/shard_map/ppermute | solution.py:538
  163.6 8.0 %collective-permute-start.13 = (f32[10,8,128]{2,1,0:T(8,128)S(1)}, f32[10,8,128]{2,1,0:T(8,128)S(1)}, u32[]{:S(2)}, u32[]{:S(2)}) collective-permute-start(f32[10,8,128]{2,1,0:T(8,128)S(1)} %get-tuple-element.83), channel_id=1, source_target_pairs={{8,16},{24,32},{40,48},{56,64},{72,80},{88,96},{104,112},{120,128}... | collective-permute-start | bytes 122888 | tf_op jit(solution)/shard_map/ppermute | solution.py:589
  202.3 9.5 %collective-permute-start.14 = (f32[64,128]{1,0:T(8,128)S(1)}, f32[64,128]{1,0:T(8,128)S(1)}, u32[]{:S(2)}, u32[]{:S(2)}) collective-permute-start(f32[64,128]{1,0:T(8,128)S(1)} %get-tuple-element.87.field_ref), channel_id=1, source_target_pairs={{1,2},{3,4},{5,6},{7,8},{9,10},{11,12},{13,14},{15,16},{17,18},{19... | collective-permute-start | bytes 98312 | tf_op jit(solution)/shard_map/ppermute | solution.py:538
  (4 other events, 4.5 us)

commit v5 on v4

--- a/solution.py
+++ b/solution.py
@@ -199,7 +199,7 @@
             out[row + i * width : row + (i + 1) * width, 0 : part.shape[1]] = part
 
 
-def pack_prolong_body(where_ref, prolong_ref, targets_ref, section_ref, fine_ref, far_ref):
+def pack_prolong_body(where_ref, prolong_ref, targets_ref, section_ref, left_ref, right_ref, fine_ref, far_ref):
     modes, rows = prolong_ref.shape[1:3]
     width, total = section_ref.shape[2:]
     for k in range(3):
@@ -214,6 +214,17 @@
         for p in range(modes):
             at = (k * modes + p) * width
             far_ref[at : at + width, :] = section_ref[k, p, :, cols].astype(F32)
+    at_top = 3 * modes * SUB + SUB
+    at_far = 3 * modes * width
+    halo = left_ref.shape[1]
+    for q in range((far_ref.shape[0] - at_far) // width * (reach // LANES)):
+        chunk, at = divmod(q * LANES, halo)
+        place = (pl.ds(at_top + chunk * width, width), pl.ds(at, LANES))
+        if at_top + (chunk + 1) * width <= left_ref.shape[0]:
+            chunk, at = divmod(q * LANES, reach)
+            far_ref[at_far + chunk * width : at_far + (chunk + 1) * width, at : at + LANES] = jnp.where(
+                where_ref[5] > 0, left_ref[place], right_ref[place]
+            )
 
 
 def setup_body(where_ref, left_ref, right_ref, blocks_ref, pattern_ref, matrix_ref, offset_ref, inverse_ref):
@@ -374,7 +385,6 @@
     left_ref,
     top_inverse_ref,
     right_ref,
-    far_top_ref,
     section_ref,
     far_ref,
     sol_ref,
@@ -411,8 +421,11 @@
     at_top = 3 * modes * SUB + SUB
 
     def rows_of(i, q):
-        if i in (1, 3):
-            return (top_inverse_ref if i == 1 else far_top_ref)[:, q * LANES : (q + 1) * LANES]
+        if i == 1:
+            return top_inverse_ref[:, q * LANES : (q + 1) * LANES]
+        if i == 3:
+            chunk, at = divmod(q * LANES, far_ref.shape[1])
+            return far_ref[pl.ds((3 * modes + chunk) * width, width), pl.ds(at, LANES)]
         chunk, at = divmod(q * LANES, halo)
         return (left_ref if i == 0 else right_ref)[pl.ds(at_top + chunk * width, width), pl.ds(at, LANES)]
 
@@ -547,10 +560,10 @@
     inverse, start = call(first_body, [fine, fine], [VMEM] * 2)(fine_blocks, source)
 
     near = nearby(start)
-    pair, *held = lax.optimization_barrier((near[0], coarse_blocks, coarse_pattern, coarsest_inverse))
+    pair, later = lax.optimization_barrier((near[0], where))
     near = (pair, *near[1:])
     side = struct(3 * modes * SUB + SUB + width * pl.cdiv(coarsest_inverse.shape[1], halo), halo)
-    low, high = call(pack_body, [side, side], [SMEM] + [VMEM] * 3)(where, *held)
+    low, high = call(pack_body, [side, side], [SMEM] + [VMEM] * 3)(later, coarse_blocks, coarse_pattern, coarsest_inverse)
     left_data, right_data = beside(high, 1), beside(low, -1)
     def step(body, outs, near, *rest):
         return call(body, outs, [SMEM] + [VMEM] * (5 + len(rest)), work)(where, *near, fine_blocks, fine_pattern, *rest)
@@ -573,14 +586,14 @@
             )(where, left_data, right_data, coarse_blocks, coarse_pattern)
         near = nearby(solution)
         if cycle == 0:
-            pair, *held = lax.optimization_barrier((near[0], prolong, prolong_pattern, section_prolong, coarsest_inverse))
-            near = (pair, *near[1:])
+            mine, later = lax.optimization_barrier((near[2], where))
+            near = (*near[:2], mine)
             fine_pack, far = call(
                 pack_prolong_body,
-                [struct(3 * modes * rows + SUB, own), struct(3 * modes * width, FAR * LANES)],
-                [SMEM] + [VMEM] * 3,
-            )(where, *held[:3])
-            far_sections, far_top = one_sided(far, 1), one_sided(held[3], 2)
+                [struct(3 * modes * rows + SUB, own), struct((3 * modes + pl.cdiv(slabs * width, FAR * LANES)) * width, FAR * LANES)],
+                [SMEM] + [VMEM] * 5,
+            )(later, prolong, prolong_pattern, section_prolong, left_data, right_data)
+            far_data = one_sided(far, 1)
             odd_prolong = lax.ppermute(fine_pack, both, odd_swap)
             even_prolong = lax.ppermute(fine_pack, both, even_swap)
         sums = step(restrict_body, [struct(secs, SUB, 3 * LANES)], near, source, prolong, prolong_pattern)[0]
@@ -592,14 +605,12 @@
             coarse_down_body, [coarse, coarse, struct(slabs, LANES)], [SMEM] + [VMEM] * 7, [line, line]
         )(where, everything, even, odd, matrix, offset, coarse_inverse, section_prolong)
         if cycle == 0:
-            top, far_sections, far_top, odd_prolong, even_prolong = lax.optimization_barrier(
-                (top, far_sections, far_top, odd_prolong, even_prolong)
-            )
+            top, far_data, odd_prolong, even_prolong = lax.optimization_barrier((top, far_data, odd_prolong, even_prolong))
         tops = lax.all_to_all(top, "slab", 0, 0, tiled=True)
         change, field = call(
-            up_body, [fine, fine], [SMEM] + [VMEM] * 22, [pltpu.VMEM((5 * width, LANES), F32), line, line, line] + work
+            up_body, [fine, fine], [SMEM] + [VMEM] * 21, [pltpu.VMEM((5 * width, LANES), F32), line, line, line] + work
         )(
-            *(where, tops, left_data, coarsest_inverse, right_data, far_top, section_prolong, far_sections, coarse_sol, rhs),
+            *(where, tops, left_data, coarsest_inverse, right_data, section_prolong, far_data, coarse_sol, rhs),
             *(matrix, offset, coarse_inverse, *near[:2], prolong, even_prolong, odd_prolong, prolong_pattern),
             *(fine_blocks, fine_pattern, source, inverse),
         )

time: 214 us -> 209 us (0.977)
  starting transfers between devices: 48.1 us -> 42.4 us
  waiting for transfers between devices: 35.2 us -> 37.5 us
    ppermute x2 -> x1, starting transfers between devices: 5.8 us -> 1.92 us  [one_sided(): return lax.ppermute(value, both, moves)]
    all_to_all x2, blocking collectives: 19.5 us -> 16.4 us  [shards(): parts = lax.all_to_all(sums, 'sec', 0, 0, tiled=True)]
    ppermute x7, waiting for transfers between devices: 33.7 us -> 36 us  [nearby(): odd = lax.ppermute(field, both, odd_swap)]
  transfers between devices with their start and end apart: 15 -> 14, of which waited for: 8 -> 8; matrix products, arithmetic and copies ran while one was open for 0% -> 0% of each run, Pallas kernels for 4% -> 4%
where the time goes in v5:
time: 209 us; the launch traced here: 208 us
  blocking collectives  99 us (47%)
  starting transfers between devices  42.4 us (20%)
  waiting for transfers between devices  37.5 us (18%)
  Pallas kernels  23.9 us (11%)
  local copies, waits for them, and re-layouts  4.66 us (2%)
    all_to_all x2, blocking collectives, shards(): tops = lax.all_to_all(top, 'slab', 0, 0, tiled=True)  59.5 us
    ppermute x7, waiting for transfers between devices, nearby(): odd = lax.ppermute(field, both, odd_swap)  36 us
    ppermute x7, starting transfers between devices, nearby(): odd = lax.ppermute(field, both, odd_swap)  17.8 us
    all_to_all x2, blocking collectives, shards(): parts = lax.all_to_all(sums, 'sec', 0, 0, tiled=True)  16.4 us
    all_gather x7, blocking collectives, nearby(): pair = lax.all_gather(field, 'sec', axis_index_groups=pairs, axis=0)  13.8 us
    pallas_call x7, Pallas kernels, step(): call(body, outs, [SMEM] + [VMEM] * (5 + len(rest)), work)  9.56 us
    all_gather x2, blocking collectives, shards(): even = lax.all_gather(ends, 'slab', axis_index_groups=slab_pairs, axis=0)  9.36 us
    ppermute x2, starting transfers between devices, beside(): lax.ppermute(value, 'slab', [(i, i + step) for i in range(max(0, -step),...  7.95 us
  transfers between devices with their start and end apart: 14, of which 8 were waited for; matrix products, arithmetic and copies ran while one was open for 0% of the time, Pallas kernels for 4%

profile of v5, /device:TPU:32, one launch (start us, length us, event | category | flops | bytes accessed | tf_op | source)
XLA Modules:
  0.0 207.8 jit_solution(3672544669069892227)
XLA Ops:
  7.3 3.4 %collective-permute-start.1 = (f32[224,512]{1,0:T(8,128)S(1)}, f32[224,512]{1,0:T(8,128)S(1)}, u32[]{:S(2)}, u32[]{:S(2)}) collective-permute-start(f32[224,512]{1,0:T(8,128)S(1)} %get-tuple-element.45), channel_id=1, source_target_pairs={{0,8},{8,16},{16,24},{24,32},{32,40},{40,48},{48,56},{56,64},{64,7... | collective-permute-start | bytes 1376264 | tf_op jit(solution)/shard_map/ppermute | solution.py:556
  10.7 4.6 %collective-permute-start.2 = (f32[224,512]{1,0:T(8,128)S(1)}, f32[224,512]{1,0:T(8,128)S(1)}, u32[]{:S(2)}, u32[]{:S(2)}) collective-permute-start(f32[224,512]{1,0:T(8,128)S(1)} %get-tuple-element.46), channel_id=1, source_target_pairs={{8,0},{16,8},{24,16},{32,24},{40,32},{48,40},{56,48},{64,56},{72,6... | collective-permute-start | bytes 1376264 | tf_op jit(solution)/shard_map/ppermute | solution.py:556
  15.2 3.9 %collective-permute-start = (f32[64,128]{1,0:T(8,128)S(1)}, f32[64,128]{1,0:T(8,128)S(1)}, u32[]{:S(2)}, u32[]{:S(2)}) collective-permute-start(f32[64,128]{1,0:T(8,128)S(1)} %get-tuple-element.41.field_ref.change_ref), channel_id=1, source_target_pairs={{1,2},{3,4},{5,6},{7,8},{9,10},{11,12},{13,14},{15,16},{17,18},{19... | collective-permute-start | bytes 98312 | tf_op jit(solution)/shard_map/ppermute | solution.py:551
  19.4 6.8 %collective-permute-done.odd_ref = f32[64,128]{1,0:T(8,128)S(1)} collective-permute-done((f32[64,128]{1,0:T(8,128)S(1)}, f32[64,128]{1,0:T(8,128)S(1)}, u32[]{:S(2)}, u32[]{:S(2)}) %collective-permute-start) | collective-permute-done | bytes 32800 | tf_op jit(solution)/shard_map/ppermute | solution.py:551
  30.4 7.2 %collective-permute-start.6 = (f32[1160,128]{1,0:T(8,128)S(1)}, f32[1160,128]{1,0:T(8,128)S(1)}, u32[]{:S(2)}, u32[]{:S(2)}) collective-permute-start(f32[1160,128]{1,0:T(8,128)S(1)} %get-tuple-element.59), channel_id=1, source_target_pairs={{1,2},{3,4},{5,6},{7,8},{9,10},{11,12},{13,14},{15,16},{17,18},{19... | collective-permute-start | bytes 1781768 | tf_op jit(solution)/shard_map/ppermute | solution.py:597
  39.5 2.6 %collective-permute-start.3 = (f32[64,128]{1,0:T(8,128)S(1)}, f32[64,128]{1,0:T(8,128)S(1)}, u32[]{:S(2)}, u32[]{:S(2)}) collective-permute-start(f32[64,128]{1,0:T(8,128)S(1)} %shard_map.93.field_ref), channel_id=1, source_target_pairs={{1,2},{3,4},{5,6},{7,8},{9,10},{11,12},{13,14},{15,16},{17,18},{19... | collective-permute-start | bytes 98312 | tf_op jit(solution)/shard_map/ppermute | solution.py:551
  44.0 5.0 %collective-permute-done.3.odd_ref = f32[64,128]{1,0:T(8,128)S(1)} collective-permute-done((f32[64,128]{1,0:T(8,128)S(1)}, f32[64,128]{1,0:T(8,128)S(1)}, u32[]{:S(2)}, u32[]{:S(2)}) %collective-permute-start.3) | collective-permute-done | bytes 32800 | tf_op jit(solution)/shard_map/ppermute | solution.py:551
  50.5 8.2 %all_to_all.32.parts_ref = f32[8,8,384]{2,1,0:T(8,128)S(1)} all-to-all(f32[8,8,384]{2,1,0:T(8,128)S(1)} %shard_map.96), channel_id=1, replica_groups=mesh['slab'=64,'sec'=8] {'sec'}, dimensions={0} | all-to-all | bytes 196608 | tf_op jit(solution)/shard_map/all_to_all | solution.py:600
  58.6 3.7 %collective-permute-start.4 = (f32[10,8,128]{2,1,0:T(8,128)S(1)}, f32[10,8,128]{2,1,0:T(8,128)S(1)}, u32[]{:S(2)}, u32[]{:S(2)}) collective-permute-start(f32[10,8,128]{2,1,0:T(8,128)S(1)} %get-tuple-element.50), channel_id=1, source_target_pairs={{8,16},{24,32},{40,48},{56,64},{72,80},{88,96},{104,112},{120,128}... | collective-permute-start | bytes 122888 | tf_op jit(solution)/shard_map/ppermute | solution.py:602
  63.1 4.7 %all-gather.2 = f32[20,8,128]{2,1,0:T(8,128)S(1)} all-gather(f32[10,8,128]{2,1,0:T(8,128)S(1)} %get-tuple-element.50), channel_id=4, replica_groups={{0,8},{16,24},{32,40},{48,56},{64,72},{80,88},{96,104},{112,120},{128,1..., dimensions={0}, use_global_device_ids=true | all-gather | bytes 122880 | tf_op jit(solution)/shard_map/all_gather | solution.py:603
  70.1 33.8 %all_to_all.33 = f32[64,1,128]{2,1,0:T(1,128)S(1)} all-to-all(f32[64,1,128]{2,1,0:T(1,128)S(1)} %bitcast.43), channel_id=1, replica_groups=mesh['slab'=64,'sec'=8] {'slab'}, dimensions={0} | all-to-all | bytes 65536 | tf_op jit(solution)/shard_map/all_to_all | solution.py:609
  103.9 2.8 %shard_map.101 = (f32[64,128]{1,0:T(8,128)S(1)}, f32[64,128]{1,0:T(8,128)S(1)}) custom-call(s32[7]{0:T(128)S(1)} %stack.35.where_ref, f32[64,128]{1,0:T(8,128)S(1)} %bitcast.42, f32[224,512]{1,0:T(8,128)S(1)} %collective-permute-done.1.left_ref, f32[24,1536]{1,0:T(8,128)S(1)} %copy-done.7, f32[224,512]{1,0:T(8,128)S(1)} %collective-permute-done.2.right_ref, ...), custom_call_target="tpu_custom_call" | custom-call | flops 1048576 | bytes 1048576 | tf_op jit(solution)/shard_map/pallas_call | solution.py:610
  111.2 5.0 %collective-permute-done.8.odd_ref = f32[64,128]{1,0:T(8,128)S(1)} collective-permute-done((f32[64,128]{1,0:T(8,128)S(1)}, f32[64,128]{1,0:T(8,128)S(1)}, u32[]{:S(2)}, u32[]{:S(2)}) %collective-permute-start.8) | collective-permute-done | bytes 32800 | tf_op jit(solution)/shard_map/ppermute | solution.py:551
  117.4 2.5 %collective-permute-start.9 = (f32[64,128]{1,0:T(8,128)S(1)}, f32[64,128]{1,0:T(8,128)S(1)}, u32[]{:S(2)}, u32[]{:S(2)}) collective-permute-start(f32[64,128]{1,0:T(8,128)S(1)} %shard_map.103.field_ref), channel_id=1, source_target_pairs={{1,2},{3,4},{5,6},{7,8},{9,10},{11,12},{13,14},{15,16},{17,18},{19... | collective-permute-start | bytes 98312 | tf_op jit(solution)/shard_map/ppermute | solution.py:551
  122.1 4.8 %collective-permute-done.9.odd_ref = f32[64,128]{1,0:T(8,128)S(1)} collective-permute-done((f32[64,128]{1,0:T(8,128)S(1)}, f32[64,128]{1,0:T(8,128)S(1)}, u32[]{:S(2)}, u32[]{:S(2)}) %collective-permute-start.9) | collective-permute-done | bytes 32800 | tf_op jit(solution)/shard_map/ppermute | solution.py:551
  128.1 2.5 %collective-permute-start.10 = (f32[64,128]{1,0:T(8,128)S(1)}, f32[64,128]{1,0:T(8,128)S(1)}, u32[]{:S(2)}, u32[]{:S(2)}) collective-permute-start(f32[64,128]{1,0:T(8,128)S(1)} %get-tuple-element.68.field_ref), channel_id=1, source_target_pairs={{1,2},{3,4},{5,6},{7,8},{9,10},{11,12},{13,14},{15,16},{17,18},{19... | collective-permute-start | bytes 98312 | tf_op jit(solution)/shard_map/ppermute | solution.py:551
  132.8 4.7 %collective-permute-done.10.odd_ref = f32[64,128]{1,0:T(8,128)S(1)} collective-permute-done((f32[64,128]{1,0:T(8,128)S(1)}, f32[64,128]{1,0:T(8,128)S(1)}, u32[]{:S(2)}, u32[]{:S(2)}) %collective-permute-start.10) | collective-permute-done | bytes 32800 | tf_op jit(solution)/shard_map/ppermute | solution.py:551
  138.7 2.5 %collective-permute-start.11 = (f32[64,128]{1,0:T(8,128)S(1)}, f32[64,128]{1,0:T(8,128)S(1)}, u32[]{:S(2)}, u32[]{:S(2)}) collective-permute-start(f32[64,128]{1,0:T(8,128)S(1)} %shard_map.107.field_ref), channel_id=1, source_target_pairs={{1,2},{3,4},{5,6},{7,8},{9,10},{11,12},{13,14},{15,16},{17,18},{19... | collective-permute-start | bytes 98312 | tf_op jit(solution)/shard_map/ppermute | solution.py:551
  143.4 4.7 %collective-permute-done.11.odd_ref = f32[64,128]{1,0:T(8,128)S(1)} collective-permute-done((f32[64,128]{1,0:T(8,128)S(1)}, f32[64,128]{1,0:T(8,128)S(1)}, u32[]{:S(2)}, u32[]{:S(2)}) %collective-permute-start.11) | collective-permute-done | bytes 32800 | tf_op jit(solution)/shard_map/ppermute | solution.py:551
  149.6 8.2 %all_to_all.34.parts_ref = f32[8,8,384]{2,1,0:T(8,128)S(1)} all-to-all(f32[8,8,384]{2,1,0:T(8,128)S(1)} %shard_map.109), channel_id=1, replica_groups=mesh['slab'=64,'sec'=8] {'sec'}, dimensions={0} | all-to-all | bytes 196608 | tf_op jit(solution)/shard_map/all_to_all | solution.py:600
  159.8 4.7 %all-gather.7 = f32[20,8,128]{2,1,0:T(8,128)S(1)} all-gather(f32[10,8,128]{2,1,0:T(8,128)S(1)} %get-tuple-element.71), channel_id=9, replica_groups={{0,8},{16,24},{32,40},{48,56},{64,72},{80,88},{96,104},{112,120},{128,1..., dimensions={0}, use_global_device_ids=true | all-gather | bytes 122880 | tf_op jit(solution)/shard_map/all_gather | solution.py:603
  168.1 25.7 %all_to_all.35 = f32[64,1,128]{2,1,0:T(1,128)S(1)} all-to-all(f32[64,1,128]{2,1,0:T(1,128)S(1)} %bitcast.44), channel_id=1, replica_groups=mesh['slab'=64,'sec'=8] {'slab'}, dimensions={0} | all-to-all | bytes 65536 | tf_op jit(solution)/shard_map/all_to_all | solution.py:609
  193.7 2.8 %shard_map.112 = (f32[64,128]{1,0:T(8,128)S(1)}, f32[64,128]{1,0:T(8,128)S(1)}) custom-call(s32[7]{0:T(128)S(1)} %stack.35.where_ref, f32[64,128]{1,0:T(8,128)S(1)} %bitcast.41, f32[224,512]{1,0:T(8,128)S(1)} %collective-permute-done.1.left_ref, f32[24,1536]{1,0:T(8,128)S(1)} %copy-done.7, f32[224,512]{1,0:T(8,128)S(1)} %collective-permute-done.2.right_ref, ...), custom_call_target="tpu_custom_call" | custom-call | flops 1048576 | bytes 1048576 | tf_op jit(solution)/shard_map/pallas_call | solution.py:610
  201.0 5.0 %collective-permute-done.13.odd_ref = f32[64,128]{1,0:T(8,128)S(1)} collective-permute-done((f32[64,128]{1,0:T(8,128)S(1)}, f32[64,128]{1,0:T(8,128)S(1)}, u32[]{:S(2)}, u32[]{:S(2)}) %collective-permute-start.13) | collective-permute-done | bytes 32800 | tf_op jit(solution)/shard_map/ppermute | solution.py:551
  (68 shorter events, 47.8 us)
Async XLA Ops:
  0.0 4.8 %copy-start.11 = (s32[3,1024]{1,0:T(4,128)S(1)}, s32[3,1024]{1,0:T(4,128)}, u32[]{:S(2)}) copy-start(s32[3,1024]{1,0:T(4,128)} %pattern_ref.12) | copy-start | bytes 36868
  0.0 1.9 copy-start
  2.7 16.4 %copy-start.1 = (bf16[3,64,64,128]{3,2,1,0:T(8,128)(2,1)S(1)}, bf16[3,64,64,128]{3,2,1,0:T(8,128)(2,1)}, u32[]{:S(2)}) copy-start(bf16[3,64,64,128]{3,2,1,0:T(8,128)(2,1)} %matrix_ref.29) | copy-start | bytes 9437188
  2.7 23.6 %copy-start.5 = (f32[64,128]{1,0:T(8,128)S(1)}, f32[64,128]{1,0:T(8,128)}, u32[]{:S(2)}) copy-start(f32[64,128]{1,0:T(8,128)} %source_ref.19) | copy-start | bytes 98308
  2.7 23.6 %copy-start.10 = (s32[3,128]{1,0:T(4,128)S(1)}, s32[3,128]{1,0:T(4,128)}, u32[]{:S(2)}) copy-start(s32[3,128]{1,0:T(4,128)} %pattern_ref.17) | copy-start | bytes 4612
  7.3 20.2 %collective-permute-start.1 = (f32[224,512]{1,0:T(8,128)S(1)}, f32[224,512]{1,0:T(8,128)S(1)}, u32[]{:S(2)}, u32[]{:S(2)}) collective-permute-start(f32[224,512]{1,0:T(8,128)S(1)} %get-tuple-element.45), channel_id=1, source_target_pairs={{0,8},{8,16},{16,24},{24,32},{32,40},{40,48},{48,56},{56,64},{64,7... | collective-permute-start | bytes 1376264 | tf_op jit(solution)/shard_map/ppermute | solution.py:556
  10.7 16.8 %collective-permute-start.2 = (f32[224,512]{1,0:T(8,128)S(1)}, f32[224,512]{1,0:T(8,128)S(1)}, u32[]{:S(2)}, u32[]{:S(2)}) collective-permute-start(f32[224,512]{1,0:T(8,128)S(1)} %get-tuple-element.46), channel_id=1, source_target_pairs={{8,0},{16,8},{24,16},{32,24},{40,32},{48,40},{56,48},{64,56},{72,6... | collective-permute-start | bytes 1376264 | tf_op jit(solution)/shard_map/ppermute | solution.py:556
  15.2 11.0 %collective-permute-start = (f32[64,128]{1,0:T(8,128)S(1)}, f32[64,128]{1,0:T(8,128)S(1)}, u32[]{:S(2)}, u32[]{:S(2)}) collective-permute-start(f32[64,128]{1,0:T(8,128)S(1)} %get-tuple-element.41.field_ref.change_ref), channel_id=1, source_target_pairs={{1,2},{3,4},{5,6},{7,8},{9,10},{11,12},{13,14},{15,16},{17,18},{19... | collective-permute-start | bytes 98312 | tf_op jit(solution)/shard_map/ppermute | solution.py:551
  26.2 1.6 copy-start.2
  26.2 1.6 copy-start.3
  26.2 1.6 copy-start.12
  27.8 34.5 %copy-start.9 = (bf16[3,6,6,1024]{3,2,1,0:T(8,128)(2,1)S(1)}, bf16[3,6,6,1024]{3,2,1,0:T(8,128)(2,1)}, u32[]{:S(2)}) copy-start(bf16[3,6,6,1024]{3,2,1,0:T(8,128)(2,1)} %blocks_ref.3) | copy-start | bytes 663556
  28.5 41.6 %collective-permute-start.5 = (f32[528,384]{1,0:T(8,128)S(1)}, f32[528,384]{1,0:T(8,128)S(1)}, u32[]{:S(2)}, u32[]{:S(2)}) collective-permute-start(f32[528,384]{1,0:T(8,128)S(1)} %get-tuple-element.58), channel_id=1, source_target_pairs={{0,8},{1,9},{2,10},{8,16},{9,17},{10,18},{16,24},{17,25},{18,26},{... | collective-permute-start | bytes 2433032 | tf_op jit(solution)/shard_map/ppermute | solution.py:545
  30.4 39.6 %collective-permute-start.6 = (f32[1160,128]{1,0:T(8,128)S(1)}, f32[1160,128]{1,0:T(8,128)S(1)}, u32[]{:S(2)}, u32[]{:S(2)}) collective-permute-start(f32[1160,128]{1,0:T(8,128)S(1)} %get-tuple-element.59), channel_id=1, source_target_pairs={{1,2},{3,4},{5,6},{7,8},{9,10},{11,12},{13,14},{15,16},{17,18},{19... | collective-permute-start | bytes 1781768 | tf_op jit(solution)/shard_map/ppermute | solution.py:597
  37.6 32.4 %collective-permute-start.7 = (f32[1160,128]{1,0:T(8,128)S(1)}, f32[1160,128]{1,0:T(8,128)S(1)}, u32[]{:S(2)}, u32[]{:S(2)}) collective-permute-start(f32[1160,128]{1,0:T(8,128)S(1)} %get-tuple-element.59), channel_id=1, source_target_pairs={{0,1},{1,0},{2,3},{3,2},{4,5},{5,4},{6,7},{7,6},{8,9},{9,8},{10,11... | collective-permute-start | bytes 1781768 | tf_op jit(solution)/shard_map/ppermute | solution.py:598
  39.5 9.5 %collective-permute-start.3 = (f32[64,128]{1,0:T(8,128)S(1)}, f32[64,128]{1,0:T(8,128)S(1)}, u32[]{:S(2)}, u32[]{:S(2)}) collective-permute-start(f32[64,128]{1,0:T(8,128)S(1)} %shard_map.93.field_ref), channel_id=1, source_target_pairs={{1,2},{3,4},{5,6},{7,8},{9,10},{11,12},{13,14},{15,16},{17,18},{19... | collective-permute-start | bytes 98312 | tf_op jit(solution)/shard_map/ppermute | solution.py:551
  49.0 54.9 %copy-start.7 = (f32[24,1536]{1,0:T(8,128)S(1)}, f32[24,1536]{1,0:T(8,128)}, u32[]{:S(2)}) copy-start(f32[24,1536]{1,0:T(8,128)} %top_inverse_ref.3) | copy-start | bytes 442372
  58.6 9.2 %collective-permute-start.4 = (f32[10,8,128]{2,1,0:T(8,128)S(1)}, f32[10,8,128]{2,1,0:T(8,128)S(1)}, u32[]{:S(2)}, u32[]{:S(2)}) collective-permute-start(f32[10,8,128]{2,1,0:T(8,128)S(1)} %get-tuple-element.50), channel_id=1, source_target_pairs={{8,16},{24,32},{40,48},{56,64},{72,80},{88,96},{104,112},{120,128}... | collective-permute-start | bytes 122888 | tf_op jit(solution)/shard_map/ppermute | solution.py:602
  106.7 9.5 %collective-permute-start.8 = (f32[64,128]{1,0:T(8,128)S(1)}, f32[64,128]{1,0:T(8,128)S(1)}, u32[]{:S(2)}, u32[]{:S(2)}) collective-permute-start(f32[64,128]{1,0:T(8,128)S(1)} %get-tuple-element.66.field_ref), channel_id=1, source_target_pairs={{1,2},{3,4},{5,6},{7,8},{9,10},{11,12},{13,14},{15,16},{17,18},{19... | collective-permute-start | bytes 98312 | tf_op jit(solution)/shard_map/ppermute | solution.py:551
  117.4 9.5 %collective-permute-start.9 = (f32[64,128]{1,0:T(8,128)S(1)}, f32[64,128]{1,0:T(8,128)S(1)}, u32[]{:S(2)}, u32[]{:S(2)}) collective-permute-start(f32[64,128]{1,0:T(8,128)S(1)} %shard_map.103.field_ref), channel_id=1, source_target_pairs={{1,2},{3,4},{5,6},{7,8},{9,10},{11,12},{13,14},{15,16},{17,18},{19... | collective-permute-start | bytes 98312 | tf_op jit(solution)/shard_map/ppermute | solution.py:551
  128.1 9.5 %collective-permute-start.10 = (f32[64,128]{1,0:T(8,128)S(1)}, f32[64,128]{1,0:T(8,128)S(1)}, u32[]{:S(2)}, u32[]{:S(2)}) collective-permute-start(f32[64,128]{1,0:T(8,128)S(1)} %get-tuple-element.68.field_ref), channel_id=1, source_target_pairs={{1,2},{3,4},{5,6},{7,8},{9,10},{11,12},{13,14},{15,16},{17,18},{19... | collective-permute-start | bytes 98312 | tf_op jit(solution)/shard_map/ppermute | solution.py:551
  138.7 9.5 %collective-permute-start.11 = (f32[64,128]{1,0:T(8,128)S(1)}, f32[64,128]{1,0:T(8,128)S(1)}, u32[]{:S(2)}, u32[]{:S(2)}) collective-permute-start(f32[64,128]{1,0:T(8,128)S(1)} %shard_map.107.field_ref), channel_id=1, source_target_pairs={{1,2},{3,4},{5,6},{7,8},{9,10},{11,12},{13,14},{15,16},{17,18},{19... | collective-permute-start | bytes 98312 | tf_op jit(solution)/shard_map/ppermute | solution.py:551
  157.8 8.0 %collective-permute-start.12 = (f32[10,8,128]{2,1,0:T(8,128)S(1)}, f32[10,8,128]{2,1,0:T(8,128)S(1)}, u32[]{:S(2)}, u32[]{:S(2)}) collective-permute-start(f32[10,8,128]{2,1,0:T(8,128)S(1)} %get-tuple-element.71), channel_id=1, source_target_pairs={{8,16},{24,32},{40,48},{56,64},{72,80},{88,96},{104,112},{120,128}... | collective-permute-start | bytes 122888 | tf_op jit(solution)/shard_map/ppermute | solution.py:602
  196.6 9.5 %collective-permute-start.13 = (f32[64,128]{1,0:T(8,128)S(1)}, f32[64,128]{1,0:T(8,128)S(1)}, u32[]{:S(2)}, u32[]{:S(2)}) collective-permute-start(f32[64,128]{1,0:T(8,128)S(1)} %get-tuple-element.75.field_ref), channel_id=1, source_target_pairs={{1,2},{3,4},{5,6},{7,8},{9,10},{11,12},{13,14},{15,16},{17,18},{19... | collective-permute-start | bytes 98312 | tf_op jit(solution)/shard_map/ppermute | solution.py:551
  (3 other events, 2.6 us)

commit v6 on v5

--- a/solution.py
+++ b/solution.py
@@ -199,15 +199,18 @@
             out[row + i * width : row + (i + 1) * width, 0 : part.shape[1]] = part
 
 
-def pack_prolong_body(where_ref, prolong_ref, targets_ref, section_ref, left_ref, right_ref, fine_ref, far_ref):
+def pack_prolong_body(where_ref, prolong_ref, targets_ref, fine_ref):
     modes, rows = prolong_ref.shape[1:3]
-    width, total = section_ref.shape[2:]
     for k in range(3):
         for m in range(modes):
             at = (k * modes + m) * rows
             fine_ref[at : at + rows, :] = prolong_ref[k, m].astype(F32)
         at = 3 * modes * rows + k
         fine_ref[at : at + 1, :] = targets_ref[k : k + 1, :].astype(F32)
+
+
+def pack_far_body(where_ref, section_ref, left_ref, right_ref, far_ref):
+    modes, width, total = section_ref.shape[1:]
     reach = far_ref.shape[1]
     cols = pl.ds(pl.multiple_of(where_ref[5] * (total - reach), LANES), reach)
     for k in range(3):
@@ -560,11 +563,10 @@
     inverse, start = call(first_body, [fine, fine], [VMEM] * 2)(fine_blocks, source)
 
     near = nearby(start)
-    pair, later = lax.optimization_barrier((near[0], where))
-    near = (pair, *near[1:])
     side = struct(3 * modes * SUB + SUB + width * pl.cdiv(coarsest_inverse.shape[1], halo), halo)
-    low, high = call(pack_body, [side, side], [SMEM] + [VMEM] * 3)(later, coarse_blocks, coarse_pattern, coarsest_inverse)
+    low, high = call(pack_body, [side, side], [SMEM] + [VMEM] * 3)(where, coarse_blocks, coarse_pattern, coarsest_inverse)
     left_data, right_data = beside(high, 1), beside(low, -1)
+    fine_pack = call(pack_prolong_body, [struct(3 * modes * rows + SUB, own)], [SMEM] + [VMEM] * 2)(where, prolong, prolong_pattern)[0]
     def step(body, outs, near, *rest):
         return call(body, outs, [SMEM] + [VMEM] * (5 + len(rest)), work)(where, *near, fine_blocks, fine_pattern, *rest)
 
@@ -586,13 +588,13 @@
             )(where, left_data, right_data, coarse_blocks, coarse_pattern)
         near = nearby(solution)
         if cycle == 0:
-            mine, later = lax.optimization_barrier((near[2], where))
+            mine, later, fine_pack = lax.optimization_barrier((near[2], where, fine_pack))
             near = (*near[:2], mine)
-            fine_pack, far = call(
-                pack_prolong_body,
-                [struct(3 * modes * rows + SUB, own), struct((3 * modes + pl.cdiv(slabs * width, FAR * LANES)) * width, FAR * LANES)],
-                [SMEM] + [VMEM] * 5,
-            )(later, prolong, prolong_pattern, section_prolong, left_data, right_data)
+            far = call(
+                pack_far_body,
+                [struct((3 * modes + pl.cdiv(slabs * width, FAR * LANES)) * width, FAR * LANES)],
+                [SMEM] + [VMEM] * 3,
+            )(later, section_prolong, left_data, right_data)[0]
             far_data = one_sided(far, 1)
             odd_prolong = lax.ppermute(fine_pack, both, odd_swap)
             even_prolong = lax.ppermute(fine_pack, both, even_swap)

time: 209 us -> 206 us (0.986)
  waiting for transfers between devices: 37.5 us -> 33 us
    ppermute x7, waiting for transfers between devices: 36 us -> 31.6 us  [nearby(): odd = lax.ppermute(field, both, odd_swap)]
    unnamed x26 -> x28, local copies, waits for them, and re-layouts: 4.57 us -> 5.27 us
where the time goes in v6:
time: 206 us; the launch traced here: 205 us
  blocking collectives  98.4 us (48%)
  starting transfers between devices  43 us (21%)
  waiting for transfers between devices  33 us (16%)
  Pallas kernels  24.6 us (12%)
  local copies, waits for them, and re-layouts  5.36 us (3%)
    all_to_all x2, blocking collectives, shards(): tops = lax.all_to_all(top, 'slab', 0, 0, tiled=True)  58.6 us
    ppermute x7, waiting for transfers between devices, nearby(): odd = lax.ppermute(field, both, odd_swap)  31.6 us
    ppermute x7, starting transfers between devices, nearby(): odd = lax.ppermute(field, both, odd_swap)  19.5 us
    all_to_all x2, blocking collectives, shards(): parts = lax.all_to_all(sums, 'sec', 0, 0, tiled=True)  16.7 us
    all_gather x7, blocking collectives, nearby(): pair = lax.all_gather(field, 'sec', axis_index_groups=pairs, axis=0)  13.7 us
    pallas_call x7, Pallas kernels, step(): call(body, outs, [SMEM] + [VMEM] * (5 + len(rest)), work)  9.7 us
    all_gather x2, blocking collectives, shards(): even = lax.all_gather(ends, 'slab', axis_index_groups=slab_pairs, axis=0)  9.36 us
    ppermute x2, starting transfers between devices, beside(): lax.ppermute(value, 'slab', [(i, i + step) for i in range(max(0, -step),...  7.95 us
  transfers between devices with their start and end apart: 14, of which 8 were waited for; matrix products, arithmetic and copies ran while one was open for 0% of the time, Pallas kernels for 4%

profile of v6, /device:TPU:32, one launch (start us, length us, event | category | flops | bytes accessed | tf_op | source)
XLA Modules:
  0.0 204.7 jit_solution(12129728773974840577)
XLA Ops:
  3.3 3.4 %collective-permute-start.1 = (f32[224,512]{1,0:T(8,128)S(1)}, f32[224,512]{1,0:T(8,128)S(1)}, u32[]{:S(2)}, u32[]{:S(2)}) collective-permute-start(f32[224,512]{1,0:T(8,128)S(1)} %get-tuple-element.40), channel_id=1, source_target_pairs={{0,8},{8,16},{16,24},{24,32},{32,40},{40,48},{48,56},{56,64},{64,7... | collective-permute-start | bytes 1376264 | tf_op jit(solution)/shard_map/ppermute | solution.py:559
  6.7 4.6 %collective-permute-start.2 = (f32[224,512]{1,0:T(8,128)S(1)}, f32[224,512]{1,0:T(8,128)S(1)}, u32[]{:S(2)}, u32[]{:S(2)}) collective-permute-start(f32[224,512]{1,0:T(8,128)S(1)} %get-tuple-element.41), channel_id=1, source_target_pairs={{8,0},{16,8},{24,16},{32,24},{40,32},{48,40},{56,48},{64,56},{72,6... | collective-permute-start | bytes 1376264 | tf_op jit(solution)/shard_map/ppermute | solution.py:559
  14.0 3.8 %collective-permute-start = (f32[64,128]{1,0:T(8,128)S(1)}, f32[64,128]{1,0:T(8,128)S(1)}, u32[]{:S(2)}, u32[]{:S(2)}) collective-permute-start(f32[64,128]{1,0:T(8,128)S(1)} %get-tuple-element.38.field_ref.change_ref), channel_id=1, source_target_pairs={{1,2},{3,4},{5,6},{7,8},{9,10},{11,12},{13,14},{15,16},{17,18},{19... | collective-permute-start | bytes 98312 | tf_op jit(solution)/shard_map/ppermute | solution.py:554
  20.6 3.1 %collective-permute-done.odd_ref = f32[64,128]{1,0:T(8,128)S(1)} collective-permute-done((f32[64,128]{1,0:T(8,128)S(1)}, f32[64,128]{1,0:T(8,128)S(1)}, u32[]{:S(2)}, u32[]{:S(2)}) %collective-permute-start) | collective-permute-done | bytes 32800 | tf_op jit(solution)/shard_map/ppermute | solution.py:554
  29.8 5.4 %collective-permute-start.6 = (f32[1160,128]{1,0:T(8,128)S(1)}, f32[1160,128]{1,0:T(8,128)S(1)}, u32[]{:S(2)}, u32[]{:S(2)}) collective-permute-start(f32[1160,128]{1,0:T(8,128)S(1)} %shard_map.96), channel_id=1, source_target_pairs={{1,2},{3,4},{5,6},{7,8},{9,10},{11,12},{13,14},{15,16},{17,18},{19... | collective-permute-start | bytes 1781768 | tf_op jit(solution)/shard_map/ppermute | solution.py:599
  35.2 4.3 %collective-permute-start.3 = (f32[64,128]{1,0:T(8,128)S(1)}, f32[64,128]{1,0:T(8,128)S(1)}, u32[]{:S(2)}, u32[]{:S(2)}) collective-permute-start(f32[64,128]{1,0:T(8,128)S(1)} %shard_map.93.field_ref), channel_id=1, source_target_pairs={{1,2},{3,4},{5,6},{7,8},{9,10},{11,12},{13,14},{15,16},{17,18},{19... | collective-permute-start | bytes 98312 | tf_op jit(solution)/shard_map/ppermute | solution.py:554
  41.4 4.2 %collective-permute-done.3.odd_ref = f32[64,128]{1,0:T(8,128)S(1)} collective-permute-done((f32[64,128]{1,0:T(8,128)S(1)}, f32[64,128]{1,0:T(8,128)S(1)}, u32[]{:S(2)}, u32[]{:S(2)}) %collective-permute-start.3) | collective-permute-done | bytes 32800 | tf_op jit(solution)/shard_map/ppermute | solution.py:554
  47.1 8.6 %all_to_all.32.parts_ref = f32[8,8,384]{2,1,0:T(8,128)S(1)} all-to-all(f32[8,8,384]{2,1,0:T(8,128)S(1)} %shard_map.97), channel_id=1, replica_groups=mesh['slab'=64,'sec'=8] {'sec'}, dimensions={0} | all-to-all | bytes 196608 | tf_op jit(solution)/shard_map/all_to_all | solution.py:602
  55.6 4.3 %collective-permute-start.4 = (f32[10,8,128]{2,1,0:T(8,128)S(1)}, f32[10,8,128]{2,1,0:T(8,128)S(1)}, u32[]{:S(2)}, u32[]{:S(2)}) collective-permute-start(f32[10,8,128]{2,1,0:T(8,128)S(1)} %get-tuple-element.45), channel_id=1, source_target_pairs={{8,16},{24,32},{40,48},{56,64},{72,80},{88,96},{104,112},{120,128}... | collective-permute-start | bytes 122888 | tf_op jit(solution)/shard_map/ppermute | solution.py:604
  60.7 4.7 %all-gather.2 = f32[20,8,128]{2,1,0:T(8,128)S(1)} all-gather(f32[10,8,128]{2,1,0:T(8,128)S(1)} %get-tuple-element.45), channel_id=4, replica_groups={{0,8},{16,24},{32,40},{48,56},{64,72},{80,88},{96,104},{112,120},{128,1..., dimensions={0}, use_global_device_ids=true | all-gather | bytes 122880 | tf_op jit(solution)/shard_map/all_gather | solution.py:605
  67.7 33.0 %all_to_all.33 = f32[64,1,128]{2,1,0:T(1,128)S(1)} all-to-all(f32[64,1,128]{2,1,0:T(1,128)S(1)} %bitcast.43), channel_id=1, replica_groups=mesh['slab'=64,'sec'=8] {'slab'}, dimensions={0} | all-to-all | bytes 65536 | tf_op jit(solution)/shard_map/all_to_all | solution.py:611
  100.7 2.8 %shard_map.102 = (f32[64,128]{1,0:T(8,128)S(1)}, f32[64,128]{1,0:T(8,128)S(1)}) custom-call(s32[7]{0:T(128)S(1)} %stack.35.where_ref, f32[64,128]{1,0:T(8,128)S(1)} %bitcast.42, f32[224,512]{1,0:T(8,128)S(1)} %collective-permute-done.1.left_ref, f32[24,1536]{1,0:T(8,128)S(1)} %copy-done.7, f32[224,512]{1,0:T(8,128)S(1)} %collective-permute-done.2.right_ref, ...), custom_call_target="tpu_custom_call" | custom-call | flops 1048576 | bytes 1048576 | tf_op jit(solution)/shard_map/pallas_call | solution.py:612
  108.0 5.0 %collective-permute-done.8.odd_ref = f32[64,128]{1,0:T(8,128)S(1)} collective-permute-done((f32[64,128]{1,0:T(8,128)S(1)}, f32[64,128]{1,0:T(8,128)S(1)}, u32[]{:S(2)}, u32[]{:S(2)}) %collective-permute-start.8) | collective-permute-done | bytes 32800 | tf_op jit(solution)/shard_map/ppermute | solution.py:554
  114.2 2.5 %collective-permute-start.9 = (f32[64,128]{1,0:T(8,128)S(1)}, f32[64,128]{1,0:T(8,128)S(1)}, u32[]{:S(2)}, u32[]{:S(2)}) collective-permute-start(f32[64,128]{1,0:T(8,128)S(1)} %shard_map.104.field_ref), channel_id=1, source_target_pairs={{1,2},{3,4},{5,6},{7,8},{9,10},{11,12},{13,14},{15,16},{17,18},{19... | collective-permute-start | bytes 98312 | tf_op jit(solution)/shard_map/ppermute | solution.py:554
  118.9 4.8 %collective-permute-done.9.odd_ref = f32[64,128]{1,0:T(8,128)S(1)} collective-permute-done((f32[64,128]{1,0:T(8,128)S(1)}, f32[64,128]{1,0:T(8,128)S(1)}, u32[]{:S(2)}, u32[]{:S(2)}) %collective-permute-start.9) | collective-permute-done | bytes 32800 | tf_op jit(solution)/shard_map/ppermute | solution.py:554
  124.9 2.5 %collective-permute-start.10 = (f32[64,128]{1,0:T(8,128)S(1)}, f32[64,128]{1,0:T(8,128)S(1)}, u32[]{:S(2)}, u32[]{:S(2)}) collective-permute-start(f32[64,128]{1,0:T(8,128)S(1)} %get-tuple-element.62.field_ref), channel_id=1, source_target_pairs={{1,2},{3,4},{5,6},{7,8},{9,10},{11,12},{13,14},{15,16},{17,18},{19... | collective-permute-start | bytes 98312 | tf_op jit(solution)/shard_map/ppermute | solution.py:554
  129.6 4.8 %collective-permute-done.10.odd_ref = f32[64,128]{1,0:T(8,128)S(1)} collective-permute-done((f32[64,128]{1,0:T(8,128)S(1)}, f32[64,128]{1,0:T(8,128)S(1)}, u32[]{:S(2)}, u32[]{:S(2)}) %collective-permute-start.10) | collective-permute-done | bytes 32800 | tf_op jit(solution)/shard_map/ppermute | solution.py:554
  135.6 2.5 %collective-permute-start.11 = (f32[64,128]{1,0:T(8,128)S(1)}, f32[64,128]{1,0:T(8,128)S(1)}, u32[]{:S(2)}, u32[]{:S(2)}) collective-permute-start(f32[64,128]{1,0:T(8,128)S(1)} %shard_map.108.field_ref), channel_id=1, source_target_pairs={{1,2},{3,4},{5,6},{7,8},{9,10},{11,12},{13,14},{15,16},{17,18},{19... | collective-permute-start | bytes 98312 | tf_op jit(solution)/shard_map/ppermute | solution.py:554
  140.3 4.8 %collective-permute-done.11.odd_ref = f32[64,128]{1,0:T(8,128)S(1)} collective-permute-done((f32[64,128]{1,0:T(8,128)S(1)}, f32[64,128]{1,0:T(8,128)S(1)}, u32[]{:S(2)}, u32[]{:S(2)}) %collective-permute-start.11) | collective-permute-done | bytes 32800 | tf_op jit(solution)/shard_map/ppermute | solution.py:554
  146.5 8.2 %all_to_all.34.parts_ref = f32[8,8,384]{2,1,0:T(8,128)S(1)} all-to-all(f32[8,8,384]{2,1,0:T(8,128)S(1)} %shard_map.110), channel_id=1, replica_groups=mesh['slab'=64,'sec'=8] {'sec'}, dimensions={0} | all-to-all | bytes 196608 | tf_op jit(solution)/shard_map/all_to_all | solution.py:602
  156.6 4.7 %all-gather.7 = f32[20,8,128]{2,1,0:T(8,128)S(1)} all-gather(f32[10,8,128]{2,1,0:T(8,128)S(1)} %get-tuple-element.65), channel_id=9, replica_groups={{0,8},{16,24},{32,40},{48,56},{64,72},{80,88},{96,104},{112,120},{128,1..., dimensions={0}, use_global_device_ids=true | all-gather | bytes 122880 | tf_op jit(solution)/shard_map/all_gather | solution.py:605
  164.9 25.7 %all_to_all.35 = f32[64,1,128]{2,1,0:T(1,128)S(1)} all-to-all(f32[64,1,128]{2,1,0:T(1,128)S(1)} %bitcast.44), channel_id=1, replica_groups=mesh['slab'=64,'sec'=8] {'slab'}, dimensions={0} | all-to-all | bytes 65536 | tf_op jit(solution)/shard_map/all_to_all | solution.py:611
  190.6 2.8 %shard_map.113 = (f32[64,128]{1,0:T(8,128)S(1)}, f32[64,128]{1,0:T(8,128)S(1)}) custom-call(s32[7]{0:T(128)S(1)} %stack.35.where_ref, f32[64,128]{1,0:T(8,128)S(1)} %bitcast.41, f32[224,512]{1,0:T(8,128)S(1)} %collective-permute-done.1.left_ref, f32[24,1536]{1,0:T(8,128)S(1)} %copy-done.7, f32[224,512]{1,0:T(8,128)S(1)} %collective-permute-done.2.right_ref, ...), custom_call_target="tpu_custom_call" | custom-call | flops 1048576 | bytes 1048576 | tf_op jit(solution)/shard_map/pallas_call | solution.py:612
  197.9 5.0 %collective-permute-done.13.odd_ref = f32[64,128]{1,0:T(8,128)S(1)} collective-permute-done((f32[64,128]{1,0:T(8,128)S(1)}, f32[64,128]{1,0:T(8,128)S(1)}, u32[]{:S(2)}, u32[]{:S(2)}) %collective-permute-start.13) | collective-permute-done | bytes 32800 | tf_op jit(solution)/shard_map/ppermute | solution.py:554
  (71 shorter events, 49.0 us)
Async XLA Ops:
  3.3 21.7 %collective-permute-start.1 = (f32[224,512]{1,0:T(8,128)S(1)}, f32[224,512]{1,0:T(8,128)S(1)}, u32[]{:S(2)}, u32[]{:S(2)}) collective-permute-start(f32[224,512]{1,0:T(8,128)S(1)} %get-tuple-element.40), channel_id=1, source_target_pairs={{0,8},{8,16},{16,24},{24,32},{32,40},{40,48},{48,56},{56,64},{64,7... | collective-permute-start | bytes 1376264 | tf_op jit(solution)/shard_map/ppermute | solution.py:559
  6.7 18.3 %collective-permute-start.2 = (f32[224,512]{1,0:T(8,128)S(1)}, f32[224,512]{1,0:T(8,128)S(1)}, u32[]{:S(2)}, u32[]{:S(2)}) collective-permute-start(f32[224,512]{1,0:T(8,128)S(1)} %get-tuple-element.41), channel_id=1, source_target_pairs={{8,0},{16,8},{24,16},{32,24},{40,32},{48,40},{56,48},{64,56},{72,6... | collective-permute-start | bytes 1376264 | tf_op jit(solution)/shard_map/ppermute | solution.py:559
  11.3 1.9 copy-start
  13.9 4.2 %copy-start.3 = (bf16[3,64,6,128]{3,1,2,0:T(8,128)(2,1)S(1)}, bf16[3,64,6,128]{3,1,2,0:T(8,128)(2,1)}, u32[]{:S(2)}) copy-start(bf16[3,64,6,128]{3,1,2,0:T(8,128)(2,1)} %param.12) | copy-start | bytes 884740
  13.9 4.2 %copy-start.13 = (s32[3,128]{1,0:T(4,128)S(1)}, s32[3,128]{1,0:T(4,128)}, u32[]{:S(2)}) copy-start(s32[3,128]{1,0:T(4,128)} %targets_ref.9) | copy-start | bytes 4612
  13.9 9.8 %copy-start.1 = (bf16[3,64,64,128]{3,2,1,0:T(8,128)(2,1)S(1)}, bf16[3,64,64,128]{3,2,1,0:T(8,128)(2,1)}, u32[]{:S(2)}) copy-start(bf16[3,64,64,128]{3,2,1,0:T(8,128)(2,1)} %matrix_ref.29) | copy-start | bytes 9437188
  13.9 9.8 %copy-start.5 = (f32[64,128]{1,0:T(8,128)S(1)}, f32[64,128]{1,0:T(8,128)}, u32[]{:S(2)}) copy-start(f32[64,128]{1,0:T(8,128)} %source_ref.19) | copy-start | bytes 98308
  13.9 9.8 %copy-start.10 = (s32[3,128]{1,0:T(4,128)S(1)}, s32[3,128]{1,0:T(4,128)}, u32[]{:S(2)}) copy-start(s32[3,128]{1,0:T(4,128)} %pattern_ref.17) | copy-start | bytes 4612
  14.0 9.7 %collective-permute-start = (f32[64,128]{1,0:T(8,128)S(1)}, f32[64,128]{1,0:T(8,128)S(1)}, u32[]{:S(2)}, u32[]{:S(2)}) collective-permute-start(f32[64,128]{1,0:T(8,128)S(1)} %get-tuple-element.38.field_ref.change_ref), channel_id=1, source_target_pairs={{1,2},{3,4},{5,6},{7,8},{9,10},{11,12},{13,14},{15,16},{17,18},{19... | collective-permute-start | bytes 98312 | tf_op jit(solution)/shard_map/ppermute | solution.py:554
  23.7 1.6 copy-start.2
  25.3 34.7 %copy-start.9 = (bf16[3,6,6,1024]{3,2,1,0:T(8,128)(2,1)S(1)}, bf16[3,6,6,1024]{3,2,1,0:T(8,128)(2,1)}, u32[]{:S(2)}) copy-start(bf16[3,6,6,1024]{3,2,1,0:T(8,128)(2,1)} %blocks_ref.3) | copy-start | bytes 663556
  25.3 34.7 %copy-start.12 = (s32[3,1024]{1,0:T(4,128)S(1)}, s32[3,1024]{1,0:T(4,128)}, u32[]{:S(2)}) copy-start(s32[3,1024]{1,0:T(4,128)} %pattern_ref.12) | copy-start | bytes 36868
  25.9 41.8 %collective-permute-start.5 = (f32[528,384]{1,0:T(8,128)S(1)}, f32[528,384]{1,0:T(8,128)S(1)}, u32[]{:S(2)}, u32[]{:S(2)}) collective-permute-start(f32[528,384]{1,0:T(8,128)S(1)} %shard_map.101), channel_id=1, source_target_pairs={{0,8},{1,9},{2,10},{8,16},{9,17},{10,18},{16,24},{17,25},{18,26},{... | collective-permute-start | bytes 2433032 | tf_op jit(solution)/shard_map/ppermute | solution.py:548
  27.9 39.8 %collective-permute-start.7 = (f32[1160,128]{1,0:T(8,128)S(1)}, f32[1160,128]{1,0:T(8,128)S(1)}, u32[]{:S(2)}, u32[]{:S(2)}) collective-permute-start(f32[1160,128]{1,0:T(8,128)S(1)} %shard_map.96), channel_id=1, source_target_pairs={{0,1},{1,0},{2,3},{3,2},{4,5},{5,4},{6,7},{7,6},{8,9},{9,8},{10,11... | collective-permute-start | bytes 1781768 | tf_op jit(solution)/shard_map/ppermute | solution.py:600
  29.8 37.9 %collective-permute-start.6 = (f32[1160,128]{1,0:T(8,128)S(1)}, f32[1160,128]{1,0:T(8,128)S(1)}, u32[]{:S(2)}, u32[]{:S(2)}) collective-permute-start(f32[1160,128]{1,0:T(8,128)S(1)} %shard_map.96), channel_id=1, source_target_pairs={{1,2},{3,4},{5,6},{7,8},{9,10},{11,12},{13,14},{15,16},{17,18},{19... | collective-permute-start | bytes 1781768 | tf_op jit(solution)/shard_map/ppermute | solution.py:599
  35.2 10.4 %collective-permute-start.3 = (f32[64,128]{1,0:T(8,128)S(1)}, f32[64,128]{1,0:T(8,128)S(1)}, u32[]{:S(2)}, u32[]{:S(2)}) collective-permute-start(f32[64,128]{1,0:T(8,128)S(1)} %shard_map.93.field_ref), channel_id=1, source_target_pairs={{1,2},{3,4},{5,6},{7,8},{9,10},{11,12},{13,14},{15,16},{17,18},{19... | collective-permute-start | bytes 98312 | tf_op jit(solution)/shard_map/ppermute | solution.py:554
  45.6 55.1 %copy-start.7 = (f32[24,1536]{1,0:T(8,128)S(1)}, f32[24,1536]{1,0:T(8,128)}, u32[]{:S(2)}) copy-start(f32[24,1536]{1,0:T(8,128)} %top_inverse_ref.3) | copy-start | bytes 442372
  55.6 9.8 %collective-permute-start.4 = (f32[10,8,128]{2,1,0:T(8,128)S(1)}, f32[10,8,128]{2,1,0:T(8,128)S(1)}, u32[]{:S(2)}, u32[]{:S(2)}) collective-permute-start(f32[10,8,128]{2,1,0:T(8,128)S(1)} %get-tuple-element.45), channel_id=1, source_target_pairs={{8,16},{24,32},{40,48},{56,64},{72,80},{88,96},{104,112},{120,128}... | collective-permute-start | bytes 122888 | tf_op jit(solution)/shard_map/ppermute | solution.py:604
  103.5 9.5 %collective-permute-start.8 = (f32[64,128]{1,0:T(8,128)S(1)}, f32[64,128]{1,0:T(8,128)S(1)}, u32[]{:S(2)}, u32[]{:S(2)}) collective-permute-start(f32[64,128]{1,0:T(8,128)S(1)} %get-tuple-element.60.field_ref), channel_id=1, source_target_pairs={{1,2},{3,4},{5,6},{7,8},{9,10},{11,12},{13,14},{15,16},{17,18},{19... | collective-permute-start | bytes 98312 | tf_op jit(solution)/shard_map/ppermute | solution.py:554
  114.2 9.5 %collective-permute-start.9 = (f32[64,128]{1,0:T(8,128)S(1)}, f32[64,128]{1,0:T(8,128)S(1)}, u32[]{:S(2)}, u32[]{:S(2)}) collective-permute-start(f32[64,128]{1,0:T(8,128)S(1)} %shard_map.104.field_ref), channel_id=1, source_target_pairs={{1,2},{3,4},{5,6},{7,8},{9,10},{11,12},{13,14},{15,16},{17,18},{19... | collective-permute-start | bytes 98312 | tf_op jit(solution)/shard_map/ppermute | solution.py:554
  124.9 9.5 %collective-permute-start.10 = (f32[64,128]{1,0:T(8,128)S(1)}, f32[64,128]{1,0:T(8,128)S(1)}, u32[]{:S(2)}, u32[]{:S(2)}) collective-permute-start(f32[64,128]{1,0:T(8,128)S(1)} %get-tuple-element.62.field_ref), channel_id=1, source_target_pairs={{1,2},{3,4},{5,6},{7,8},{9,10},{11,12},{13,14},{15,16},{17,18},{19... | collective-permute-start | bytes 98312 | tf_op jit(solution)/shard_map/ppermute | solution.py:554
  135.6 9.5 %collective-permute-start.11 = (f32[64,128]{1,0:T(8,128)S(1)}, f32[64,128]{1,0:T(8,128)S(1)}, u32[]{:S(2)}, u32[]{:S(2)}) collective-permute-start(f32[64,128]{1,0:T(8,128)S(1)} %shard_map.108.field_ref), channel_id=1, source_target_pairs={{1,2},{3,4},{5,6},{7,8},{9,10},{11,12},{13,14},{15,16},{17,18},{19... | collective-permute-start | bytes 98312 | tf_op jit(solution)/shard_map/ppermute | solution.py:554
  154.7 8.0 %collective-permute-start.12 = (f32[10,8,128]{2,1,0:T(8,128)S(1)}, f32[10,8,128]{2,1,0:T(8,128)S(1)}, u32[]{:S(2)}, u32[]{:S(2)}) collective-permute-start(f32[10,8,128]{2,1,0:T(8,128)S(1)} %get-tuple-element.65), channel_id=1, source_target_pairs={{8,16},{24,32},{40,48},{56,64},{72,80},{88,96},{104,112},{120,128}... | collective-permute-start | bytes 122888 | tf_op jit(solution)/shard_map/ppermute | solution.py:604
  193.4 9.5 %collective-permute-start.13 = (f32[64,128]{1,0:T(8,128)S(1)}, f32[64,128]{1,0:T(8,128)S(1)}, u32[]{:S(2)}, u32[]{:S(2)}) collective-permute-start(f32[64,128]{1,0:T(8,128)S(1)} %get-tuple-element.69.field_ref), channel_id=1, source_target_pairs={{1,2},{3,4},{5,6},{7,8},{9,10},{11,12},{13,14},{15,16},{17,18},{19... | collective-permute-start | bytes 98312 | tf_op jit(solution)/shard_map/ppermute | solution.py:554
  (4 other events, 3.3 us)

commit v7 on v6

--- a/solution.py
+++ b/solution.py
@@ -135,24 +135,45 @@
         field_ref[part, :] = inverse * source_ref[part, :]
 
 
-def field_body(where_ref, pair_ref, odd_ref, own_ref, matrix_ref, pattern_ref, source_ref, inverse_ref, change_ref, field_ref, ext, picked, out):
-    load_halo(where_ref, pair_ref, odd_ref, ext)
-    fine_product(where_ref, matrix_ref, pattern_ref, ext, picked, out, own_ref)
+def pick_body(where_ref, pair_ref, pattern_ref, picked_ref):
+    parity = where_ref[0]
+    for k in (1, 2):
+        target = pattern_ref[k : k + 1, :] - where_ref[1]
+        lane = jnp.broadcast_to(target & (LANES - 1), (SUB, LANES))
+        block = jnp.broadcast_to((target + LANES) >> 7, (SUB, LANES))
+        for t in range(picked_ref.shape[1] // SUB):
+            part = pl.ds(t * SUB, SUB)
+            mine, other = take(pair_ref[parity, part, :], lane), take(pair_ref[1 - parity, part, :], lane)
+            picked_ref[k - 1, part, :] = jnp.where(block == 1, mine, other)
+
+
+def finish_product(where_ref, matrix_ref, pattern_ref, odd_ref, near_ref, own_ref, picked, out):
+    odd = 2 * where_ref[0]
+    for k in (1, 2):
+        target = pattern_ref[k : k + 1, :] - where_ref[1]
+        lane = jnp.broadcast_to(target & (LANES - 1), (SUB, LANES))
+        block = jnp.broadcast_to((target + LANES) >> 7, (SUB, LANES))
+        for t in range(out.shape[0] // SUB):
+            part = pl.ds(t * SUB, SUB)
+            picked[k - 1, part, :] = jnp.where(block == odd, take(odd_ref[part, :], lane), near_ref[k - 1, part, :])
+    product_rows(matrix_ref, (1, 2), {1: picked.at[0], 2: picked.at[1]}, out, own_ref)
+
+
+def field_body(where_ref, pair_ref, odd_ref, own_ref, near_ref, matrix_ref, pattern_ref, source_ref, inverse_ref, change_ref, field_ref, picked, out):
+    finish_product(where_ref, matrix_ref, pattern_ref, odd_ref, near_ref, own_ref, picked, out)
     change = inverse_ref[...] * (source_ref[...] - out[...])
     change_ref[...] = change
-    field_ref[...] = ext[1] + change
-
-
-def solution_body(where_ref, pair_ref, odd_ref, own_ref, matrix_ref, pattern_ref, source_ref, inverse_ref, change_ref, field_ref, ext, picked, out):
-    load_halo(where_ref, pair_ref, odd_ref, ext)
-    fine_product(where_ref, matrix_ref, pattern_ref, ext, picked, out, own_ref)
+    field_ref[...] = pair_ref[where_ref[0]] + change
+
+
+def solution_body(where_ref, pair_ref, odd_ref, own_ref, near_ref, matrix_ref, pattern_ref, source_ref, inverse_ref, change_ref, field_ref, picked, out):
+    finish_product(where_ref, matrix_ref, pattern_ref, odd_ref, near_ref, own_ref, picked, out)
     second = KEEP * change_ref[...] + FRESH * inverse_ref[...] * (source_ref[...] - out[...])
-    field_ref[...] = ext[1] + second
-
-
-def restrict_body(where_ref, pair_ref, odd_ref, own_ref, matrix_ref, pattern_ref, source_ref, prolong_ref, targets_ref, sums_ref, ext, picked, out):
-    load_halo(where_ref, pair_ref, odd_ref, ext)
-    fine_product(where_ref, matrix_ref, pattern_ref, ext, picked, out, own_ref)
+    field_ref[...] = pair_ref[where_ref[0]] + second
+
+
+def restrict_body(where_ref, pair_ref, odd_ref, own_ref, near_ref, matrix_ref, pattern_ref, source_ref, prolong_ref, targets_ref, sums_ref, picked, out):
+    finish_product(where_ref, matrix_ref, pattern_ref, odd_ref, near_ref, own_ref, picked, out)
     residual = source_ref[...] - out[...]
     modes = prolong_ref.shape[1]
     rows = residual.shape[0]
@@ -553,7 +574,8 @@
     def nearby(field):
         odd = lax.ppermute(field, both, odd_swap)
         pair = lax.all_gather(field, "sec", axis_index_groups=pairs, axis=0)
-        return pair, odd, call(own_body, [fine], [VMEM] * 2)(fine_blocks, field)[0]
+        picked = call(pick_body, [struct(2, rows, own)], [SMEM] + [VMEM] * 2)(where, pair, fine_pattern)[0]
+        return pair, odd, call(own_body, [fine], [VMEM] * 2)(fine_blocks, field)[0], picked
 
     def beside(value, step):
         return lax.ppermute(value, "slab", [(i, i + step) for i in range(max(0, -step), min(slabs, slabs - step))])
@@ -568,7 +590,7 @@
     left_data, right_data = beside(high, 1), beside(low, -1)
     fine_pack = call(pack_prolong_body, [struct(3 * modes * rows + SUB, own)], [SMEM] + [VMEM] * 2)(where, prolong, prolong_pattern)[0]
     def step(body, outs, near, *rest):
-        return call(body, outs, [SMEM] + [VMEM] * (5 + len(rest)), work)(where, *near, fine_blocks, fine_pattern, *rest)
+        return call(body, outs, [SMEM] + [VMEM] * (6 + len(rest)), work[1:])(where, *near, fine_blocks, fine_pattern, *rest)
 
     coarse = struct(blocks, SUB, LANES)
     line = pltpu.VMEM((blocks + 2, SUB, LANES), F32)
@@ -589,7 +611,7 @@
         near = nearby(solution)
         if cycle == 0:
             mine, later, fine_pack = lax.optimization_barrier((near[2], where, fine_pack))
-            near = (*near[:2], mine)
+            near = (*near[:2], mine, near[3])
             far = call(
                 pack_far_body,
                 [struct((3 * modes + pl.cdiv(slabs * width, FAR * LANES)) * width, FAR * LANES)],

time: 206 us -> 205 us (level)
  waiting for transfers between devices: 33 us -> 25.9 us
  Pallas kernels: 24.6 us -> 28.9 us
  starting transfers between devices: 43 us -> 45.5 us
    ppermute x7, waiting for transfers between devices: 31.6 us -> 25 us  [nearby(): odd = lax.ppermute(field, both, odd_swap)]
    pallas_call x7 -> x14, Pallas kernels: 9.7 us -> 13.9 us  [the longest x7 9.42 us: step(): call(body, outs, [SMEM] + [VMEM] * (6 + len(rest)), work[1:])]
  transfers between devices with their start and end apart: 14 -> 14, of which waited for: 8 -> 8; matrix products, arithmetic and copies ran while one was open for 0% -> 0% of each run, Pallas kernels for 4% -> 6%
where the time goes in v7:
time: 205 us; the launch traced here: 204 us
  blocking collectives  98.4 us (48%)
  starting transfers between devices  45.5 us (22%)
  Pallas kernels  28.9 us (14%)
  waiting for transfers between devices  25.9 us (13%)
  local copies, waits for them, and re-layouts  5.36 us (3%)
    all_to_all x2, blocking collectives, shards(): tops = lax.all_to_all(top, 'slab', 0, 0, tiled=True)  58.6 us
    ppermute x7, waiting for transfers between devices, nearby(): odd = lax.ppermute(field, both, odd_swap)  25 us
    ppermute x7, starting transfers between devices, nearby(): odd = lax.ppermute(field, both, odd_swap)  21.5 us
    all_to_all x2, blocking collectives, shards(): parts = lax.all_to_all(sums, 'sec', 0, 0, tiled=True)  16.7 us
    all_gather x7, blocking collectives, nearby(): pair = lax.all_gather(field, 'sec', axis_index_groups=pairs, axis=0)  13.7 us
    pallas_call x7, Pallas kernels, step(): call(body, outs, [SMEM] + [VMEM] * (6 + len(rest)), work[1:])  9.42 us
    all_gather x2, blocking collectives, shards(): even = lax.all_gather(ends, 'slab', axis_index_groups=slab_pairs, axis=0)  9.36 us
    ppermute x2, starting transfers between devices, beside(): lax.ppermute(value, 'slab', [(i, i + step) for i in range(max(0, -step),...  7.95 us
  transfers between devices with their start and end apart: 14, of which 8 were waited for; matrix products, arithmetic and copies ran while one was open for 0% of the time, Pallas kernels for 6%

profile of v7, /device:TPU:32, one launch (start us, length us, event | category | flops | bytes accessed | tf_op | source)
XLA Modules:
  0.0 204.4 jit_solution(17851774495773502764)
XLA Ops:
  3.3 3.4 %collective-permute-start.1 = (f32[224,512]{1,0:T(8,128)S(1)}, f32[224,512]{1,0:T(8,128)S(1)}, u32[]{:S(2)}, u32[]{:S(2)}) collective-permute-start(f32[224,512]{1,0:T(8,128)S(1)} %get-tuple-element.40), channel_id=1, source_target_pairs={{0,8},{8,16},{16,24},{24,32},{32,40},{40,48},{48,56},{56,64},{64,7... | collective-permute-start | bytes 1376264 | tf_op jit(solution)/shard_map/ppermute | solution.py:581
  6.7 4.6 %collective-permute-start.2 = (f32[224,512]{1,0:T(8,128)S(1)}, f32[224,512]{1,0:T(8,128)S(1)}, u32[]{:S(2)}, u32[]{:S(2)}) collective-permute-start(f32[224,512]{1,0:T(8,128)S(1)} %get-tuple-element.41), channel_id=1, source_target_pairs={{8,0},{16,8},{24,16},{32,24},{40,32},{48,40},{56,48},{64,56},{72,6... | collective-permute-start | bytes 1376264 | tf_op jit(solution)/shard_map/ppermute | solution.py:581
  14.0 3.8 %collective-permute-start = (f32[64,128]{1,0:T(8,128)S(1)}, f32[64,128]{1,0:T(8,128)S(1)}, u32[]{:S(2)}, u32[]{:S(2)}) collective-permute-start(f32[64,128]{1,0:T(8,128)S(1)} %get-tuple-element.38.field_ref.change_ref), channel_id=1, source_target_pairs={{1,2},{3,4},{5,6},{7,8},{9,10},{11,12},{13,14},{15,16},{17,18},{19... | collective-permute-start | bytes 98312 | tf_op jit(solution)/shard_map/ppermute | solution.py:575
  29.7 5.4 %collective-permute-start.6 = (f32[1160,128]{1,0:T(8,128)S(1)}, f32[1160,128]{1,0:T(8,128)S(1)}, u32[]{:S(2)}, u32[]{:S(2)}) collective-permute-start(f32[1160,128]{1,0:T(8,128)S(1)} %shard_map.97), channel_id=1, source_target_pairs={{1,2},{3,4},{5,6},{7,8},{9,10},{11,12},{13,14},{15,16},{17,18},{19... | collective-permute-start | bytes 1781768 | tf_op jit(solution)/shard_map/ppermute | solution.py:621
  35.2 4.3 %collective-permute-start.3 = (f32[64,128]{1,0:T(8,128)S(1)}, f32[64,128]{1,0:T(8,128)S(1)}, u32[]{:S(2)}, u32[]{:S(2)}) collective-permute-start(f32[64,128]{1,0:T(8,128)S(1)} %shard_map.94.field_ref), channel_id=1, source_target_pairs={{1,2},{3,4},{5,6},{7,8},{9,10},{11,12},{13,14},{15,16},{17,18},{19... | collective-permute-start | bytes 98312 | tf_op jit(solution)/shard_map/ppermute | solution.py:575
  42.0 3.5 %collective-permute-done.3.odd_ref = f32[64,128]{1,0:T(8,128)S(1)} collective-permute-done((f32[64,128]{1,0:T(8,128)S(1)}, f32[64,128]{1,0:T(8,128)S(1)}, u32[]{:S(2)}, u32[]{:S(2)}) %collective-permute-start.3) | collective-permute-done | bytes 32800 | tf_op jit(solution)/shard_map/ppermute | solution.py:575
  47.0 8.6 %all_to_all.32.parts_ref = f32[8,8,384]{2,1,0:T(8,128)S(1)} all-to-all(f32[8,8,384]{2,1,0:T(8,128)S(1)} %shard_map.99), channel_id=1, replica_groups=mesh['slab'=64,'sec'=8] {'sec'}, dimensions={0} | all-to-all | bytes 196608 | tf_op jit(solution)/shard_map/all_to_all | solution.py:624
  55.5 4.3 %collective-permute-start.4 = (f32[10,8,128]{2,1,0:T(8,128)S(1)}, f32[10,8,128]{2,1,0:T(8,128)S(1)}, u32[]{:S(2)}, u32[]{:S(2)}) collective-permute-start(f32[10,8,128]{2,1,0:T(8,128)S(1)} %get-tuple-element.45), channel_id=1, source_target_pairs={{8,16},{24,32},{40,48},{56,64},{72,80},{88,96},{104,112},{120,128}... | collective-permute-start | bytes 122888 | tf_op jit(solution)/shard_map/ppermute | solution.py:626
  60.7 4.7 %all-gather.2 = f32[20,8,128]{2,1,0:T(8,128)S(1)} all-gather(f32[10,8,128]{2,1,0:T(8,128)S(1)} %get-tuple-element.45), channel_id=4, replica_groups={{0,8},{16,24},{32,40},{48,56},{64,72},{80,88},{96,104},{112,120},{128,1..., dimensions={0}, use_global_device_ids=true | all-gather | bytes 122880 | tf_op jit(solution)/shard_map/all_gather | solution.py:627
  67.6 33.0 %all_to_all.33 = f32[64,1,128]{2,1,0:T(1,128)S(1)} all-to-all(f32[64,1,128]{2,1,0:T(1,128)S(1)} %bitcast.50), channel_id=1, replica_groups=mesh['slab'=64,'sec'=8] {'slab'}, dimensions={0} | all-to-all | bytes 65536 | tf_op jit(solution)/shard_map/all_to_all | solution.py:633
  100.6 2.8 %shard_map.104 = (f32[64,128]{1,0:T(8,128)S(1)}, f32[64,128]{1,0:T(8,128)S(1)}) custom-call(s32[7]{0:T(128)S(1)} %stack.35.where_ref, f32[64,128]{1,0:T(8,128)S(1)} %bitcast.49, f32[224,512]{1,0:T(8,128)S(1)} %collective-permute-done.1.left_ref, f32[24,1536]{1,0:T(8,128)S(1)} %copy-done.7, f32[224,512]{1,0:T(8,128)S(1)} %collective-permute-done.2.right_ref, ...), custom_call_target="tpu_custom_call" | custom-call | flops 1048576 | bytes 1048576 | tf_op jit(solution)/shard_map/pallas_call | solution.py:634
  108.5 4.3 %collective-permute-done.8.odd_ref = f32[64,128]{1,0:T(8,128)S(1)} collective-permute-done((f32[64,128]{1,0:T(8,128)S(1)}, f32[64,128]{1,0:T(8,128)S(1)}, u32[]{:S(2)}, u32[]{:S(2)}) %collective-permute-start.8) | collective-permute-done | bytes 32800 | tf_op jit(solution)/shard_map/ppermute | solution.py:575
  114.1 3.2 %collective-permute-start.9 = (f32[64,128]{1,0:T(8,128)S(1)}, f32[64,128]{1,0:T(8,128)S(1)}, u32[]{:S(2)}, u32[]{:S(2)}) collective-permute-start(f32[64,128]{1,0:T(8,128)S(1)} %shard_map.107.field_ref), channel_id=1, source_target_pairs={{1,2},{3,4},{5,6},{7,8},{9,10},{11,12},{13,14},{15,16},{17,18},{19... | collective-permute-start | bytes 98312 | tf_op jit(solution)/shard_map/ppermute | solution.py:575
  120.1 3.4 %collective-permute-done.9.odd_ref = f32[64,128]{1,0:T(8,128)S(1)} collective-permute-done((f32[64,128]{1,0:T(8,128)S(1)}, f32[64,128]{1,0:T(8,128)S(1)}, u32[]{:S(2)}, u32[]{:S(2)}) %collective-permute-start.9) | collective-permute-done | bytes 32800 | tf_op jit(solution)/shard_map/ppermute | solution.py:575
  124.7 3.2 %collective-permute-start.10 = (f32[64,128]{1,0:T(8,128)S(1)}, f32[64,128]{1,0:T(8,128)S(1)}, u32[]{:S(2)}, u32[]{:S(2)}) collective-permute-start(f32[64,128]{1,0:T(8,128)S(1)} %get-tuple-element.62.field_ref), channel_id=1, source_target_pairs={{1,2},{3,4},{5,6},{7,8},{9,10},{11,12},{13,14},{15,16},{17,18},{19... | collective-permute-start | bytes 98312 | tf_op jit(solution)/shard_map/ppermute | solution.py:575
  130.7 3.4 %collective-permute-done.10.odd_ref = f32[64,128]{1,0:T(8,128)S(1)} collective-permute-done((f32[64,128]{1,0:T(8,128)S(1)}, f32[64,128]{1,0:T(8,128)S(1)}, u32[]{:S(2)}, u32[]{:S(2)}) %collective-permute-start.10) | collective-permute-done | bytes 32800 | tf_op jit(solution)/shard_map/ppermute | solution.py:575
  135.4 3.2 %collective-permute-start.11 = (f32[64,128]{1,0:T(8,128)S(1)}, f32[64,128]{1,0:T(8,128)S(1)}, u32[]{:S(2)}, u32[]{:S(2)}) collective-permute-start(f32[64,128]{1,0:T(8,128)S(1)} %shard_map.113.field_ref), channel_id=1, source_target_pairs={{1,2},{3,4},{5,6},{7,8},{9,10},{11,12},{13,14},{15,16},{17,18},{19... | collective-permute-start | bytes 98312 | tf_op jit(solution)/shard_map/ppermute | solution.py:575
  141.4 3.4 %collective-permute-done.11.odd_ref = f32[64,128]{1,0:T(8,128)S(1)} collective-permute-done((f32[64,128]{1,0:T(8,128)S(1)}, f32[64,128]{1,0:T(8,128)S(1)}, u32[]{:S(2)}, u32[]{:S(2)}) %collective-permute-start.11) | collective-permute-done | bytes 32800 | tf_op jit(solution)/shard_map/ppermute | solution.py:575
  146.2 8.2 %all_to_all.34.parts_ref = f32[8,8,384]{2,1,0:T(8,128)S(1)} all-to-all(f32[8,8,384]{2,1,0:T(8,128)S(1)} %shard_map.116), channel_id=1, replica_groups=mesh['slab'=64,'sec'=8] {'sec'}, dimensions={0} | all-to-all | bytes 196608 | tf_op jit(solution)/shard_map/all_to_all | solution.py:624
  154.4 2.5 %collective-permute-start.12 = (f32[10,8,128]{2,1,0:T(8,128)S(1)}, f32[10,8,128]{2,1,0:T(8,128)S(1)}, u32[]{:S(2)}, u32[]{:S(2)}) collective-permute-start(f32[10,8,128]{2,1,0:T(8,128)S(1)} %get-tuple-element.65), channel_id=1, source_target_pairs={{8,16},{24,32},{40,48},{56,64},{72,80},{88,96},{104,112},{120,128}... | collective-permute-start | bytes 122888 | tf_op jit(solution)/shard_map/ppermute | solution.py:626
  156.9 4.7 %all-gather.7 = f32[20,8,128]{2,1,0:T(8,128)S(1)} all-gather(f32[10,8,128]{2,1,0:T(8,128)S(1)} %get-tuple-element.65), channel_id=9, replica_groups={{0,8},{16,24},{32,40},{48,56},{64,72},{80,88},{96,104},{112,120},{128,1..., dimensions={0}, use_global_device_ids=true | all-gather | bytes 122880 | tf_op jit(solution)/shard_map/all_gather | solution.py:627
  164.7 25.7 %all_to_all.35 = f32[64,1,128]{2,1,0:T(1,128)S(1)} all-to-all(f32[64,1,128]{2,1,0:T(1,128)S(1)} %bitcast.51), channel_id=1, replica_groups=mesh['slab'=64,'sec'=8] {'slab'}, dimensions={0} | all-to-all | bytes 65536 | tf_op jit(solution)/shard_map/all_to_all | solution.py:633
  190.3 2.8 %shard_map.119 = (f32[64,128]{1,0:T(8,128)S(1)}, f32[64,128]{1,0:T(8,128)S(1)}) custom-call(s32[7]{0:T(128)S(1)} %stack.35.where_ref, f32[64,128]{1,0:T(8,128)S(1)} %bitcast.48, f32[224,512]{1,0:T(8,128)S(1)} %collective-permute-done.1.left_ref, f32[24,1536]{1,0:T(8,128)S(1)} %copy-done.7, f32[224,512]{1,0:T(8,128)S(1)} %collective-permute-done.2.right_ref, ...), custom_call_target="tpu_custom_call" | custom-call | flops 1048576 | bytes 1048576 | tf_op jit(solution)/shard_map/pallas_call | solution.py:634
  198.3 4.3 %collective-permute-done.13.odd_ref = f32[64,128]{1,0:T(8,128)S(1)} collective-permute-done((f32[64,128]{1,0:T(8,128)S(1)}, f32[64,128]{1,0:T(8,128)S(1)}, u32[]{:S(2)}, u32[]{:S(2)}) %collective-permute-start.13) | collective-permute-done | bytes 32800 | tf_op jit(solution)/shard_map/ppermute | solution.py:575
  (78 shorter events, 53.3 us)
Async XLA Ops:
  3.3 21.6 %collective-permute-start.1 = (f32[224,512]{1,0:T(8,128)S(1)}, f32[224,512]{1,0:T(8,128)S(1)}, u32[]{:S(2)}, u32[]{:S(2)}) collective-permute-start(f32[224,512]{1,0:T(8,128)S(1)} %get-tuple-element.40), channel_id=1, source_target_pairs={{0,8},{8,16},{16,24},{24,32},{32,40},{40,48},{48,56},{56,64},{64,7... | collective-permute-start | bytes 1376264 | tf_op jit(solution)/shard_map/ppermute | solution.py:581
  6.7 18.2 %collective-permute-start.2 = (f32[224,512]{1,0:T(8,128)S(1)}, f32[224,512]{1,0:T(8,128)S(1)}, u32[]{:S(2)}, u32[]{:S(2)}) collective-permute-start(f32[224,512]{1,0:T(8,128)S(1)} %get-tuple-element.41), channel_id=1, source_target_pairs={{8,0},{16,8},{24,16},{32,24},{40,32},{48,40},{56,48},{64,56},{72,6... | collective-permute-start | bytes 1376264 | tf_op jit(solution)/shard_map/ppermute | solution.py:581
  11.3 1.9 copy-start
  13.9 6.0 %copy-start.10 = (s32[3,128]{1,0:T(4,128)S(1)}, s32[3,128]{1,0:T(4,128)}, u32[]{:S(2)}) copy-start(s32[3,128]{1,0:T(4,128)} %pattern_ref.31) | copy-start | bytes 4612
  13.9 6.7 %copy-start.3 = (bf16[3,64,6,128]{3,1,2,0:T(8,128)(2,1)S(1)}, bf16[3,64,6,128]{3,1,2,0:T(8,128)(2,1)}, u32[]{:S(2)}) copy-start(bf16[3,64,6,128]{3,1,2,0:T(8,128)(2,1)} %param.12) | copy-start | bytes 884740
  13.9 6.7 %copy-start.13 = (s32[3,128]{1,0:T(4,128)S(1)}, s32[3,128]{1,0:T(4,128)}, u32[]{:S(2)}) copy-start(s32[3,128]{1,0:T(4,128)} %targets_ref.9) | copy-start | bytes 4612
  13.9 9.8 %copy-start.1 = (bf16[3,64,64,128]{3,2,1,0:T(8,128)(2,1)S(1)}, bf16[3,64,64,128]{3,2,1,0:T(8,128)(2,1)}, u32[]{:S(2)}) copy-start(bf16[3,64,64,128]{3,2,1,0:T(8,128)(2,1)} %matrix_ref.29) | copy-start | bytes 9437188
  13.9 9.8 %copy-start.5 = (f32[64,128]{1,0:T(8,128)S(1)}, f32[64,128]{1,0:T(8,128)}, u32[]{:S(2)}) copy-start(f32[64,128]{1,0:T(8,128)} %source_ref.19) | copy-start | bytes 98308
  14.0 9.7 %collective-permute-start = (f32[64,128]{1,0:T(8,128)S(1)}, f32[64,128]{1,0:T(8,128)S(1)}, u32[]{:S(2)}, u32[]{:S(2)}) collective-permute-start(f32[64,128]{1,0:T(8,128)S(1)} %get-tuple-element.38.field_ref.change_ref), channel_id=1, source_target_pairs={{1,2},{3,4},{5,6},{7,8},{9,10},{11,12},{13,14},{15,16},{17,18},{19... | collective-permute-start | bytes 98312 | tf_op jit(solution)/shard_map/ppermute | solution.py:575
  23.7 1.5 copy-start.2
  25.2 34.6 %copy-start.9 = (bf16[3,6,6,1024]{3,2,1,0:T(8,128)(2,1)S(1)}, bf16[3,6,6,1024]{3,2,1,0:T(8,128)(2,1)}, u32[]{:S(2)}) copy-start(bf16[3,6,6,1024]{3,2,1,0:T(8,128)(2,1)} %blocks_ref.3) | copy-start | bytes 663556
  25.2 34.6 %copy-start.12 = (s32[3,1024]{1,0:T(4,128)S(1)}, s32[3,1024]{1,0:T(4,128)}, u32[]{:S(2)}) copy-start(s32[3,1024]{1,0:T(4,128)} %pattern_ref.21) | copy-start | bytes 36868
  25.9 41.7 %collective-permute-start.5 = (f32[528,384]{1,0:T(8,128)S(1)}, f32[528,384]{1,0:T(8,128)S(1)}, u32[]{:S(2)}, u32[]{:S(2)}) collective-permute-start(f32[528,384]{1,0:T(8,128)S(1)} %shard_map.103), channel_id=1, source_target_pairs={{0,8},{1,9},{2,10},{8,16},{9,17},{10,18},{16,24},{17,25},{18,26},{... | collective-permute-start | bytes 2433032 | tf_op jit(solution)/shard_map/ppermute | solution.py:569
  27.8 39.8 %collective-permute-start.7 = (f32[1160,128]{1,0:T(8,128)S(1)}, f32[1160,128]{1,0:T(8,128)S(1)}, u32[]{:S(2)}, u32[]{:S(2)}) collective-permute-start(f32[1160,128]{1,0:T(8,128)S(1)} %shard_map.97), channel_id=1, source_target_pairs={{0,1},{1,0},{2,3},{3,2},{4,5},{5,4},{6,7},{7,6},{8,9},{9,8},{10,11... | collective-permute-start | bytes 1781768 | tf_op jit(solution)/shard_map/ppermute | solution.py:622
  29.7 37.9 %collective-permute-start.6 = (f32[1160,128]{1,0:T(8,128)S(1)}, f32[1160,128]{1,0:T(8,128)S(1)}, u32[]{:S(2)}, u32[]{:S(2)}) collective-permute-start(f32[1160,128]{1,0:T(8,128)S(1)} %shard_map.97), channel_id=1, source_target_pairs={{1,2},{3,4},{5,6},{7,8},{9,10},{11,12},{13,14},{15,16},{17,18},{19... | collective-permute-start | bytes 1781768 | tf_op jit(solution)/shard_map/ppermute | solution.py:621
  35.2 10.4 %collective-permute-start.3 = (f32[64,128]{1,0:T(8,128)S(1)}, f32[64,128]{1,0:T(8,128)S(1)}, u32[]{:S(2)}, u32[]{:S(2)}) collective-permute-start(f32[64,128]{1,0:T(8,128)S(1)} %shard_map.94.field_ref), channel_id=1, source_target_pairs={{1,2},{3,4},{5,6},{7,8},{9,10},{11,12},{13,14},{15,16},{17,18},{19... | collective-permute-start | bytes 98312 | tf_op jit(solution)/shard_map/ppermute | solution.py:575
  42.0 58.5 %copy-start.7 = (f32[24,1536]{1,0:T(8,128)S(1)}, f32[24,1536]{1,0:T(8,128)}, u32[]{:S(2)}) copy-start(f32[24,1536]{1,0:T(8,128)} %top_inverse_ref.3) | copy-start | bytes 442372
  55.5 9.8 %collective-permute-start.4 = (f32[10,8,128]{2,1,0:T(8,128)S(1)}, f32[10,8,128]{2,1,0:T(8,128)S(1)}, u32[]{:S(2)}, u32[]{:S(2)}) collective-permute-start(f32[10,8,128]{2,1,0:T(8,128)S(1)} %get-tuple-element.45), channel_id=1, source_target_pairs={{8,16},{24,32},{40,48},{56,64},{72,80},{88,96},{104,112},{120,128}... | collective-permute-start | bytes 122888 | tf_op jit(solution)/shard_map/ppermute | solution.py:626
  103.4 9.5 %collective-permute-start.8 = (f32[64,128]{1,0:T(8,128)S(1)}, f32[64,128]{1,0:T(8,128)S(1)}, u32[]{:S(2)}, u32[]{:S(2)}) collective-permute-start(f32[64,128]{1,0:T(8,128)S(1)} %get-tuple-element.60.field_ref), channel_id=1, source_target_pairs={{1,2},{3,4},{5,6},{7,8},{9,10},{11,12},{13,14},{15,16},{17,18},{19... | collective-permute-start | bytes 98312 | tf_op jit(solution)/shard_map/ppermute | solution.py:575
  114.1 9.5 %collective-permute-start.9 = (f32[64,128]{1,0:T(8,128)S(1)}, f32[64,128]{1,0:T(8,128)S(1)}, u32[]{:S(2)}, u32[]{:S(2)}) collective-permute-start(f32[64,128]{1,0:T(8,128)S(1)} %shard_map.107.field_ref), channel_id=1, source_target_pairs={{1,2},{3,4},{5,6},{7,8},{9,10},{11,12},{13,14},{15,16},{17,18},{19... | collective-permute-start | bytes 98312 | tf_op jit(solution)/shard_map/ppermute | solution.py:575
  124.7 9.5 %collective-permute-start.10 = (f32[64,128]{1,0:T(8,128)S(1)}, f32[64,128]{1,0:T(8,128)S(1)}, u32[]{:S(2)}, u32[]{:S(2)}) collective-permute-start(f32[64,128]{1,0:T(8,128)S(1)} %get-tuple-element.62.field_ref), channel_id=1, source_target_pairs={{1,2},{3,4},{5,6},{7,8},{9,10},{11,12},{13,14},{15,16},{17,18},{19... | collective-permute-start | bytes 98312 | tf_op jit(solution)/shard_map/ppermute | solution.py:575
  135.4 9.5 %collective-permute-start.11 = (f32[64,128]{1,0:T(8,128)S(1)}, f32[64,128]{1,0:T(8,128)S(1)}, u32[]{:S(2)}, u32[]{:S(2)}) collective-permute-start(f32[64,128]{1,0:T(8,128)S(1)} %shard_map.113.field_ref), channel_id=1, source_target_pairs={{1,2},{3,4},{5,6},{7,8},{9,10},{11,12},{13,14},{15,16},{17,18},{19... | collective-permute-start | bytes 98312 | tf_op jit(solution)/shard_map/ppermute | solution.py:575
  154.4 8.0 %collective-permute-start.12 = (f32[10,8,128]{2,1,0:T(8,128)S(1)}, f32[10,8,128]{2,1,0:T(8,128)S(1)}, u32[]{:S(2)}, u32[]{:S(2)}) collective-permute-start(f32[10,8,128]{2,1,0:T(8,128)S(1)} %get-tuple-element.65), channel_id=1, source_target_pairs={{8,16},{24,32},{40,48},{56,64},{72,80},{88,96},{104,112},{120,128}... | collective-permute-start | bytes 122888 | tf_op jit(solution)/shard_map/ppermute | solution.py:626
  193.2 9.5 %collective-permute-start.13 = (f32[64,128]{1,0:T(8,128)S(1)}, f32[64,128]{1,0:T(8,128)S(1)}, u32[]{:S(2)}, u32[]{:S(2)}) collective-permute-start(f32[64,128]{1,0:T(8,128)S(1)} %get-tuple-element.69.field_ref), channel_id=1, source_target_pairs={{1,2},{3,4},{5,6},{7,8},{9,10},{11,12},{13,14},{15,16},{17,18},{19... | collective-permute-start | bytes 98312 | tf_op jit(solution)/shard_map/ppermute | solution.py:575
  (4 other events, 3.3 us)

commit v8 on v7

--- a/solution.py
+++ b/solution.py
@@ -296,15 +296,17 @@
     return fold_rows(terms)
 
 
-def by_two(first, number, body):
+def by_many(first, number, body, unroll=7):
+    each = min(unroll, number)
+
     def trip(i, carry):
-        body(first + 2 * i)
-        body(first + 2 * i + 1)
+        for j in range(each):
+            body(first + each * i + j)
         return carry
 
-    lax.fori_loop(0, number // 2, trip, 0)
-    if number % 2:
-        body(first + number - 1)
+    lax.fori_loop(0, number // each, trip, 0)
+    for j in range(number - number % each, number):
+        body(first + j)
 
 
 def gather_body(parts_ref, ends_ref, all_ref):
@@ -355,7 +357,7 @@
         other[b + 1] = start + second
         sol_ref[b] = start + second
 
-    by_two(EXT - FAR, count + 2 * FAR, first)
+    by_many(EXT - FAR, count + 2 * FAR, first)
 
     def down(i, carry):
         for j in range(2):
@@ -489,13 +491,13 @@
         final[b] = change
         other[b + 1] = field[b + 1] + change
 
-    by_two(middle - 3, 7, smooth_first)
+    by_many(middle - 3, 7, smooth_first)
 
     def smooth_second(b):
         second = KEEP * final[b] + FRESH * inverse_ref[b] * (rhs_ref[b] - coarse_product(matrix_ref, offset_ref, other, b))
         final[b] = other[b + 1] + second
 
-    by_two(middle - 2, 5, smooth_second)
+    by_many(middle - 2, 5, smooth_second)
     load_halo(where_ref, pair_ref, odd_ref, ext)
     rows = ext.shape[1]
     parity = where_ref[0]

time: 205 us -> 204 us (level)
  no operation moved by 1% of the time
where the time goes in v8:
time: 204 us; the launch traced here: 203 us
  blocking collectives  98.4 us (48%)
  starting transfers between devices  45.5 us (22%)
  Pallas kernels  27.2 us (13%)
  waiting for transfers between devices  25.9 us (13%)
  local copies, waits for them, and re-layouts  5.36 us (3%)
    all_to_all x2, blocking collectives, shards(): tops = lax.all_to_all(top, 'slab', 0, 0, tiled=True)  58.6 us
    ppermute x7, waiting for transfers between devices, nearby(): odd = lax.ppermute(field, both, odd_swap)  25 us
    ppermute x7, starting transfers between devices, nearby(): odd = lax.ppermute(field, both, odd_swap)  21.5 us
    all_to_all x2, blocking collectives, shards(): parts = lax.all_to_all(sums, 'sec', 0, 0, tiled=True)  16.7 us
    all_gather x7, blocking collectives, nearby(): pair = lax.all_gather(field, 'sec', axis_index_groups=pairs, axis=0)  13.7 us
    pallas_call x7, Pallas kernels, step(): call(body, outs, [SMEM] + [VMEM] * (6 + len(rest)), work[1:])  9.42 us
    all_gather x2, blocking collectives, shards(): even = lax.all_gather(ends, 'slab', axis_index_groups=slab_pairs, axis=0)  9.36 us
    ppermute x2, starting transfers between devices, beside(): lax.ppermute(value, 'slab', [(i, i + step) for i in range(max(0, -step),...  7.95 us
  transfers between devices with their start and end apart: 14, of which 8 were waited for; matrix products, arithmetic and copies ran while one was open for 0% of the time, Pallas kernels for 6%

profile of v8, /device:TPU:32, one launch (start us, length us, event | category | flops | bytes accessed | tf_op | source)
XLA Modules:
  0.0 202.7 jit_solution(5560187429720373)
XLA Ops:
  3.3 3.4 %collective-permute-start.1 = (f32[224,512]{1,0:T(8,128)S(1)}, f32[224,512]{1,0:T(8,128)S(1)}, u32[]{:S(2)}, u32[]{:S(2)}) collective-permute-start(f32[224,512]{1,0:T(8,128)S(1)} %get-tuple-element.40), channel_id=1, source_target_pairs={{0,8},{8,16},{16,24},{24,32},{32,40},{40,48},{48,56},{56,64},{64,7... | collective-permute-start | bytes 1376264 | tf_op jit(solution)/shard_map/ppermute | solution.py:583
  6.7 4.6 %collective-permute-start.2 = (f32[224,512]{1,0:T(8,128)S(1)}, f32[224,512]{1,0:T(8,128)S(1)}, u32[]{:S(2)}, u32[]{:S(2)}) collective-permute-start(f32[224,512]{1,0:T(8,128)S(1)} %get-tuple-element.41), channel_id=1, source_target_pairs={{8,0},{16,8},{24,16},{32,24},{40,32},{48,40},{56,48},{64,56},{72,6... | collective-permute-start | bytes 1376264 | tf_op jit(solution)/shard_map/ppermute | solution.py:583
  14.0 3.8 %collective-permute-start = (f32[64,128]{1,0:T(8,128)S(1)}, f32[64,128]{1,0:T(8,128)S(1)}, u32[]{:S(2)}, u32[]{:S(2)}) collective-permute-start(f32[64,128]{1,0:T(8,128)S(1)} %get-tuple-element.38.field_ref.change_ref), channel_id=1, source_target_pairs={{1,2},{3,4},{5,6},{7,8},{9,10},{11,12},{13,14},{15,16},{17,18},{19... | collective-permute-start | bytes 98312 | tf_op jit(solution)/shard_map/ppermute | solution.py:577
  21.2 2.5 %collective-permute-done.odd_ref = f32[64,128]{1,0:T(8,128)S(1)} collective-permute-done((f32[64,128]{1,0:T(8,128)S(1)}, f32[64,128]{1,0:T(8,128)S(1)}, u32[]{:S(2)}, u32[]{:S(2)}) %collective-permute-start) | collective-permute-done | bytes 32800 | tf_op jit(solution)/shard_map/ppermute | solution.py:577
  29.7 5.4 %collective-permute-start.6 = (f32[1160,128]{1,0:T(8,128)S(1)}, f32[1160,128]{1,0:T(8,128)S(1)}, u32[]{:S(2)}, u32[]{:S(2)}) collective-permute-start(f32[1160,128]{1,0:T(8,128)S(1)} %shard_map.97), channel_id=1, source_target_pairs={{1,2},{3,4},{5,6},{7,8},{9,10},{11,12},{13,14},{15,16},{17,18},{19... | collective-permute-start | bytes 1781768 | tf_op jit(solution)/shard_map/ppermute | solution.py:623
  35.2 4.3 %collective-permute-start.3 = (f32[64,128]{1,0:T(8,128)S(1)}, f32[64,128]{1,0:T(8,128)S(1)}, u32[]{:S(2)}, u32[]{:S(2)}) collective-permute-start(f32[64,128]{1,0:T(8,128)S(1)} %shard_map.94.field_ref), channel_id=1, source_target_pairs={{1,2},{3,4},{5,6},{7,8},{9,10},{11,12},{13,14},{15,16},{17,18},{19... | collective-permute-start | bytes 98312 | tf_op jit(solution)/shard_map/ppermute | solution.py:577
  42.0 3.5 %collective-permute-done.3.odd_ref = f32[64,128]{1,0:T(8,128)S(1)} collective-permute-done((f32[64,128]{1,0:T(8,128)S(1)}, f32[64,128]{1,0:T(8,128)S(1)}, u32[]{:S(2)}, u32[]{:S(2)}) %collective-permute-start.3) | collective-permute-done | bytes 32800 | tf_op jit(solution)/shard_map/ppermute | solution.py:577
  47.0 8.6 %all_to_all.32.parts_ref = f32[8,8,384]{2,1,0:T(8,128)S(1)} all-to-all(f32[8,8,384]{2,1,0:T(8,128)S(1)} %shard_map.99), channel_id=1, replica_groups=mesh['slab'=64,'sec'=8] {'sec'}, dimensions={0} | all-to-all | bytes 196608 | tf_op jit(solution)/shard_map/all_to_all | solution.py:626
  55.5 4.3 %collective-permute-start.4 = (f32[10,8,128]{2,1,0:T(8,128)S(1)}, f32[10,8,128]{2,1,0:T(8,128)S(1)}, u32[]{:S(2)}, u32[]{:S(2)}) collective-permute-start(f32[10,8,128]{2,1,0:T(8,128)S(1)} %get-tuple-element.45), channel_id=1, source_target_pairs={{8,16},{24,32},{40,48},{56,64},{72,80},{88,96},{104,112},{120,128}... | collective-permute-start | bytes 122888 | tf_op jit(solution)/shard_map/ppermute | solution.py:628
  60.7 4.7 %all-gather.2 = f32[20,8,128]{2,1,0:T(8,128)S(1)} all-gather(f32[10,8,128]{2,1,0:T(8,128)S(1)} %get-tuple-element.45), channel_id=4, replica_groups={{0,8},{16,24},{32,40},{48,56},{64,72},{80,88},{96,104},{112,120},{128,1..., dimensions={0}, use_global_device_ids=true | all-gather | bytes 122880 | tf_op jit(solution)/shard_map/all_gather | solution.py:629
  67.2 33.0 %all_to_all.33 = f32[64,1,128]{2,1,0:T(1,128)S(1)} all-to-all(f32[64,1,128]{2,1,0:T(1,128)S(1)} %bitcast.50), channel_id=1, replica_groups=mesh['slab'=64,'sec'=8] {'slab'}, dimensions={0} | all-to-all | bytes 65536 | tf_op jit(solution)/shard_map/all_to_all | solution.py:635
  100.1 2.4 %shard_map.104 = (f32[64,128]{1,0:T(8,128)S(1)}, f32[64,128]{1,0:T(8,128)S(1)}) custom-call(s32[7]{0:T(128)S(1)} %stack.35.where_ref, f32[64,128]{1,0:T(8,128)S(1)} %bitcast.49, f32[224,512]{1,0:T(8,128)S(1)} %collective-permute-done.1.left_ref, f32[24,1536]{1,0:T(8,128)S(1)} %copy-done.7, f32[224,512]{1,0:T(8,128)S(1)} %collective-permute-done.2.right_ref, ...), custom_call_target="tpu_custom_call" | custom-call | flops 1048576 | bytes 1048576 | tf_op jit(solution)/shard_map/pallas_call | solution.py:636
  107.7 4.3 %collective-permute-done.8.odd_ref = f32[64,128]{1,0:T(8,128)S(1)} collective-permute-done((f32[64,128]{1,0:T(8,128)S(1)}, f32[64,128]{1,0:T(8,128)S(1)}, u32[]{:S(2)}, u32[]{:S(2)}) %collective-permute-start.8) | collective-permute-done | bytes 32800 | tf_op jit(solution)/shard_map/ppermute | solution.py:577
  113.2 3.2 %collective-permute-start.9 = (f32[64,128]{1,0:T(8,128)S(1)}, f32[64,128]{1,0:T(8,128)S(1)}, u32[]{:S(2)}, u32[]{:S(2)}) collective-permute-start(f32[64,128]{1,0:T(8,128)S(1)} %shard_map.107.field_ref), channel_id=1, source_target_pairs={{1,2},{3,4},{5,6},{7,8},{9,10},{11,12},{13,14},{15,16},{17,18},{19... | collective-permute-start | bytes 98312 | tf_op jit(solution)/shard_map/ppermute | solution.py:577
  119.2 3.4 %collective-permute-done.9.odd_ref = f32[64,128]{1,0:T(8,128)S(1)} collective-permute-done((f32[64,128]{1,0:T(8,128)S(1)}, f32[64,128]{1,0:T(8,128)S(1)}, u32[]{:S(2)}, u32[]{:S(2)}) %collective-permute-start.9) | collective-permute-done | bytes 32800 | tf_op jit(solution)/shard_map/ppermute | solution.py:577
  123.9 3.2 %collective-permute-start.10 = (f32[64,128]{1,0:T(8,128)S(1)}, f32[64,128]{1,0:T(8,128)S(1)}, u32[]{:S(2)}, u32[]{:S(2)}) collective-permute-start(f32[64,128]{1,0:T(8,128)S(1)} %get-tuple-element.62.field_ref), channel_id=1, source_target_pairs={{1,2},{3,4},{5,6},{7,8},{9,10},{11,12},{13,14},{15,16},{17,18},{19... | collective-permute-start | bytes 98312 | tf_op jit(solution)/shard_map/ppermute | solution.py:577
  129.9 3.4 %collective-permute-done.10.odd_ref = f32[64,128]{1,0:T(8,128)S(1)} collective-permute-done((f32[64,128]{1,0:T(8,128)S(1)}, f32[64,128]{1,0:T(8,128)S(1)}, u32[]{:S(2)}, u32[]{:S(2)}) %collective-permute-start.10) | collective-permute-done | bytes 32800 | tf_op jit(solution)/shard_map/ppermute | solution.py:577
  134.5 3.2 %collective-permute-start.11 = (f32[64,128]{1,0:T(8,128)S(1)}, f32[64,128]{1,0:T(8,128)S(1)}, u32[]{:S(2)}, u32[]{:S(2)}) collective-permute-start(f32[64,128]{1,0:T(8,128)S(1)} %shard_map.113.field_ref), channel_id=1, source_target_pairs={{1,2},{3,4},{5,6},{7,8},{9,10},{11,12},{13,14},{15,16},{17,18},{19... | collective-permute-start | bytes 98312 | tf_op jit(solution)/shard_map/ppermute | solution.py:577
  140.5 3.4 %collective-permute-done.11.odd_ref = f32[64,128]{1,0:T(8,128)S(1)} collective-permute-done((f32[64,128]{1,0:T(8,128)S(1)}, f32[64,128]{1,0:T(8,128)S(1)}, u32[]{:S(2)}, u32[]{:S(2)}) %collective-permute-start.11) | collective-permute-done | bytes 32800 | tf_op jit(solution)/shard_map/ppermute | solution.py:577
  145.4 8.2 %all_to_all.34.parts_ref = f32[8,8,384]{2,1,0:T(8,128)S(1)} all-to-all(f32[8,8,384]{2,1,0:T(8,128)S(1)} %shard_map.116), channel_id=1, replica_groups=mesh['slab'=64,'sec'=8] {'sec'}, dimensions={0} | all-to-all | bytes 196608 | tf_op jit(solution)/shard_map/all_to_all | solution.py:626
  153.6 2.5 %collective-permute-start.12 = (f32[10,8,128]{2,1,0:T(8,128)S(1)}, f32[10,8,128]{2,1,0:T(8,128)S(1)}, u32[]{:S(2)}, u32[]{:S(2)}) collective-permute-start(f32[10,8,128]{2,1,0:T(8,128)S(1)} %get-tuple-element.65), channel_id=1, source_target_pairs={{8,16},{24,32},{40,48},{56,64},{72,80},{88,96},{104,112},{120,128}... | collective-permute-start | bytes 122888 | tf_op jit(solution)/shard_map/ppermute | solution.py:628
  156.1 4.7 %all-gather.7 = f32[20,8,128]{2,1,0:T(8,128)S(1)} all-gather(f32[10,8,128]{2,1,0:T(8,128)S(1)} %get-tuple-element.65), channel_id=9, replica_groups={{0,8},{16,24},{32,40},{48,56},{64,72},{80,88},{96,104},{112,120},{128,1..., dimensions={0}, use_global_device_ids=true | all-gather | bytes 122880 | tf_op jit(solution)/shard_map/all_gather | solution.py:629
  163.4 25.7 %all_to_all.35 = f32[64,1,128]{2,1,0:T(1,128)S(1)} all-to-all(f32[64,1,128]{2,1,0:T(1,128)S(1)} %bitcast.51), channel_id=1, replica_groups=mesh['slab'=64,'sec'=8] {'slab'}, dimensions={0} | all-to-all | bytes 65536 | tf_op jit(solution)/shard_map/all_to_all | solution.py:635
  196.6 4.3 %collective-permute-done.13.odd_ref = f32[64,128]{1,0:T(8,128)S(1)} collective-permute-done((f32[64,128]{1,0:T(8,128)S(1)}, f32[64,128]{1,0:T(8,128)S(1)}, u32[]{:S(2)}, u32[]{:S(2)}) %collective-permute-start.13) | collective-permute-done | bytes 32800 | tf_op jit(solution)/shard_map/ppermute | solution.py:577
  (78 shorter events, 52.4 us)
Async XLA Ops:
  3.3 21.6 %collective-permute-start.1 = (f32[224,512]{1,0:T(8,128)S(1)}, f32[224,512]{1,0:T(8,128)S(1)}, u32[]{:S(2)}, u32[]{:S(2)}) collective-permute-start(f32[224,512]{1,0:T(8,128)S(1)} %get-tuple-element.40), channel_id=1, source_target_pairs={{0,8},{8,16},{16,24},{24,32},{32,40},{40,48},{48,56},{56,64},{64,7... | collective-permute-start | bytes 1376264 | tf_op jit(solution)/shard_map/ppermute | solution.py:583
  6.7 18.2 %collective-permute-start.2 = (f32[224,512]{1,0:T(8,128)S(1)}, f32[224,512]{1,0:T(8,128)S(1)}, u32[]{:S(2)}, u32[]{:S(2)}) collective-permute-start(f32[224,512]{1,0:T(8,128)S(1)} %get-tuple-element.41), channel_id=1, source_target_pairs={{8,0},{16,8},{24,16},{32,24},{40,32},{48,40},{56,48},{64,56},{72,6... | collective-permute-start | bytes 1376264 | tf_op jit(solution)/shard_map/ppermute | solution.py:583
  11.3 1.9 copy-start
  13.9 6.0 %copy-start.10 = (s32[3,128]{1,0:T(4,128)S(1)}, s32[3,128]{1,0:T(4,128)}, u32[]{:S(2)}) copy-start(s32[3,128]{1,0:T(4,128)} %pattern_ref.31) | copy-start | bytes 4612
  13.9 6.7 %copy-start.3 = (bf16[3,64,6,128]{3,1,2,0:T(8,128)(2,1)S(1)}, bf16[3,64,6,128]{3,1,2,0:T(8,128)(2,1)}, u32[]{:S(2)}) copy-start(bf16[3,64,6,128]{3,1,2,0:T(8,128)(2,1)} %param.12) | copy-start | bytes 884740
  13.9 6.7 %copy-start.13 = (s32[3,128]{1,0:T(4,128)S(1)}, s32[3,128]{1,0:T(4,128)}, u32[]{:S(2)}) copy-start(s32[3,128]{1,0:T(4,128)} %targets_ref.9) | copy-start | bytes 4612
  13.9 9.8 %copy-start.1 = (bf16[3,64,64,128]{3,2,1,0:T(8,128)(2,1)S(1)}, bf16[3,64,64,128]{3,2,1,0:T(8,128)(2,1)}, u32[]{:S(2)}) copy-start(bf16[3,64,64,128]{3,2,1,0:T(8,128)(2,1)} %matrix_ref.29) | copy-start | bytes 9437188
  13.9 9.8 %copy-start.5 = (f32[64,128]{1,0:T(8,128)S(1)}, f32[64,128]{1,0:T(8,128)}, u32[]{:S(2)}) copy-start(f32[64,128]{1,0:T(8,128)} %source_ref.19) | copy-start | bytes 98308
  14.0 9.7 %collective-permute-start = (f32[64,128]{1,0:T(8,128)S(1)}, f32[64,128]{1,0:T(8,128)S(1)}, u32[]{:S(2)}, u32[]{:S(2)}) collective-permute-start(f32[64,128]{1,0:T(8,128)S(1)} %get-tuple-element.38.field_ref.change_ref), channel_id=1, source_target_pairs={{1,2},{3,4},{5,6},{7,8},{9,10},{11,12},{13,14},{15,16},{17,18},{19... | collective-permute-start | bytes 98312 | tf_op jit(solution)/shard_map/ppermute | solution.py:577
  23.7 1.5 copy-start.2
  25.2 34.6 %copy-start.9 = (bf16[3,6,6,1024]{3,2,1,0:T(8,128)(2,1)S(1)}, bf16[3,6,6,1024]{3,2,1,0:T(8,128)(2,1)}, u32[]{:S(2)}) copy-start(bf16[3,6,6,1024]{3,2,1,0:T(8,128)(2,1)} %blocks_ref.3) | copy-start | bytes 663556
  25.2 34.6 %copy-start.12 = (s32[3,1024]{1,0:T(4,128)S(1)}, s32[3,1024]{1,0:T(4,128)}, u32[]{:S(2)}) copy-start(s32[3,1024]{1,0:T(4,128)} %pattern_ref.21) | copy-start | bytes 36868
  25.9 41.3 %collective-permute-start.5 = (f32[528,384]{1,0:T(8,128)S(1)}, f32[528,384]{1,0:T(8,128)S(1)}, u32[]{:S(2)}, u32[]{:S(2)}) collective-permute-start(f32[528,384]{1,0:T(8,128)S(1)} %shard_map.103), channel_id=1, source_target_pairs={{0,8},{1,9},{2,10},{8,16},{9,17},{10,18},{16,24},{17,25},{18,26},{... | collective-permute-start | bytes 2433032 | tf_op jit(solution)/shard_map/ppermute | solution.py:571
  27.8 39.3 %collective-permute-start.7 = (f32[1160,128]{1,0:T(8,128)S(1)}, f32[1160,128]{1,0:T(8,128)S(1)}, u32[]{:S(2)}, u32[]{:S(2)}) collective-permute-start(f32[1160,128]{1,0:T(8,128)S(1)} %shard_map.97), channel_id=1, source_target_pairs={{0,1},{1,0},{2,3},{3,2},{4,5},{5,4},{6,7},{7,6},{8,9},{9,8},{10,11... | collective-permute-start | bytes 1781768 | tf_op jit(solution)/shard_map/ppermute | solution.py:624
  29.7 37.4 %collective-permute-start.6 = (f32[1160,128]{1,0:T(8,128)S(1)}, f32[1160,128]{1,0:T(8,128)S(1)}, u32[]{:S(2)}, u32[]{:S(2)}) collective-permute-start(f32[1160,128]{1,0:T(8,128)S(1)} %shard_map.97), channel_id=1, source_target_pairs={{1,2},{3,4},{5,6},{7,8},{9,10},{11,12},{13,14},{15,16},{17,18},{19... | collective-permute-start | bytes 1781768 | tf_op jit(solution)/shard_map/ppermute | solution.py:623
  35.2 10.4 %collective-permute-start.3 = (f32[64,128]{1,0:T(8,128)S(1)}, f32[64,128]{1,0:T(8,128)S(1)}, u32[]{:S(2)}, u32[]{:S(2)}) collective-permute-start(f32[64,128]{1,0:T(8,128)S(1)} %shard_map.94.field_ref), channel_id=1, source_target_pairs={{1,2},{3,4},{5,6},{7,8},{9,10},{11,12},{13,14},{15,16},{17,18},{19... | collective-permute-start | bytes 98312 | tf_op jit(solution)/shard_map/ppermute | solution.py:577
  42.0 58.1 %copy-start.7 = (f32[24,1536]{1,0:T(8,128)S(1)}, f32[24,1536]{1,0:T(8,128)}, u32[]{:S(2)}) copy-start(f32[24,1536]{1,0:T(8,128)} %top_inverse_ref.3) | copy-start | bytes 442372
  55.5 9.8 %collective-permute-start.4 = (f32[10,8,128]{2,1,0:T(8,128)S(1)}, f32[10,8,128]{2,1,0:T(8,128)S(1)}, u32[]{:S(2)}, u32[]{:S(2)}) collective-permute-start(f32[10,8,128]{2,1,0:T(8,128)S(1)} %get-tuple-element.45), channel_id=1, source_target_pairs={{8,16},{24,32},{40,48},{56,64},{72,80},{88,96},{104,112},{120,128}... | collective-permute-start | bytes 122888 | tf_op jit(solution)/shard_map/ppermute | solution.py:628
  102.6 9.5 %collective-permute-start.8 = (f32[64,128]{1,0:T(8,128)S(1)}, f32[64,128]{1,0:T(8,128)S(1)}, u32[]{:S(2)}, u32[]{:S(2)}) collective-permute-start(f32[64,128]{1,0:T(8,128)S(1)} %get-tuple-element.60.field_ref), channel_id=1, source_target_pairs={{1,2},{3,4},{5,6},{7,8},{9,10},{11,12},{13,14},{15,16},{17,18},{19... | collective-permute-start | bytes 98312 | tf_op jit(solution)/shard_map/ppermute | solution.py:577
  113.2 9.5 %collective-permute-start.9 = (f32[64,128]{1,0:T(8,128)S(1)}, f32[64,128]{1,0:T(8,128)S(1)}, u32[]{:S(2)}, u32[]{:S(2)}) collective-permute-start(f32[64,128]{1,0:T(8,128)S(1)} %shard_map.107.field_ref), channel_id=1, source_target_pairs={{1,2},{3,4},{5,6},{7,8},{9,10},{11,12},{13,14},{15,16},{17,18},{19... | collective-permute-start | bytes 98312 | tf_op jit(solution)/shard_map/ppermute | solution.py:577
  123.9 9.5 %collective-permute-start.10 = (f32[64,128]{1,0:T(8,128)S(1)}, f32[64,128]{1,0:T(8,128)S(1)}, u32[]{:S(2)}, u32[]{:S(2)}) collective-permute-start(f32[64,128]{1,0:T(8,128)S(1)} %get-tuple-element.62.field_ref), channel_id=1, source_target_pairs={{1,2},{3,4},{5,6},{7,8},{9,10},{11,12},{13,14},{15,16},{17,18},{19... | collective-permute-start | bytes 98312 | tf_op jit(solution)/shard_map/ppermute | solution.py:577
  134.5 9.5 %collective-permute-start.11 = (f32[64,128]{1,0:T(8,128)S(1)}, f32[64,128]{1,0:T(8,128)S(1)}, u32[]{:S(2)}, u32[]{:S(2)}) collective-permute-start(f32[64,128]{1,0:T(8,128)S(1)} %shard_map.113.field_ref), channel_id=1, source_target_pairs={{1,2},{3,4},{5,6},{7,8},{9,10},{11,12},{13,14},{15,16},{17,18},{19... | collective-permute-start | bytes 98312 | tf_op jit(solution)/shard_map/ppermute | solution.py:577
  153.6 8.0 %collective-permute-start.12 = (f32[10,8,128]{2,1,0:T(8,128)S(1)}, f32[10,8,128]{2,1,0:T(8,128)S(1)}, u32[]{:S(2)}, u32[]{:S(2)}) collective-permute-start(f32[10,8,128]{2,1,0:T(8,128)S(1)} %get-tuple-element.65), channel_id=1, source_target_pairs={{8,16},{24,32},{40,48},{56,64},{72,80},{88,96},{104,112},{120,128}... | collective-permute-start | bytes 122888 | tf_op jit(solution)/shard_map/ppermute | solution.py:628
  191.5 9.5 %collective-permute-start.13 = (f32[64,128]{1,0:T(8,128)S(1)}, f32[64,128]{1,0:T(8,128)S(1)}, u32[]{:S(2)}, u32[]{:S(2)}) collective-permute-start(f32[64,128]{1,0:T(8,128)S(1)} %get-tuple-element.69.field_ref), channel_id=1, source_target_pairs={{1,2},{3,4},{5,6},{7,8},{9,10},{11,12},{13,14},{15,16},{17,18},{19... | collective-permute-start | bytes 98312 | tf_op jit(solution)/shard_map/ppermute | solution.py:577
  (4 other events, 3.3 us)
